TPU v7x, 32 devices: a whole 2x2x4 slice. The times are simulated.
32 devices in a mesh: dp: 8 (over z, x), mp: 4 (over y, core).
Axes of the slice: x: 2, y: 2, z: 4, core: 2. Of those that a mesh axis runs over, the one named last changes fastest.
Arguments:
- tokens: bfloat16 [18432, 1024], P('dp'), may hold values from -6 to 6
- cotangent: bfloat16 [18432, 1024], P('dp'), may hold values from -6 to 6
- seq_lengths: int32 [16, 4], P('dp'), may hold values from 1 to 1024, 1152 in all within a row
- deal: int32 [64], replicated, may hold values from 0 to 63, as said below
- w_query: bfloat16 [1024, 1024], P(None, 'mp'), may hold values from -0.1875 to 0.1875
- w_keyval: bfloat16 [1024, 2, 512], P(None, None, 'mp'), may hold values from -0.1875 to 0.1875
- w_output: bfloat16 [1024, 1024], P('mp'), may hold values from -3 to 3
- w_gateup: bfloat16 [1024, 2, 4608], P(None, None, 'mp'), may hold values from -0.1875 to 0.1875
- w_down: bfloat16 [4608, 1024], P('mp'), may hold values from -0.09375 to 0.09375
- norm_gains: float32 [2, 1024], replicated, may hold values from 0.5 to 1.5
- head_gains: float32 [2, 64], replicated, may hold values from 0.5 to 1.5
- master_query: float32 [1024, 1024], P('dp', 'mp'), may hold values from -0.1875 to 0.1875
- master_keyval: float32 [1024, 2, 512], P('dp', None, 'mp'), may hold values from -0.1875 to 0.1875
- master_output: float32 [1024, 1024], P('mp', 'dp'), may hold values from -0.1875 to 0.1875
- master_gateup: float32 [1024, 2, 4608], P('dp', None, 'mp'), may hold values from -0.1875 to 0.1875
- master_down: float32 [4608, 1024], P('mp', 'dp'), may hold values from -0.09375 to 0.09375
- start_query: float32 [1024, 1024], P('dp', 'mp'), may hold values from -6 to 6
- start_keyval: float32 [1024, 2, 512], P('dp', None, 'mp'), may hold values from -6 to 6
- start_output: float32 [1024, 1024], P('mp', 'dp'), may hold values from -6 to 6
- start_gateup: float32 [1024, 2, 4608], P('dp', None, 'mp'), may hold values from -6 to 6
- start_down: float32 [4608, 1024], P('mp', 'dp'), may hold values from -6 to 6
- start_norms: float32 [2, 1024], replicated, may hold values from -6 to 6
- start_heads: float32 [2, 64], replicated, may hold values from -6 to 6
- step_size: float32 [1], replicated, may hold values from 0.03 to 0.2
Outputs:
- output: bfloat16 [18432, 1024], P('dp')
- input_grad: bfloat16 [18432, 1024], P('dp')
- clip_norm: float32 [1], replicated
- moment_query: float32 [1024, 1024], P('dp', 'mp')
- moment_keyval: float32 [1024, 2, 512], P('dp', None, 'mp')
- moment_output: float32 [1024, 1024], P('mp', 'dp')
- moment_gateup: float32 [1024, 2, 4608], P('dp', None, 'mp')
- moment_down: float32 [4608, 1024], P('mp', 'dp')
- moment_norms: float32 [2, 1024], replicated
- moment_heads: float32 [2, 64], replicated
- next_query: float32 [1024, 1024], P('dp', 'mp')
- next_keyval: float32 [1024, 2, 512], P('dp', None, 'mp')
- next_output: float32 [1024, 1024], P('mp', 'dp')
- next_gateup: float32 [1024, 2, 4608], P('dp', None, 'mp')
- next_down: float32 [4608, 1024], P('mp', 'dp')
- next_norms: float32 [2, 1024], replicated
- next_heads: float32 [2, 64], replicated
- weight_query: bfloat16 [1024, 1024], P(None, 'mp')
- weight_keyval: bfloat16 [1024, 2, 512], P(None, None, 'mp')
- weight_output: bfloat16 [1024, 1024], P('mp')
- weight_gateup: bfloat16 [1024, 2, 4608], P(None, None, 'mp')
- weight_down: bfloat16 [4608, 1024], P('mp')
Inputs may be any that keep to these rules, and one draw needn't show every extreme that they name: A permutation: given piece g (piece g % 8 of device g // 8) goes to dealt place deal[g], held by device deal[g] // 8; every device sends exactly 1 pieces to every device. `seq_lengths`: row s lists the sequence lengths of slot s in order; each row sums to 1152 and its largest is 1024.
All inputs are finite; a program needn't handle non-finite values.
Results may differ from a plain program's by a relative error of at most 0.02.
Values may be sent and summed in bfloat16 or wider, within the bound.
No kernel may reach another device: no remote copies, remote signals or barrier semaphores. Data moves between devices by JAX's collectives and lax.ppermute only.
A program may use at most 256 MiB of HBM per device.

v0:
```python
import math

import jax
import jax.numpy as jnp
from jax import lax
from jax.sharding import PartitionSpec as P

D = 1024
H = 16
KV = 8
HD = 64
FF = 4608


EPSILON = 1e-05
ROPE_BASE = 1000000.0


def layout(lengths_row, count):
    ends = jnp.cumsum(lengths_row)
    index_row = jnp.arange(count, dtype=jnp.int32)
    passed = (index_row[:, None] >= ends[None, :]).astype(jnp.int32)
    segment = jnp.sum(passed, axis=1)
    position = index_row - jnp.sum(passed * lengths_row[None, :], axis=1)
    return (segment, position)


def rotation(position, head_dim):
    half = head_dim // 2
    freqs = ROPE_BASE ** (-jnp.arange(half, dtype=jnp.float32) * (2.0 / head_dim))
    angles = position.astype(jnp.float32)[:, None] * freqs[None, :]
    return (jnp.cos(angles)[:, None, :], jnp.sin(angles)[:, None, :])


def rotate(values, cosine, sine):
    half = values.shape[-1] // 2
    first = values[..., :half]
    second = values[..., half:]
    return jnp.concatenate(
        [first * cosine - second * sine, second * cosine + first * sine], axis=-1
    )


def row_norm(values, gain_row):
    inverse = lax.rsqrt(jnp.mean(values * values, axis=-1, keepdims=True) + EPSILON)
    return (values * inverse * gain_row, inverse)


def row_norm_back(gradient, values, inverse, gain_row):
    scaled = gradient * gain_row
    d_values = inverse * scaled - values * (inverse * inverse * inverse) * jnp.mean(
        scaled * values, axis=-1, keepdims=True
    )
    d_gain = jnp.sum((gradient * values * inverse).reshape(-1, values.shape[-1]), axis=0)
    return (d_values, d_gain)


def visible(segment, begin_row, end_row):
    query_index = jnp.arange(begin_row, end_row, dtype=jnp.int32)
    key_index = jnp.arange(end_row, dtype=jnp.int32)
    same_doc = segment[begin_row:end_row][:, None] == segment[:end_row][None, :]
    return (key_index[None, :] <= query_index[:, None]) & same_doc


def attend(query_heads, key_heads, value_heads, segment, score_scale):
    block_rows = query_heads.shape[0] // 2
    pieces_out = []
    pieces_sum = []
    for block_index in range(2):
        begin_row = block_index * block_rows
        end_row = begin_row + block_rows
        scores = (
            jnp.einsum(
                "qkrd,skd->krqs",
                query_heads[begin_row:end_row],
                key_heads[:end_row],
                preferred_element_type=jnp.float32,
            )
            * score_scale
        )
        scores = jnp.where(visible(segment, begin_row, end_row), scores, -1e30)
        row_max = jnp.max(scores, axis=-1, keepdims=True)
        exponent = jnp.exp(scores - row_max)
        row_sum = jnp.sum(exponent, axis=-1, keepdims=True)
        attn_probs = (exponent / row_sum).astype(jnp.bfloat16)
        pieces_out.append(
            jnp.einsum(
                "krqs,skd->qkrd",
                attn_probs,
                value_heads[:end_row],
                preferred_element_type=jnp.float32,
            )
        )
        pieces_sum.append(row_max + jnp.log(row_sum))
    return (jnp.concatenate(pieces_out, axis=0), jnp.concatenate(pieces_sum, axis=2))


def attend_back(query_heads, key_heads, value_heads, grad_out, log_sums, segment, score_scale):
    block_rows = query_heads.shape[0] // 2
    d_query_parts = []
    d_keys = jnp.zeros(key_heads.shape, jnp.float32)
    d_values = jnp.zeros(value_heads.shape, jnp.float32)
    for block_index in range(2):
        begin_row = block_index * block_rows
        end_row = begin_row + block_rows
        query_block = query_heads[begin_row:end_row]
        grad_block = grad_out[begin_row:end_row]
        scores = (
            jnp.einsum(
                "qkrd,skd->krqs",
                query_block,
                key_heads[:end_row],
                preferred_element_type=jnp.float32,
            )
            * score_scale
        )
        scores = jnp.where(visible(segment, begin_row, end_row), scores, -1e30)
        attn_probs = jnp.exp(scores - log_sums[:, :, begin_row:end_row])
        d_probs = jnp.einsum(
            "qkrd,skd->krqs", grad_block, value_heads[:end_row], preferred_element_type=jnp.float32
        )
        delta = jnp.sum(attn_probs * d_probs, axis=-1, keepdims=True)
        d_scores = (attn_probs * (d_probs - delta)).astype(jnp.bfloat16)
        d_query_parts.append(
            jnp.einsum(
                "krqs,skd->qkrd", d_scores, key_heads[:end_row], preferred_element_type=jnp.float32
            )
            * score_scale
        )
        d_keys = d_keys.at[:end_row].add(
            jnp.einsum("krqs,qkrd->skd", d_scores, query_block, preferred_element_type=jnp.float32)
            * score_scale
        )
        d_values = d_values.at[:end_row].add(
            jnp.einsum(
                "krqs,qkrd->skd",
                attn_probs.astype(jnp.bfloat16),
                grad_block,
                preferred_element_type=jnp.float32,
            )
        )
    return (jnp.concatenate(d_query_parts, axis=0), d_keys, d_values)


def local(
    tokens,
    cotangent,
    seq_lengths,
    deal,
    w_query,
    w_keyval,
    w_output,
    w_gateup,
    w_down,
    norm_gains,
    head_gains,
    master_query,
    master_keyval,
    master_output,
    master_gateup,
    master_down,
    start_query,
    start_keyval,
    start_output,
    start_gateup,
    start_down,
    start_norms,
    start_heads,
    step_size,
):
    devices = lax.axis_size("dp")
    tensor_ways = lax.axis_size("mp")
    device = lax.axis_index("dp")
    row_count = tokens.shape[0]
    model_width = tokens.shape[1]
    total_pieces = deal.shape[0]
    pieces_dev = total_pieces // devices
    piece_rows = row_count // pieces_dev
    per_peer = pieces_dev // devices
    slot_count = seq_lengths.shape[0]
    slot_rows = row_count // slot_count
    head_dim = head_gains.shape[1]
    score_scale = head_dim ** (-0.5)
    local_heads = w_query.shape[1] // head_dim
    local_kv = w_keyval.shape[2] // head_dim
    repeat = local_heads // local_kv
    placed = jnp.arange(pieces_dev, dtype=jnp.int32)
    my_places = lax.dynamic_slice_in_dim(deal, device * pieces_dev, pieces_dev)
    target = my_places // pieces_dev
    earlier = (target[:, None] == target[None, :]) & (my_places[None, :] < my_places[:, None])
    send_slot = target * per_peer + jnp.sum(earlier.astype(jnp.int32), axis=1)
    send_order = jnp.zeros((pieces_dev,), jnp.int32).at[send_slot].set(placed)
    inverse = (
        jnp.zeros((total_pieces,), jnp.int32)
        .at[deal]
        .set(jnp.arange(total_pieces, dtype=jnp.int32))
    )
    source = lax.dynamic_slice_in_dim(inverse, device * pieces_dev, pieces_dev) // pieces_dev
    before = (source[:, None] == source[None, :]) & (placed[None, :] < placed[:, None])
    arrive_slot = source * per_peer + jnp.sum(before.astype(jnp.int32), axis=1)
    return_order = jnp.zeros((pieces_dev,), jnp.int32).at[arrive_slot].set(placed)

    def to_pieces(values, order):
        return values.reshape(pieces_dev, piece_rows, model_width)[order].reshape(
            row_count, model_width
        )

    arrived_x, arrived_c = (
        lax.all_to_all(
            to_pieces(tokens, send_order), "dp", split_axis=0, concat_axis=0, tiled=True
        ),
        lax.all_to_all(
            to_pieces(cotangent, send_order), "dp", split_axis=0, concat_axis=0, tiled=True
        ),
    )
    dealt_x = to_pieces(arrived_x, arrive_slot)
    dealt_c = to_pieces(arrived_c, arrive_slot)
    outputs = []
    d_inputs = []
    summed = None
    owned_parts = None
    gain_norm_acc = jnp.zeros(norm_gains.shape, jnp.float32)
    gain_head_acc = jnp.zeros(head_gains.shape, jnp.float32)
    for micro in range(slot_count):
        lower = micro * slot_rows
        x_rows = dealt_x[lower : lower + slot_rows].astype(jnp.float32)
        back_rows = dealt_c[lower : lower + slot_rows].astype(jnp.float32)
        segment, position = layout(seq_lengths[micro], slot_rows)
        norm_one_f, inv_one = row_norm(x_rows, norm_gains[0])
        norm_one = norm_one_f.astype(jnp.bfloat16)
        query_raw = jnp.dot(norm_one, w_query, preferred_element_type=jnp.float32).reshape(
            slot_rows, local_heads, head_dim
        )
        keyval_raw = jnp.einsum(
            "td,dsc->tsc", norm_one, w_keyval, preferred_element_type=jnp.float32
        )
        key_raw = keyval_raw[:, 0].reshape(slot_rows, local_kv, head_dim)
        value_heads = keyval_raw[:, 1].astype(jnp.bfloat16).reshape(slot_rows, local_kv, head_dim)
        query_normed, query_inv = row_norm(query_raw, head_gains[0])
        key_normed, key_inv = row_norm(key_raw, head_gains[1])
        cosine, sine = rotation(position, head_dim)
        query_heads = (
            rotate(query_normed, cosine, sine)
            .astype(jnp.bfloat16)
            .reshape(slot_rows, local_kv, repeat, head_dim)
        )
        key_heads = rotate(key_normed, cosine, sine).astype(jnp.bfloat16)
        mixed, log_sums = attend(query_heads, key_heads, value_heads, segment, score_scale)
        mixed_low = mixed.astype(jnp.bfloat16).reshape(slot_rows, local_heads * head_dim)
        attn_sum = lax.psum(
            jnp.dot(mixed_low, w_output, preferred_element_type=jnp.float32).astype(jnp.bfloat16),
            "mp",
        ).astype(jnp.float32)
        hidden_one = x_rows + attn_sum
        norm_two_f, inv_two = row_norm(hidden_one, norm_gains[1])
        norm_two = norm_two_f.astype(jnp.bfloat16)
        gateup = jnp.einsum("td,dsf->tsf", norm_two, w_gateup, preferred_element_type=jnp.float32)
        gate = gateup[:, 0]
        up_part = gateup[:, 1]
        inner = (gate * jax.nn.sigmoid(gate) * up_part).astype(jnp.bfloat16)
        ffn_sum = lax.psum(
            jnp.dot(inner, w_down, preferred_element_type=jnp.float32).astype(jnp.bfloat16), "mp"
        ).astype(jnp.float32)
        outputs.append((hidden_one + ffn_sum).astype(jnp.bfloat16))
        back_low_rows = back_rows.astype(jnp.bfloat16)
        grad_down = jnp.einsum(
            "tf,td->fd", inner, back_low_rows, preferred_element_type=jnp.float32
        )
        d_inner = jnp.einsum("td,fd->tf", back_low_rows, w_down, preferred_element_type=jnp.float32)
        sigma = jax.nn.sigmoid(gate)
        d_gate = d_inner * up_part * sigma * (1.0 + gate * (1.0 - sigma))
        d_up = d_inner * gate * sigma
        d_gateup = jnp.stack([d_gate, d_up], axis=1).astype(jnp.bfloat16)
        grad_gateup = jnp.einsum(
            "td,tsf->dsf", norm_two, d_gateup, preferred_element_type=jnp.float32
        )
        d_norm_two = lax.psum(
            jnp.einsum(
                "tsf,dsf->td", d_gateup, w_gateup, preferred_element_type=jnp.float32
            ).astype(jnp.bfloat16),
            "mp",
        ).astype(jnp.float32)
        d_hidden_part, gain_two = row_norm_back(d_norm_two, hidden_one, inv_two, norm_gains[1])
        d_hidden = back_rows + d_hidden_part
        d_hidden_low = d_hidden.astype(jnp.bfloat16)
        grad_output = jnp.einsum(
            "tc,td->cd", mixed_low, d_hidden_low, preferred_element_type=jnp.float32
        )
        d_mixed = (
            jnp.einsum("td,cd->tc", d_hidden_low, w_output, preferred_element_type=jnp.float32)
            .astype(jnp.bfloat16)
            .reshape(slot_rows, local_kv, repeat, head_dim)
        )
        d_query_heads, d_key_heads, d_value_heads = attend_back(
            query_heads, key_heads, value_heads, d_mixed, log_sums, segment, score_scale
        )
        d_query_normed = rotate(
            d_query_heads.reshape(slot_rows, local_heads, head_dim), cosine, -sine
        )
        d_key_normed = rotate(d_key_heads, cosine, -sine)
        d_query_raw, gain_query = row_norm_back(d_query_normed, query_raw, query_inv, head_gains[0])
        d_key_raw, gain_key = row_norm_back(d_key_normed, key_raw, key_inv, head_gains[1])
        d_query_low = d_query_raw.reshape(slot_rows, local_heads * head_dim).astype(jnp.bfloat16)
        d_keyval_low = jnp.stack(
            [
                d_key_raw.reshape(slot_rows, local_kv * head_dim),
                d_value_heads.reshape(slot_rows, local_kv * head_dim),
            ],
            axis=1,
        ).astype(jnp.bfloat16)
        grad_query = jnp.einsum(
            "td,tc->dc", norm_one, d_query_low, preferred_element_type=jnp.float32
        )
        grad_keyval = jnp.einsum(
            "td,tsc->dsc", norm_one, d_keyval_low, preferred_element_type=jnp.float32
        )
        d_norm_part = jnp.einsum(
            "tc,dc->td", d_query_low, w_query, preferred_element_type=jnp.float32
        ) + jnp.einsum("tsc,dsc->td", d_keyval_low, w_keyval, preferred_element_type=jnp.float32)
        d_norm_one = lax.psum(d_norm_part.astype(jnp.bfloat16), "mp").astype(jnp.float32)
        d_input_part, gain_one = row_norm_back(d_norm_one, x_rows, inv_one, norm_gains[0])
        d_inputs.append((d_hidden + d_input_part).astype(jnp.bfloat16))
        gain_norm_acc = gain_norm_acc + jnp.stack([gain_one, gain_two], axis=0)
        gain_head_acc = gain_head_acc + jnp.stack([gain_query, gain_key], axis=0)
        grads_now = (grad_query, grad_keyval, grad_output, grad_gateup, grad_down)
        if summed is None:
            summed = grads_now
        else:
            summed = tuple(
                (first_term + second_term for first_term, second_term in zip(summed, grads_now))
            )
    owned_parts = (
        lax.psum_scatter(summed[0], "dp", scatter_dimension=0, tiled=True),
        lax.psum_scatter(summed[1], "dp", scatter_dimension=0, tiled=True),
        lax.psum_scatter(summed[2], "dp", scatter_dimension=1, tiled=True),
        lax.psum_scatter(summed[3], "dp", scatter_dimension=0, tiled=True),
        lax.psum_scatter(summed[4], "dp", scatter_dimension=1, tiled=True),
    )
    own_square = sum([jnp.sum(part_grad * part_grad) for part_grad in owned_parts])
    norm_sum, head_sum, square_sum = lax.psum(
        (gain_norm_acc / tensor_ways, gain_head_acc, own_square), ("dp", "mp")
    )
    clip_value = jnp.sqrt(square_sum + jnp.sum(norm_sum * norm_sum) + jnp.sum(head_sum * head_sum))
    limit = math.sqrt(2 * D * H * HD + 2 * D * KV * HD + 3 * D * FF + 2 * D + 2 * HD)
    factor = jnp.minimum(1.0, limit / clip_value)
    starts = (start_query, start_keyval, start_output, start_gateup, start_down)
    masters = (master_query, master_keyval, master_output, master_gateup, master_down)
    moments = [0.5 * begin + factor * part_grad for begin, part_grad in zip(starts, owned_parts)]
    nexts = [held - step_size[0] * moved for held, moved in zip(masters, moments)]
    moment_norms = 0.5 * start_norms + factor * norm_sum
    moment_heads = 0.5 * start_heads + factor * head_sum
    next_norms = norm_gains - step_size[0] * moment_norms
    next_heads = head_gains - step_size[0] * moment_heads
    gathered = (
        lax.all_gather(nexts[0].astype(jnp.bfloat16), "dp", axis=0, tiled=True),
        lax.all_gather(nexts[1].astype(jnp.bfloat16), "dp", axis=0, tiled=True),
        lax.all_gather(nexts[2].astype(jnp.bfloat16), "dp", axis=1, tiled=True),
        lax.all_gather(nexts[3].astype(jnp.bfloat16), "dp", axis=0, tiled=True),
        lax.all_gather(nexts[4].astype(jnp.bfloat16), "dp", axis=1, tiled=True),
    )
    out_rows = jnp.concatenate(outputs, axis=0)
    d_rows = jnp.concatenate(d_inputs, axis=0)
    back_out, back_grad = (
        lax.all_to_all(
            to_pieces(out_rows, return_order), "dp", split_axis=0, concat_axis=0, tiled=True
        ),
        lax.all_to_all(
            to_pieces(d_rows, return_order), "dp", split_axis=0, concat_axis=0, tiled=True
        ),
    )
    output = to_pieces(back_out, send_slot)
    input_grad = to_pieces(back_grad, send_slot)
    return (
        output,
        input_grad,
        clip_value.reshape(1),
        moments[0],
        moments[1],
        moments[2],
        moments[3],
        moments[4],
        moment_norms,
        moment_heads,
        nexts[0],
        nexts[1],
        nexts[2],
        nexts[3],
        nexts[4],
        next_norms,
        next_heads,
        gathered[0],
        gathered[1],
        gathered[2],
        gathered[3],
        gathered[4],
    )


def solution(mesh):
    in_specs = (
        P("dp", None),
        P("dp", None),
        P("dp", None),
        P(),
        P(None, "mp"),
        P(None, None, "mp"),
        P("mp", None),
        P(None, None, "mp"),
        P("mp", None),
        P(),
        P(),
        P("dp", "mp"),
        P("dp", None, "mp"),
        P("mp", "dp"),
        P("dp", None, "mp"),
        P("mp", "dp"),
        P("dp", "mp"),
        P("dp", None, "mp"),
        P("mp", "dp"),
        P("dp", None, "mp"),
        P("mp", "dp"),
        P(),
        P(),
        P(),
    )
    out_specs = (
        P("dp", None),
        P("dp", None),
        P(),
        P("dp", "mp"),
        P("dp", None, "mp"),
        P("mp", "dp"),
        P("dp", None, "mp"),
        P("mp", "dp"),
        P(),
        P(),
        P("dp", "mp"),
        P("dp", None, "mp"),
        P("mp", "dp"),
        P("dp", None, "mp"),
        P("mp", "dp"),
        P(),
        P(),
        P(None, "mp"),
        P(None, None, "mp"),
        P("mp", None),
        P(None, None, "mp"),
        P("mp", None),
    )
    return jax.shard_map(local, mesh=mesh, in_specs=in_specs, out_specs=out_specs, check_vma=False)
```

profile of v0, /device:TPU:0, one launch (start us, length us, event | category | flops | bytes accessed | tf_op | source)
XLA Modules:
  0.0 1586.0 jit_solution(14200816477389000630)
XLA Ops:
  15.8 7.4 all-to-all-start
  39.0 88.7 %all-to-all-done = bf16[8,288,1024]{2,1,0:T(8,128)(2,1)} async-done(((bf16[8,288,1024]{2,1,0:T(8,128)(2,1)}), bf16[8,288,1024]{2,1,0:T(8,128)(2,1)}, u32[]{:S(2)}, u32[]{:S(2)}) %all-to-all-start) | async-done | bytes 4718624 | tf_op jit(solution)/shard_map/all_to_all | solution.py:209
  192.0 44.1 %all-to-all-done.2 = bf16[8,288,1024]{2,1,0:T(8,128)(2,1)} async-done(((bf16[8,288,1024]{2,1,0:T(8,128)(2,1)}), bf16[8,288,1024]{2,1,0:T(8,128)(2,1)}, u32[]{:S(2)}, u32[]{:S(2)}) %all-to-all-start.2) | async-done | bytes 4718624 | tf_op jit(solution)/shard_map/all_to_all | solution.py:212
  248.1 38.9 %all-reduce.16.cloned.1.call-done = (bf16[1152,1024]{1,0:T(8,128)(2,1)}, bf16[1152,1024]{1,0:T(8,128)(2,1)}) async-done(((bf16[1152,1024]{1,0:T(8,128)(2,1)}, bf16[1152,1024]{1,0:T(8,128)(2,1)}), (bf16[1152,1024]{1,0:T(8,128)(2,1)}, bf16[1152,1024]{1,0:T(8,128)(2,1)})) %all-reduce.16.cloned.1.call-update) | async-done | bytes 4718608 | tf_op jit(solution)/shard_map/psum | solution.py:250
  295.4 8.2 fusion.97
  303.6 8.2 fusion.95
  311.8 7.2 fusion.116
  319.1 7.2 bitcast_convert_fusion.1
  326.3 7.7 fusion.117
  343.5 8.8 convolution_convert_fusion.3
  352.3 9.0 convolution_convert_fusion.2
  361.3 76.7 %all-reduce.14.cloned.1.call-done = (bf16[1152,1024]{1,0:T(8,128)(2,1)}, bf16[1152,1024]{1,0:T(8,128)(2,1)}) async-done(((bf16[1152,1024]{1,0:T(8,128)(2,1)}, bf16[1152,1024]{1,0:T(8,128)(2,1)}), (bf16[1152,1024]{1,0:T(8,128)(2,1)}, bf16[1152,1024]{1,0:T(8,128)(2,1)})) %all-reduce.14.cloned.1.call-update) | async-done | bytes 4718608 | tf_op jit(solution)/shard_map/psum | solution.py:277
  438.0 8.1 fusion.69
  487.7 7.8 fusion.3
  502.4 9.1 fusion
  568.2 8.5 fusion.108
  576.7 9.8 convolution_add_fusion.3
  588.2 9.5 fusion.92
  597.8 9.2 convolution_add_fusion
  608.4 111.6 %all-reduce.12.cloned.1.call-done = (bf16[1152,1024]{1,0:T(8,128)(2,1)}, bf16[1152,1024]{1,0:T(8,128)(2,1)}, bf16[1152,1024]{1,0:T(8,128)(2,1)}, bf16[1152,1024]{1,0:T(8,128)(2,1)}) async-done(((bf16[1152,1024]{1,0:T(8,128)(2,1)}, bf16[1152,1024]{1,0:T(8,128)(2,1)}, bf16[1152,1024]{1,0:T(8,128)(2,1)}, bf16[1152,1024]{1,0:T(8,128)(2,1)}), (bf16[1152,1024]{1,0:T(8,128)(2,1)}, bf16[1152,1024]{1,0:T(8,128)(2,1)}, ...) | async-done | bytes 9437200 | tf_op jit(solution)/shard_map/psum | solution.py:261
  727.2 10.5 fusion.63
  770.7 73.0 %reduce-scatter.6.cloned.1.call-done = f32[128,256]{1,0:T(8,128)} async-done(((f32[1024,256]{1,0:T(8,128)}), f32[128,256]{1,0:T(8,128)}) %reduce-scatter.6.cloned.1.call-update) | async-done | bytes 131088 | tf_op jit(solution)/shard_map/reduce_scatter | solution.py:333
  845.2 64.9 %reduce-scatter.8.cloned.1.call-done = f32[128,2,128]{2,0,1:T(8,128)} async-done(((f32[1024,2,128]{2,0,1:T(8,128)}), f32[128,2,128]{2,0,1:T(8,128)}) %reduce-scatter.8.cloned.1.call-update) | async-done | bytes 131088 | tf_op jit(solution)/shard_map/reduce_scatter | solution.py:334
  913.0 63.4 %reduce-scatter.10.cloned.1.call-done = f32[256,128]{1,0:T(8,128)} async-done(((f32[256,1024]{1,0:T(8,128)}), f32[256,128]{1,0:T(8,128)}) %reduce-scatter.10.cloned.1.call-update) | async-done | bytes 131088 | tf_op jit(solution)/shard_map/reduce_scatter | solution.py:335
  979.3 95.9 %reduce-scatter.14.cloned.1.call-done = f32[1152,128]{1,0:T(8,128)} async-done(((f32[1152,1024]{1,0:T(8,128)}), f32[1152,128]{1,0:T(8,128)}) %reduce-scatter.14.cloned.1.call-update) | async-done | bytes 589840 | tf_op jit(solution)/shard_map/reduce_scatter | solution.py:337
  1077.0 165.3 %reduce-scatter.12.cloned.1.call-done = f32[128,2,1152]{2,0,1:T(8,128)} async-done(((f32[1024,2,1152]{2,0,1:T(8,128)}), f32[128,2,1152]{2,0,1:T(8,128)}) %reduce-scatter.12.cloned.1.call-update) | async-done | bytes 1179664 | tf_op jit(solution)/shard_map/reduce_scatter | solution.py:336
  1246.4 39.5 %all-reduce.4 = (f32[]{:T(128)}, f32[2,1024]{1,0:T(2,128)S(1)}, f32[2,64]{1,0:T(2,128)S(1)}) all-reduce(f32[]{:T(128)S(6)} %add.470, f32[2,1024]{1,0:T(2,128)S(1)} %fusion.210, f32[2,64]{1,0:T(2,128)S(1)} %maximum_add_fusion.1), channel_id=1, replica_groups=mesh['dp'=8,'mp'=4] {'dp','mp'}, use_global_device_ids=true, to_apply=%region_57.58 | all-reduce | flops 2177 | bytes 17416 | tf_op jit(solution)/shard_map/psum | solution.py:340
  1315.6 135.4 %all-to-all-done.1 = bf16[8,288,1024]{2,1,0:T(8,128)(2,1)} async-done(((bf16[8,288,1024]{2,1,0:T(8,128)(2,1)}), bf16[8,288,1024]{2,1,0:T(8,128)(2,1)}, u32[]{:S(2)}, u32[]{:S(2)}) %all-to-all-start.1) | async-done | bytes 4718624 | tf_op jit(solution)/shard_map/all_to_all | solution.py:364
  1459.6 35.1 %all_gather.15 = bf16[1024,256]{1,0:T(8,128)(2,1)} all-gather(bf16[128,256]{1,0:T(8,128)(2,1)S(1)} %get-tuple-element.287), channel_id=1, replica_groups=mesh['dp'=8,'mp'=4] {'dp'}, dimensions={0}, use_global_device_ids=true | all-gather | bytes 589824 | tf_op jit(solution)/shard_map/all_gather | solution.py:355
  1494.8 32.4 %all_gather.16 = bf16[1024,2,128]{2,0,1:T(8,128)(2,1)S(1)} all-gather(bf16[128,2,128]{2,0,1:T(8,128)(2,1)S(1)} %get-tuple-element.284), channel_id=1, replica_groups=mesh['dp'=8,'mp'=4] {'dp'}, dimensions={0}, use_global_device_ids=true | all-gather | bytes 589824 | tf_op jit(solution)/shard_map/all_gather | solution.py:356
  1530.2 28.2 %all_gather.17 = bf16[256,1024]{1,0:T(8,128)(2,1)} all-gather(bf16[256,128]{1,0:T(8,128)(2,1)S(1)} %get-tuple-element.281), channel_id=1, replica_groups=mesh['dp'=8,'mp'=4] {'dp'}, dimensions={1}, use_global_device_ids=true | all-gather | bytes 589824 | tf_op jit(solution)/shard_map/all_gather | solution.py:357
  1563.5 9.5 copy.234
  (614 shorter events, 323.1 us)
Async XLA Ops:
  7.2 304.6 %copy-start = (bf16[1152,1024]{1,0:T(8,128)(2,1)S(1)}, bf16[1152,1024]{1,0:T(8,128)(2,1)}, u32[]{:S(2)}) copy-start(bf16[1152,1024]{1,0:T(8,128)(2,1)} %param.56) | copy-start | bytes 7077892
  15.8 111.9 %all-to-all-start = ((bf16[8,288,1024]{2,1,0:T(8,128)(2,1)}), bf16[8,288,1024]{2,1,0:T(8,128)(2,1)}, u32[]{:S(2)}, u32[]{:S(2)}) async-start(bf16[8,288,1024]{2,1,0:T(8,128)(2,1)} %gather_fusion), calls=%async_computation | async-start | bytes 9437184 | tf_op jit(solution)/shard_map/all_to_all | solution.py:209
  24.9 126.8 %copy-start.39 = (bf16[1024,2,128]{0,2,1:T(8,128)(2,1)}, bf16[1024,2,128]{0,2,1:T(8,128)(2,1)S(1)}, u32[]{:S(2)}) copy-start(bf16[1024,2,128]{0,2,1:T(8,128)(2,1)S(1)} %copy.188) | copy-start | bytes 1572868
  31.5 100.8 %copy-start.148 = (s32[1024]{0:T(1024)}, s32[1024]{0:T(1024)S(1)}, u32[]{:S(2)}) copy-start(s32[1024]{0:T(1024)S(1)} %pad_clamp_fusion.2) | copy-start | bytes 12292
  36.8 139.3 %copy-start.42 = (f32[1152,32]{0,1:T(8,128)}, f32[1152,32]{0,1:T(8,128)S(1)}, u32[]{:S(2)}) copy-start(f32[1152,32]{0,1:T(8,128)S(1)} %get-tuple-element.378) | copy-start | bytes 442372
  127.7 108.4 %all-to-all-start.2 = ((bf16[8,288,1024]{2,1,0:T(8,128)(2,1)}), bf16[8,288,1024]{2,1,0:T(8,128)(2,1)}, u32[]{:S(2)}, u32[]{:S(2)}) async-start(bf16[8,288,1024]{2,1,0:T(8,128)(2,1)} %gather_fusion.4), calls=%async_computation.2 | async-start | bytes 9437184 | tf_op jit(solution)/shard_map/all_to_all | solution.py:212
  132.3 154.7 %all-reduce.16.cloned.1.call-start = ((), (), s32[]{:S(2)}) async-start(), calls=%async_computation.18 | async-start | bytes 9437184 | tf_op jit(solution)/shard_map/psum | solution.py:250
  191.3 246.7 %all-reduce.14.cloned.1.call-start = ((), (), s32[]{:S(2)}) async-start(), calls=%async_computation.17 | async-start | bytes 9437184 | tf_op jit(solution)/shard_map/psum | solution.py:277
  343.4 376.6 %all-reduce.12.cloned.1.call-start = ((), (), s32[]{:S(2)}) async-start(), calls=%async_computation.16 | async-start | bytes 18874368 | tf_op jit(solution)/shard_map/psum | solution.py:261
  548.9 294.8 %reduce-scatter.6.cloned.1.call-start = ((), (), s32[]{:S(2)}) async-start(), calls=%async_computation.9 | async-start | bytes 1179648 | tf_op jit(solution)/shard_map/reduce_scatter | solution.py:333
  553.7 356.4 %reduce-scatter.8.cloned.1.call-start = ((), (), s32[]{:S(2)}) async-start(), calls=%async_computation.10 | async-start | bytes 1179648 | tf_op jit(solution)/shard_map/reduce_scatter | solution.py:334
  560.1 416.2 %reduce-scatter.10.cloned.1.call-start = ((), (), s32[]{:S(2)}) async-start(), calls=%async_computation.11 | async-start | bytes 1179648 | tf_op jit(solution)/shard_map/reduce_scatter | solution.py:335
  568.2 507.0 %reduce-scatter.14.cloned.1.call-start = ((), (), s32[]{:S(2)}) async-start(), calls=%async_computation.13 | async-start | bytes 5308416 | tf_op jit(solution)/shard_map/reduce_scatter | solution.py:337
  586.5 655.8 %reduce-scatter.12.cloned.1.call-start = ((), (), s32[]{:S(2)}) async-start(), calls=%async_computation.12 | async-start | bytes 10616832 | tf_op jit(solution)/shard_map/reduce_scatter | solution.py:336
  607.0 113.0 %copy-start.131 = (f32[1,1024]{1,0:T(1,128)S(1)}, f32[1,1024]{1,0:T(1,128)}, u32[]{:S(2)}) copy-start(f32[1,1024]{1,0:T(1,128)} %get-tuple-element.359) | copy-start | bytes 12292
  607.0 120.2 %slice-start.4 = ((s8[4718592]{0:T(1024)(128)(4,1)}), s8[524288]{0:T(1024)(128)(4,1)S(1)}, s32[]{:S(2)}) async-start(s8[4718592]{0:T(1024)(128)(4,1)} %bitcast.567), calls=%async_computation.23 | async-start | bytes 1048576
  608.3 133.7 %copy-start.149 = (s32[1024]{0:T(1024)}, s32[1024]{0:T(1024)S(1)}, u32[]{:S(2)}) copy-start(s32[1024]{0:T(1024)S(1)} %pad_clamp_fusion.1) | copy-start | bytes 12292
  747.5 554.2 %all-to-all-start.3 = ((bf16[8,288,1024]{2,1,0:T(8,128)(2,1)}), bf16[8,288,1024]{2,1,0:T(8,128)(2,1)}, u32[]{:S(2)}, u32[]{:S(2)}) async-start(bf16[8,288,1024]{2,1,0:T(8,128)(2,1)} %gather_fusion.6), calls=%async_computation.3 | async-start | bytes 9437184 | tf_op jit(solution)/shard_map/all_to_all | solution.py:367
  753.1 810.4 %all-gather.5.cloned.1.call-start = ((), (), s32[]{:S(2)}) async-start(), calls=%async_computation.15 | async-start | bytes 2654208 | tf_op jit(solution)/shard_map/all_gather | solution.py:359
  768.2 523.7 %copy-start.33 = (bf16[1152,1024]{1,0:T(8,128)(2,1)S(1)}, bf16[1152,1024]{1,0:T(8,128)(2,1)}, u32[]{:S(2)}) copy-start(bf16[1152,1024]{1,0:T(8,128)(2,1)} %get-tuple-element.310) | copy-start | bytes 7077892
  1301.7 149.3 %all-to-all-start.1 = ((bf16[8,288,1024]{2,1,0:T(8,128)(2,1)}), bf16[8,288,1024]{2,1,0:T(8,128)(2,1)}, u32[]{:S(2)}, u32[]{:S(2)}) async-start(bf16[8,288,1024]{2,1,0:T(8,128)(2,1)} %gather_fusion.2), calls=%async_computation.1 | async-start | bytes 9437184 | tf_op jit(solution)/shard_map/all_to_all | solution.py:364
  1307.2 256.3 %all-gather.3.cloned.1.call-start = ((), (), s32[]{:S(2)}) async-start(), calls=%async_computation.14 | async-start | bytes 5308416 | tf_op jit(solution)/shard_map/all_gather | solution.py:358
  1315.5 140.8 %copy-start.110 = (f32[128,2,128]{2,0,1:T(8,128)S(1)}, f32[128,2,128]{2,0,1:T(8,128)}, u32[]{:S(2)}) copy-start(f32[128,2,128]{2,0,1:T(8,128)} %reduce-scatter.8.cloned.1.call-done) | copy-start | bytes 393220
  1315.5 140.8 %copy-start.127 = (f32[128,2,128]{2,1,0:T(2,128)S(1)}, f32[128,2,128]{2,1,0:T(2,128)}, u32[]{:S(2)}) copy-start(f32[128,2,128]{2,1,0:T(2,128)} %param.60) | copy-start | bytes 393220
  1315.5 140.8 %copy-start.128 = (f32[128,2,128]{2,1,0:T(2,128)S(1)}, f32[128,2,128]{2,1,0:T(2,128)}, u32[]{:S(2)}) copy-start(f32[128,2,128]{2,1,0:T(2,128)} %param.65) | copy-start | bytes 393220
  1315.5 142.5 %copy-start.108 = (f32[128,256]{1,0:T(8,128)S(1)}, f32[128,256]{1,0:T(8,128)}, u32[]{:S(2)}) copy-start(f32[128,256]{1,0:T(8,128)} %reduce-scatter.6.cloned.1.call-done) | copy-start | bytes 393220
  1315.5 142.5 %copy-start.129 = (f32[128,256]{1,0:T(8,128)S(1)}, f32[128,256]{1,0:T(8,128)}, u32[]{:S(2)}) copy-start(f32[128,256]{1,0:T(8,128)} %param.59) | copy-start | bytes 393220
  1315.5 213.0 %copy-start.109 = (f32[256,128]{1,0:T(8,128)S(1)}, f32[256,128]{1,0:T(8,128)}, u32[]{:S(2)}) copy-start(f32[256,128]{1,0:T(8,128)} %reduce-scatter.10.cloned.1.call-done) | copy-start | bytes 393220
  1456.4 105.9 %copy-start.154 = (f32[2,64]{1,0:T(2,128)S(1)}, f32[2,64]{1,0:T(2,128)}, u32[]{:S(2)}) copy-start(f32[2,64]{1,0:T(2,128)} %param.58) | copy-start | bytes 1540
  1456.4 105.8 %copy-start.158 = (f32[2,64]{1,0:T(2,128)S(1)}, f32[2,64]{1,0:T(2,128)}, u32[]{:S(2)}) copy-start(f32[2,64]{1,0:T(2,128)} %param.70) | copy-start | bytes 1540
  1456.4 106.4 %copy-start.144 = (f32[2,1024]{1,0:T(2,128)S(1)}, f32[2,1024]{1,0:T(2,128)}, u32[]{:S(2)}) copy-start(f32[2,1024]{1,0:T(2,128)} %param.57) | copy-start | bytes 24580
  1456.4 106.4 %copy-start.145 = (f32[2,1024]{1,0:T(2,128)S(1)}, f32[2,1024]{1,0:T(2,128)}, u32[]{:S(2)}) copy-start(f32[2,1024]{1,0:T(2,128)} %param.69) | copy-start | bytes 24580
  (169 other events, 1019.8 us)
Sparse Core Ops, SparseCore 0:
  191.4 95.5 all-reduce.15
  343.6 94.3 all-reduce.13
  549.0 171.0 all-reduce.11
  723.3 120.3 reduce-scatter.5
  847.3 62.7 reduce-scatter.7
  913.4 62.9 reduce-scatter.9
  980.5 94.6 reduce-scatter.13
  1079.2 163.0 reduce-scatter.11
  1292.0 126.2 all-gather.4
  1421.1 94.9 all-gather.2
where the time goes:
time: 1590 us
  waiting for transfers between devices  958 us (60%)
  matrix products  209 us (13%)
  blocking collectives  135 us (8%)
  other arithmetic  125 us (8%)
  local copies, waits for them, and re-layouts  111 us (7%)
  between operations  24.1 us (2%)
  starting transfers between devices  24 us (2%)
    reduce_scatter x1, waiting for transfers between devices, local(): lax.psum_scatter(summed[3], 'dp', scatter_dimension=0, tiled=True)  165 us
    all_to_all x1, waiting for transfers between devices, local(): lax.all_to_all(to_pieces(out_rows, return_order), 'dp', split_axis=0, con...  135 us
    psum x1, waiting for transfers between devices, local(): lax.psum(jnp.dot(inner, w_down, preferred_element_type=jnp.float32).astyp...  112 us
    reduce_scatter x1, waiting for transfers between devices, local(): lax.psum_scatter(summed[4], 'dp', scatter_dimension=1, tiled=True)  95.9 us
    all_to_all x1, waiting for transfers between devices, local(): lax.all_to_all(to_pieces(tokens, send_order), 'dp', split_axis=0, concat_...  88.7 us
    psum x1, waiting for transfers between devices, local(): lax.psum(jnp.einsum('tsf,dsf->td', d_gateup, w_gateup, preferred_element_...  76.7 us
    reduce_scatter x1, waiting for transfers between devices, local(): lax.psum_scatter(summed[0], 'dp', scatter_dimension=0, tiled=True)  73 us
    reduce_scatter x1, waiting for transfers between devices, local(): lax.psum_scatter(summed[1], 'dp', scatter_dimension=0, tiled=True)  64.9 us
  transfers between devices with their start and end apart: 14, of which 11 were waited for; matrix products, arithmetic and copies ran while one was open for 16% of the time, Pallas kernels for 0%

commit v1 on v0

v1 whole, which is shorter than its diff:
```python
import functools
import math

import jax
import jax.numpy as jnp
from jax import lax
from jax.experimental import pallas as pl
from jax.experimental.pallas import tpu as pltpu
from jax.sharding import PartitionSpec as P

D = 1024
H = 16
KV = 8
HD = 64
FF = 4608


EPSILON = 1e-05
ROPE_BASE = 1000000.0
LOW = jnp.bfloat16
FULL = jnp.float32
LANES = 128


def dot(left, right, left_dim=1, right_dim=0):
    return lax.dot_general(
        left, right, (((left_dim,), (right_dim,)), ((), ())), preferred_element_type=FULL
    )


def swap(values, axis, bit):
    size = lax.axis_size(axis)
    return lax.ppermute(values, axis, [(place, place ^ bit) for place in range(size)])


def far(values):
    return swap(values, "mp", 2)


def near(values):
    return swap(values, "mp", 1)


def bits_of(count):
    return [1 << place for place in range(count.bit_length() - 1)]


RELATIVE = (0, 2, 1, 3)
VMEM = pl.BlockSpec(memory_space=pltpu.VMEM)
SMEM = pl.BlockSpec(memory_space=pltpu.SMEM)
VMEM_BYTES = 60 * 1024 * 1024


def group_sums(values, ones):
    high = values.astype(LOW)
    rest = (values - high.astype(FULL)).astype(LOW)
    return dot(high, ones) + dot(rest, ones)


def head_ones(head_dim):
    row = lax.broadcasted_iota(jnp.int32, (LANES, LANES), 0) // head_dim
    col = lax.broadcasted_iota(jnp.int32, (LANES, LANES), 1) // head_dim
    return (row == col).astype(FULL).astype(LOW)


def turn_halves(values, half):
    lane = lax.broadcasted_iota(jnp.int32, values.shape, 1)
    ahead = pltpu.roll(values, LANES - half, 1)
    behind = pltpu.roll(values, half, 1)
    return jnp.where(lane % (2 * half) < half, ahead, behind)


def attend_body(last, dims, *refs):
    rows, pieces, part, block, head_dim, heads = dims
    (member, n_own, n_near, w_q, w_kv, cos, sin, start, gain_q, gain_k) = refs[:10]
    refs = refs[10:]
    if last:
        (w_o, w_o_first, mixed_first) = refs[:3]
        refs = refs[3:]
    (mixed, raw, inverse, q_pair, k_lo, k_hi, v_lo, v_hi) = refs[:8]
    refs = refs[8:]
    if last:
        (sum_own, sum_near) = refs[:2]
        refs = refs[2:]
    (by_token, a_token, r_token) = refs
    quarter_rows = pieces * part
    piece = 4 * part
    ones = head_ones(head_dim)

    def place(k, p):
        quarter = member[0] ^ RELATIVE[k]
        return pl.multiple_of(p * piece + quarter * part, 8)

    for k in range(4):
        here = pl.ds(k * quarter_rows, quarter_rows)
        source = n_own if k < 2 else n_near
        n_rows = source[(k % 2) * quarter_rows : (k % 2 + 1) * quarter_rows, :]
        query = dot(n_rows, w_q[...])
        keyval = dot(n_rows, w_kv[...])
        raw[here, : heads * LANES] = query.astype(LOW)
        raw[here, heads * LANES :] = keyval[:, :LANES].astype(LOW)
        parts = [query[:, h * LANES : (h + 1) * LANES] for h in range(heads)]
        parts.append(keyval[:, :LANES])
        turned = []
        for index, values in enumerate(parts):
            gain = gain_k if index == heads else gain_q
            mean = group_sums(values * values, ones) * (1.0 / head_dim)
            normed = values * lax.rsqrt(mean + EPSILON) * gain[...]
            turned.append(
                normed * cos[here, :] + turn_halves(normed, head_dim // 2) * sin[here, :]
            )
        turned.append(keyval[:, LANES:])
        for p in range(pieces):
            there = pl.ds(place(k, p), part)
            for index, values in enumerate(turned):
                by_token[index, there, :] = values[p * part : (p + 1) * part, :]

    scale = head_dim ** (-0.5)

    def prepare(i, carry):
        there = pl.ds(pl.multiple_of(i * block, block), block)
        low = lax.broadcasted_iota(jnp.int32, (block, LANES), 1) < head_dim
        for h in range(heads):
            q_pair[h, there, :] = (by_token[h, there, :] * scale).astype(LOW)
        key = by_token[heads, there, :]
        value = by_token[heads + 1, there, :]
        key_low = jnp.where(low, key, 0.0)
        key_high = jnp.where(low, 0.0, key)
        value_low = jnp.where(low, value, 1.0)
        value_high = jnp.where(low, 1.0, value)
        k_lo[0, there, :] = key_low.astype(LOW)
        k_hi[0, there, :] = pltpu.roll(key_low, head_dim, 1).astype(LOW)
        k_lo[1, there, :] = pltpu.roll(key_high, head_dim, 1).astype(LOW)
        k_hi[1, there, :] = key_high.astype(LOW)
        v_lo[0, there, :] = value_low.astype(LOW)
        v_hi[0, there, :] = pltpu.roll(value_low, head_dim, 1).astype(LOW)
        v_lo[1, there, :] = pltpu.roll(value_high, head_dim, 1).astype(LOW)
        v_hi[1, there, :] = value_high.astype(LOW)
        return carry

    lax.fori_loop(0, rows // block, prepare, 0)

    def one_head(h, carry):
        for i in range(rows // block):
            here = pl.ds(i * block, block)
            end = (i + 1) * block
            query = q_pair[h, here, :]
            key_row = lax.broadcasted_iota(jnp.int32, (block, end), 1)
            query_row = lax.broadcasted_iota(jnp.int32, (block, end), 0) + i * block
            seen = (key_row <= query_row) & (key_row >= start[here, :])
            mixed_parts = []
            for keys, values in ((k_lo, v_lo), (k_hi, v_hi)):
                scores = dot(query, keys[h, :end, :], 1, 1)
                weight = jnp.where(seen, jnp.exp(scores), 0.0).astype(LOW)
                mixed_parts.append(dot(weight, values[h, :end, :]))
            even, odd = mixed_parts
            low = lax.broadcasted_iota(jnp.int32, (block, LANES), 1) < head_dim
            divided = 1.0 / pltpu.roll(jnp.where(low, odd, even), head_dim, 1)
            a_token[h, here, :] = jnp.where(low, even, odd) * divided
            r_token[h, here, :] = divided
        return carry

    lax.fori_loop(0, heads, one_head, 0)

    for k in range(4):
        here = pl.ds(k * quarter_rows, quarter_rows)
        for h in range(heads):
            pieces_a = [a_token[h, pl.ds(place(k, p), part), :] for p in range(pieces)]
            pieces_r = [r_token[h, pl.ds(place(k, p), part), :] for p in range(pieces)]
            mixed[here, h * LANES : (h + 1) * LANES] = jnp.concatenate(pieces_a, axis=0).astype(LOW)
            inverse[h, here, :] = jnp.concatenate(pieces_r, axis=0)
        if last:
            total = dot(mixed[here, :], w_o[...]) + dot(mixed_first[here, :], w_o_first[...])
            target = sum_own if k < 2 else sum_near
            target[(k % 2) * quarter_rows : (k % 2 + 1) * quarter_rows, :] = total.astype(LOW)


def attend_back_body(last, dims, *refs):
    rows, pieces, part, block, head_dim, heads = dims
    (member, d_own, d_near, w_o, mixed, inverse, raw, cos, sin, start, gain_q, gain_k) = refs[:12]
    (q_pair, k_lo, k_hi, v_lo, v_hi) = refs[12:17]
    refs = refs[17:]
    if last:
        (w_q, w_kv, w_q_first, w_kv_first, d_raw_first) = refs[:5]
        refs = refs[5:]
    (d_raw, gains) = refs[:2]
    refs = refs[2:]
    if last:
        (sum_own, sum_near) = refs[:2]
        refs = refs[2:]
    (grad_token, grad_even, grad_odd, dq_token, dk_token, dv_token) = refs
    quarter_rows = pieces * part
    piece = 4 * part
    ones = head_ones(head_dim)
    scale = head_dim ** (-0.5)

    def place(k, p):
        quarter = member[0] ^ RELATIVE[k]
        return pl.multiple_of(p * piece + quarter * part, 8)

    for k in range(4):
        here = pl.ds(k * quarter_rows, quarter_rows)
        source = d_own if k < 2 else d_near
        d_rows = source[(k % 2) * quarter_rows : (k % 2 + 1) * quarter_rows, :]
        d_mixed = dot(d_rows, w_o[...], 1, 1)
        lane = lax.broadcasted_iota(jnp.int32, (quarter_rows, LANES), 1)
        low = lane < head_dim
        for h in range(heads):
            cols = slice(h * LANES, (h + 1) * LANES)
            grad = d_mixed[:, cols] * inverse[h, here, :]
            delta = group_sums(grad * mixed[here, cols].astype(FULL), ones)
            other = -pltpu.roll(delta, head_dim, 1)
            high = other.astype(LOW).astype(FULL)
            extra = jnp.where(lane % head_dim == 0, high, 0.0)
            extra = jnp.where(lane % head_dim == 1, other - high, extra)
            even = jnp.where(low, grad, extra)
            odd = jnp.where(low, extra, grad)
            for p in range(pieces):
                there = pl.ds(place(k, p), part)
                grad_token[2 * h, there, :] = even[p * part : (p + 1) * part, :]
                grad_token[2 * h + 1, there, :] = odd[p * part : (p + 1) * part, :]

    def prepare(i, carry):
        there = pl.ds(pl.multiple_of(i * block, block), block)
        for h in range(heads):
            grad_even[h, there, :] = grad_token[2 * h, there, :].astype(LOW)
            grad_odd[h, there, :] = grad_token[2 * h + 1, there, :].astype(LOW)
            dq_token[h, there, :] = jnp.zeros((block, LANES), FULL)
        return carry

    lax.fori_loop(0, rows // block, prepare, 0)

    def one_head(h, carry):
        for i in range(rows // block):
            first = i * block
            count = rows - first
            here = pl.ds(first, block)
            after = pl.ds(first, count)
            query = q_pair[h, after, :]
            key_row = lax.broadcasted_iota(jnp.int32, (block, count), 0)
            query_row = lax.broadcasted_iota(jnp.int32, (block, count), 1)
            seen = (key_row <= query_row) & (key_row + first >= start[:, after])
            d_keys = []
            d_values = []
            d_query = None
            for keys, values, grads in ((k_lo, v_lo, grad_even), (k_hi, v_hi, grad_odd)):
                key = keys[h, here, :]
                grad = grads[h, after, :]
                weight = jnp.where(seen, jnp.exp(dot(key, query, 1, 1)), 0.0)
                d_scores = (weight * dot(values[h, here, :], grad, 1, 1)).astype(LOW)
                d_values.append(dot(weight.astype(LOW), grad))
                d_keys.append(dot(d_scores, query))
                moved = dot(d_scores, key, 0, 0)
                d_query = moved if d_query is None else d_query + moved
            dq_token[h, after, :] += d_query
            low = lax.broadcasted_iota(jnp.int32, (block, LANES), 1) < head_dim
            for (even, odd), kept in ((d_keys, dk_token), (d_values, dv_token)):
                kept[h, here, :] = even + pltpu.roll(odd, head_dim, 1)
        return carry

    lax.fori_loop(0, heads, one_head, 0)

    gain_sums = [jnp.zeros((8, LANES), FULL), jnp.zeros((8, LANES), FULL)]
    for k in range(4):
        here = pl.ds(k * quarter_rows, quarter_rows)
        low = lax.broadcasted_iota(jnp.int32, (quarter_rows, LANES), 1) < head_dim

        def rows_of(token, h):
            return jnp.concatenate(
                [token[h, pl.ds(place(k, p), part), :] for p in range(pieces)], axis=0
            )

        def pair_of(token):
            return jnp.where(
                low, rows_of(token, 0), pltpu.roll(rows_of(token, 1), head_dim, 1)
            )

        turned = [rows_of(dq_token, h) * scale for h in range(heads)] + [pair_of(dk_token)]
        for index, values in enumerate(turned):
            is_key = index == heads
            gain = gain_k if is_key else gain_q
            cols = slice(index * LANES, (index + 1) * LANES)
            held = raw[here, cols].astype(FULL)
            root = lax.rsqrt(group_sums(held * held, ones) * (1.0 / head_dim) + EPSILON)
            normed = held * root
            back = values * cos[here, :] - turn_halves(values, head_dim // 2) * sin[here, :]
            scaled = back * gain[...]
            mean = group_sums(scaled * normed, ones) * (1.0 / head_dim)
            d_raw[here, cols] = (root * (scaled - normed * mean)).astype(LOW)
            products = (back * normed).reshape(quarter_rows // 8, 8, LANES)
            gain_sums[int(is_key)] = gain_sums[int(is_key)] + jnp.sum(products, axis=0)
        d_raw[here, (heads + 1) * LANES :] = pair_of(dv_token).astype(LOW)
        if last:
            wide = heads * LANES
            total = dot(d_raw[here, :wide], w_q[...], 1, 1)
            total = total + dot(d_raw[here, wide:], w_kv[...], 1, 1)
            total = total + dot(d_raw_first[here, :wide], w_q_first[...], 1, 1)
            total = total + dot(d_raw_first[here, wide:], w_kv_first[...], 1, 1)
            target = sum_own if k < 2 else sum_near
            target[(k % 2) * quarter_rows : (k % 2 + 1) * quarter_rows, :] = total.astype(LOW)
    gains[:8, :] = gain_sums[0]
    gains[8:, :] = gain_sums[1]


def feed_body(chunk, n_own, n_near, c_own, c_near, w_gate, w_up, w_down, *refs):
    refs = refs[-7:]
    (inner, d_gate, d_up, n_all, c_all, d_norm, partial) = refs
    step = pl.program_id(0)

    def run(n_ref, c_ref):
        n_rows = n_ref[...]
        c_rows = c_ref[...]
        n_all[...] = n_rows
        c_all[...] = c_rows
        hidden = w_gate.shape[1]
        total_n = None
        total_y = None
        for begin in range(0, hidden, chunk):
            cols = slice(begin, begin + chunk)
            gate = dot(n_rows, w_gate[:, cols])
            up_part = dot(n_rows, w_up[:, cols])
            d_inner = dot(c_rows, w_down[cols, :], 1, 1)
            sigma = 1.0 / (1.0 + jnp.exp(-gate))
            held = gate * sigma
            inner_low = (held * up_part).astype(LOW)
            d_gate_low = (d_inner * up_part * sigma * (1.0 + gate * (1.0 - sigma))).astype(LOW)
            d_up_low = (d_inner * held).astype(LOW)
            inner[:, cols] = inner_low
            d_gate[:, cols] = d_gate_low
            d_up[:, cols] = d_up_low
            more_n = dot(d_gate_low, w_gate[:, cols], 1, 1) + dot(d_up_low, w_up[:, cols], 1, 1)
            more_y = dot(inner_low, w_down[cols, :])
            total_n = more_n if total_n is None else total_n + more_n
            total_y = more_y if total_y is None else total_y + more_y
        d_norm[...] = total_n.astype(LOW)
        partial[...] = total_y.astype(LOW)

    @pl.when(step == 0)
    def _():
        run(n_own, c_own)

    @pl.when(step == 1)
    def _():
        run(n_near, c_near)


def feed(half, kept, n_own, n_near, c_own, c_near, w_gate, w_up, w_down):
    rows, width = n_own.shape
    hidden = w_gate.shape[1]
    whole = lambda shape: pl.BlockSpec(shape, lambda i: (0, 0))
    part = lambda cols: pl.BlockSpec((rows, cols), lambda i: (i + 2 * half, 0))
    in_specs = [whole(v.shape) for v in (n_own, n_near, c_own, c_near, w_gate, w_up, w_down)]
    all_rows = [
        jax.ShapeDtypeStruct((4 * rows, cols), LOW) for cols in (hidden, hidden, hidden, width, width)
    ]
    outs = all_rows + [jax.ShapeDtypeStruct((2 * rows, width), LOW)] * 2
    out_specs = [part(hidden)] * 3 + [part(width)] * 2
    out_specs += [pl.BlockSpec((rows, width), lambda i: (i, 0))] * 2
    aliases = {}
    if half:
        in_specs += [pl.BlockSpec(memory_space=pl.ANY)] * 5
        aliases = {7 + index: index for index in range(5)}
    work = 2 * rows * width * hidden * 2 * 6
    return pl.pallas_call(
        functools.partial(feed_body, hidden // 3),
        grid=(2,),
        in_specs=in_specs,
        out_specs=out_specs,
        out_shape=outs,
        input_output_aliases=aliases,
        compiler_params=pltpu.CompilerParams(
            vmem_limit_bytes=VMEM_BYTES, dimension_semantics=("arbitrary",)
        ),
        cost_estimate=pl.CostEstimate(
            flops=work, bytes_accessed=12 * rows * width * 4, transcendentals=0
        ),
    )(n_own, n_near, c_own, c_near, w_gate, w_up, w_down, *(kept if half else ()))


def each(count, act):
    if count <= 8:
        for index in range(count):
            act(index)
    else:
        lax.fori_loop(0, count, lambda index, carry: (act(index), carry)[1], 0)


def fetch(copies):
    for count, copy_of in copies:
        each(count, lambda index: copy_of(index).start())
    for count, copy_of in copies:
        each(count, lambda index: copy_of(index).wait())


HELD = pl.BlockSpec(memory_space=pl.ANY)


def pick_body(order, source, target, arrived):
    def copy_of(index):
        return pltpu.make_async_copy(
            source.at[order[index]], target.at[index], arrived.at[index]
        )

    fetch([(order.shape[0], copy_of)])


def pick(values, order):
    count = order.shape[0]
    return pl.pallas_call(
        pick_body,
        in_specs=[SMEM, HELD],
        out_specs=VMEM,
        out_shape=jax.ShapeDtypeStruct((count,) + values.shape[1:], values.dtype),
        scratch_shapes=[pltpu.SemaphoreType.DMA((count,))],
        compiler_params=pltpu.CompilerParams(vmem_limit_bytes=VMEM_BYTES),
    )(order, values)


def across_dp(values):
    return lax.all_to_all(values, "dp", split_axis=0, concat_axis=0, tiled=True)


def join_body(first_order, second_order, first, second, target, arrived):
    count = first_order.shape[0]

    def first_copy(index):
        return pltpu.make_async_copy(
            first.at[first_order[index]], target.at[index], arrived.at[index]
        )

    def second_copy(index):
        return pltpu.make_async_copy(
            second.at[second_order[index]], target.at[count + index], arrived.at[count + index]
        )

    fetch([(count, first_copy), (count, second_copy)])


def join(first, first_order, second, second_order):
    count = first_order.shape[0]
    return pl.pallas_call(
        join_body,
        in_specs=[SMEM, SMEM, HELD, HELD],
        out_specs=VMEM,
        out_shape=jax.ShapeDtypeStruct((2 * count,) + first.shape[1:], first.dtype),
        scratch_shapes=[pltpu.SemaphoreType.DMA((2 * count,))],
        compiler_params=pltpu.CompilerParams(vmem_limit_bytes=VMEM_BYTES),
    )(first_order, second_order, first, second)


def place_body(order, member, *refs):
    sources = refs[:4]
    target, arrived = refs[4:]
    copies = []
    for k, source in enumerate(sources):

        def copy_of(index, k=k, source=source):
            return pltpu.make_async_copy(
                source.at[order[index]],
                target.at[index, member[0] ^ RELATIVE[k]],
                arrived.at[k, index],
            )

        copies.append((order.shape[0], copy_of))
    fetch(copies)


def place_pieces(parts, order, member):
    count, part_rows, width = parts[0].shape
    pieces = pl.pallas_call(
        place_body,
        in_specs=[SMEM, SMEM] + [HELD] * 4,
        out_specs=VMEM,
        out_shape=jax.ShapeDtypeStruct((count, 4, part_rows, width), parts[0].dtype),
        scratch_shapes=[pltpu.SemaphoreType.DMA((4, count))],
        compiler_params=pltpu.CompilerParams(vmem_limit_bytes=VMEM_BYTES),
    )(order, member, *parts)
    return pieces.reshape(count * 4 * part_rows, width)


def fence(*values):
    return lax.optimization_barrier(values)


def reduce_step(total, step, device):
    bit = (device // step) & 1
    split = total.reshape((total.shape[0] // 2, 2) + total.shape[1:])
    sent = lax.dynamic_index_in_dim(split, 1 - bit, 1, keepdims=False).astype(LOW)
    kept = lax.dynamic_index_in_dim(split, bit, 1, keepdims=False)
    return (kept, swap(sent, "dp", step))


def add(first, second):
    return first.astype(FULL) + second.astype(FULL)


def reduce_rest(kept, got, steps, device):
    for step in steps:
        kept, got = reduce_step(add(kept, got), step, device)
    return add(kept, got)[0]


def by_device(product, devices):
    return product.reshape((devices, product.shape[0] // devices) + product.shape[1:])


def gather_dp(own, devices):
    held = own[None]
    for step in reversed(bits_of(devices)):
        held = jnp.concatenate([held, swap(held, "dp", step)], axis=0)
    return held


def places_of(devices, device):
    apart = jnp.arange(devices, dtype=jnp.int32) ^ device
    place = jnp.zeros_like(apart)
    for index, step in enumerate(bits_of(devices)):
        place = place + ((apart // step) & 1) * (devices // 2 // step)
    return place


def row_norm(values, gain_row):
    inverse = lax.rsqrt(jnp.mean(values * values, axis=-1, keepdims=True) + EPSILON)
    return (values * inverse * gain_row, inverse)


def row_norm_back(gradient, values, inverse, gain_row):
    scaled = gradient * gain_row
    d_values = inverse * scaled - values * (inverse * inverse * inverse) * jnp.mean(
        scaled * values, axis=-1, keepdims=True
    )
    d_gain = jnp.sum(gradient * values * inverse, axis=0)
    return (d_values, d_gain)


def local(
    tokens,
    cotangent,
    seq_lengths,
    deal,
    w_query,
    w_keyval,
    w_output,
    w_gateup,
    w_down,
    norm_gains,
    head_gains,
    master_query,
    master_keyval,
    master_output,
    master_gateup,
    master_down,
    start_query,
    start_keyval,
    start_output,
    start_gateup,
    start_down,
    start_norms,
    start_heads,
    step_size,
):
    devices = lax.axis_size("dp")
    ways = lax.axis_size("mp")
    device = lax.axis_index("dp")
    member = lax.axis_index("mp")
    row_count, width = tokens.shape
    total_pieces = deal.shape[0]
    pieces_dev = total_pieces // devices
    piece_rows = row_count // pieces_dev
    part_rows = piece_rows // ways
    slot_count = seq_lengths.shape[0]
    slot_rows = row_count // slot_count
    slot_pieces = pieces_dev // slot_count
    quarter_rows = slot_pieces * part_rows
    half_rows = 2 * quarter_rows
    head_dim = head_gains.shape[1]
    query_cols = w_query.shape[1]
    key_cols = w_keyval.shape[2]
    heads = query_cols // LANES
    hidden = w_down.shape[0]
    step = step_size[0]
    slot = member // 2
    member_ref = member.reshape(1).astype(jnp.int32)

    placed = jnp.arange(pieces_dev, dtype=jnp.int32)
    my_places = lax.dynamic_slice_in_dim(deal, device * pieces_dev, pieces_dev)
    target = my_places // pieces_dev
    piece_to = jnp.sum((target[:, None] == placed[None, :]) * placed[:, None], axis=0)
    whole = jnp.arange(total_pieces, dtype=jnp.int32)
    held_here = deal[:, None] == (device * pieces_dev + placed)[None, :]
    source = jnp.sum(held_here * (whole // pieces_dev)[:, None], axis=0)
    place_from = jnp.sum((source[:, None] == placed[None, :]) * placed[:, None], axis=0)
    slot_source = source.reshape(slot_count, slot_pieces)
    own_source = lax.dynamic_index_in_dim(slot_source, slot, 0, keepdims=False)
    other_source = lax.dynamic_index_in_dim(slot_source, 1 - slot, 0, keepdims=False)
    in_order = jnp.arange(slot_pieces, dtype=jnp.int32)

    def deal_in(values):
        quarters = values.reshape(pieces_dev * ways, part_rows, width)
        return across_dp(pick(quarters, piece_to * ways + member))

    def rows_of(pieces):
        return pieces.reshape(-1, width)

    x_got = deal_in(tokens)

    lengths = lax.dynamic_index_in_dim(seq_lengths, slot, 0, keepdims=False)
    ends = jnp.cumsum(lengths)

    def position_of(token):
        passed = (token[:, None] >= ends[None, :]).astype(jnp.int32)
        return token - jnp.sum(passed * lengths[None, :], axis=1)

    token_row = jnp.arange(slot_rows, dtype=jnp.int32)
    start = token_row - position_of(token_row)
    quarters = jnp.asarray(RELATIVE, jnp.int32) ^ member
    relative_token = (
        (in_order * piece_rows)[None, :, None]
        + (quarters * part_rows)[:, None, None]
        + jnp.arange(part_rows, dtype=jnp.int32)[None, None, :]
    ).reshape(-1)
    lane = jnp.arange(LANES, dtype=jnp.int32)
    half = head_dim // 2
    freqs = ROPE_BASE ** (-(lane % half).astype(FULL) * (2.0 / head_dim))
    angles = position_of(relative_token).astype(FULL)[:, None] * freqs[None, :]
    cosine = jnp.cos(angles)
    sine = jnp.sin(angles) * jnp.where(lane % head_dim < half, -1.0, 1.0)[None, :]
    gain_q = jnp.tile(head_gains[0:1], (1, LANES // head_dim))
    gain_k = jnp.tile(head_gains[1:2], (1, LANES // head_dim))

    w_keyval_flat = w_keyval.reshape(width, 2 * key_cols)
    groups = (
        (w_query, w_keyval_flat, w_output),
        (far(w_query), far(w_keyval_flat), far(w_output)),
    )
    w_gate = w_gateup[:, 0]
    w_up = w_gateup[:, 1]

    def ahead(master, begin):
        return (master - 0.5 * step * begin).astype(LOW)

    small = jnp.concatenate(
        [
            ahead(master_query, start_query),
            ahead(master_keyval, start_keyval).reshape(-1, 2 * key_cols),
            ahead(master_output, start_output).T,
        ],
        axis=1,
    )
    part_gateup = ahead(master_gateup, start_gateup)
    part_down = ahead(master_down, start_down)

    early = fence(x_got, small, part_gateup, part_down, cosine, sine, w_gate, w_up, groups)
    x_got, small, part_gateup, part_down, cosine, sine, w_gate, w_up, groups = early
    x_other = far(pick(x_got, other_source))
    cotangent, _ = fence(cotangent, x_got)
    c_got = deal_in(cotangent)
    x_own = rows_of(join(x_got, own_source, x_other, in_order))
    ahead_small = lax.all_gather(small, "dp", axis=0, tiled=True)
    ahead_gateup = lax.all_gather(part_gateup, "dp", axis=0, tiled=True)
    ahead_down = lax.all_gather(part_down, "dp", axis=0, tiled=False)

    x_full = x_own.astype(FULL)
    norm_one_f, inv_one = row_norm(x_full, norm_gains[0])
    norm_own = norm_one_f.astype(LOW)
    norm_near = near(norm_own)

    dims = (slot_rows, slot_pieces, part_rows, slot_rows // 6, head_dim, heads)
    shape = jax.ShapeDtypeStruct

    def attend(last, weights, more):
        token_shape = (heads, slot_rows, LANES)
        outs = [
            shape((slot_rows, query_cols), LOW),
            shape((slot_rows, query_cols + key_cols), LOW),
            shape(token_shape, FULL),
        ] + [shape(token_shape, LOW)] * 5
        if last:
            outs += [shape((half_rows, width), LOW)] * 2
        arguments = (
            member_ref,
            norm_own,
            norm_near,
            weights[0],
            weights[1],
            cosine,
            sine,
            start.reshape(-1, 1),
            gain_q,
            gain_k,
        ) + more
        return pl.pallas_call(
            functools.partial(attend_body, last, dims),
            in_specs=[SMEM] + [VMEM] * (len(arguments) - 1),
            out_specs=[VMEM] * len(outs),
            out_shape=outs,
            scratch_shapes=[
                pltpu.VMEM((heads + 2, slot_rows, LANES), FULL),
                pltpu.VMEM((heads, slot_rows, LANES), FULL),
                pltpu.VMEM((heads, slot_rows, LANES), FULL),
            ],
            compiler_params=pltpu.CompilerParams(vmem_limit_bytes=VMEM_BYTES),
            cost_estimate=pl.CostEstimate(
                flops=12_000_000_000, bytes_accessed=12_000_000, transcendentals=0
            ),
        )(*arguments)

    def attend_back(last, weights, kept, d_own, d_near, more):
        token_shape = (heads, slot_rows, LANES)
        mixed, raw, inverse, *tables = kept
        outs = [shape((slot_rows, query_cols + 2 * key_cols), LOW), shape((16, LANES), FULL)]
        if last:
            outs += [shape((half_rows, width), LOW)] * 2
        arguments = (
            member_ref,
            d_own,
            d_near,
            weights[2],
            mixed,
            inverse,
            raw,
            cosine,
            sine,
            start.reshape(1, -1),
            gain_q,
            gain_k,
            *tables,
        ) + more
        return pl.pallas_call(
            functools.partial(attend_back_body, last, dims),
            in_specs=[SMEM] + [VMEM] * (len(arguments) - 1),
            out_specs=[VMEM] * len(outs),
            out_shape=outs,
            scratch_shapes=[
                pltpu.VMEM((2 * heads, slot_rows, LANES), FULL),
                pltpu.VMEM(token_shape, LOW),
                pltpu.VMEM(token_shape, LOW),
                pltpu.VMEM(token_shape, FULL),
                pltpu.VMEM(token_shape, FULL),
                pltpu.VMEM(token_shape, FULL),
            ],
            compiler_params=pltpu.CompilerParams(vmem_limit_bytes=VMEM_BYTES),
            cost_estimate=pl.CostEstimate(
                flops=20_000_000_000, bytes_accessed=14_000_000, transcendentals=0
            ),
        )(*arguments)

    first_kept = attend(False, groups[0], ())
    c_got, first_kept = fence(c_got, first_kept)
    c_own_far = far(pick(c_got, other_source))
    c_other_far = far(pick(c_got, own_source))
    *second_kept, attn_own, attn_near = attend(
        True, groups[1], (groups[1][2], groups[0][2], first_kept[0])
    )
    c_own = rows_of(join(c_got, own_source, c_own_far, in_order))
    c_near = near(c_own)
    attn_sum = add(attn_own, near(attn_near))
    hidden_one = x_full + attn_sum
    norm_two_f, inv_two = row_norm(hidden_one, norm_gains[1])
    two_own = norm_two_f.astype(LOW)
    two_near = near(two_own)
    two_far = far(two_own)
    two_across = near(two_far)
    c_far = rows_of(join(c_other_far, in_order, c_got, other_source))
    c_across = near(c_far)

    *kept, d_two_own, ffn_own = feed(0, (), two_own, two_near, c_own, c_near, w_gate, w_up, w_down)
    near_own = near(d_two_own[half_rows:])
    *kept, d_two_far, ffn_far = feed(
        1, kept, two_far, two_across, c_far, c_across, w_gate, w_up, w_down
    )
    near_far = near(d_two_far[half_rows:])
    pair_far = add(d_two_far[:half_rows], near_far).astype(LOW)
    pair_far, kept, ffn_far = fence(pair_far, kept, ffn_far)
    inner, d_gate, d_up, two_all, c_all = kept
    pair_got = far(pair_far)
    grad_down = dot(c_all, inner, 0, 0).astype(LOW)
    grad_gate = dot(two_all, d_gate, 0, 0).astype(LOW)
    grad_up = dot(two_all, d_up, 0, 0).astype(LOW)
    ffn_pair_far = add(ffn_far[:half_rows], near(ffn_far[half_rows:])).astype(LOW)
    ffn_pair_own = add(ffn_own[:half_rows], near(ffn_own[half_rows:]))
    stepped = fence(pair_got, grad_down, grad_gate, grad_up, ffn_pair_far)
    pair_got, grad_down, grad_gate, grad_up, ffn_pair_far = stepped
    steps = bits_of(devices)
    down_kept, down_got = reduce_step(by_device(grad_down, devices), steps[0], device)
    gate_kept, gate_got = reduce_step(by_device(grad_gate, devices), steps[0], device)
    up_kept, up_got = reduce_step(by_device(grad_up, devices), steps[0], device)
    ffn_got = far(ffn_pair_far)

    d_norm_two = add(d_two_own[:half_rows], near_own) + pair_got.astype(FULL)
    d_hidden_part, gain_two = row_norm_back(d_norm_two, hidden_one, inv_two, norm_gains[1])
    d_hidden = c_own.astype(FULL) + d_hidden_part
    dh_own = d_hidden.astype(LOW)
    dh_near = near(dh_own)

    def over_rows(own, other, values):
        return dot(own, values[:half_rows], 0, 0) + dot(other, values[half_rows:], 0, 0)

    d_raw_far, gains_far = attend_back(False, groups[1], second_kept, dh_own, dh_near, ())
    stepped = fence(d_raw_far, down_got, gate_got, ffn_got)
    d_raw_far, down_got, gate_got, ffn_got = stepped
    down_kept, down_got = reduce_step(add(down_kept, down_got), steps[1], device)
    gate_kept, gate_got = reduce_step(add(gate_kept, gate_got), steps[1], device)
    out_own = (hidden_one + ffn_pair_own + ffn_got.astype(FULL)).astype(LOW)
    out_other = far(out_own[quarter_rows:])
    grad_output_got = far(over_rows(dh_own, dh_near, second_kept[0]).astype(LOW))
    grad_qkv_got = far(over_rows(norm_own, norm_near, d_raw_far).astype(LOW))
    grad_output_mine = over_rows(dh_own, dh_near, first_kept[0])
    d_raw_own, gains_own, d_one_own, d_one_near = attend_back(
        True,
        groups[0],
        first_kept,
        dh_own,
        dh_near,
        (groups[0][0], groups[0][1], groups[1][0], groups[1][1], d_raw_far),
    )
    stepped = fence(d_raw_own, d_one_near, down_got, gate_got, up_got, out_other, grad_output_got)
    d_raw_own, d_one_near, down_got, gate_got, up_got, out_other, grad_output_got = stepped
    d_norm_one = add(d_one_own, near(d_one_near))
    d_input_part, gain_one = row_norm_back(d_norm_one, x_full, inv_one, norm_gains[0])
    dx_own = (d_hidden + d_input_part).astype(LOW)

    own_down = reduce_rest(down_kept, down_got, steps[2:], device)
    own_gate = reduce_rest(gate_kept, gate_got, steps[2:], device)
    own_up = reduce_rest(up_kept, up_got, steps[1:], device)
    grad_output = add(grad_output_mine, grad_output_got)
    grad_qkv = add(over_rows(norm_own, norm_near, d_raw_own), grad_qkv_got)
    own_output = reduce_rest(
        *reduce_step(by_device(grad_output, devices), steps[0], device), steps[1:], device
    )
    own_qkv = reduce_rest(
        *reduce_step(by_device(grad_qkv, devices), steps[0], device), steps[1:], device
    )

    def deal_out(values, other):
        mine = values[:quarter_rows].reshape(slot_pieces, part_rows, width)
        other = other.reshape(slot_pieces, part_rows, width)
        held = jnp.concatenate([mine, other], axis=0)
        order = (place_from + (slot_count - slot) * slot_pieces) % pieces_dev
        got = across_dp(pick(held, order))
        got_far = far(got)
        return place_pieces((got, got_far, near(got), near(got_far)), target, member_ref)

    output = deal_out(out_own, out_other)
    input_grad = deal_out(dx_own, far(dx_own[quarter_rows:]))

    owned = (own_qkv, own_output, own_gate, own_up, own_down)
    own_square = sum([jnp.sum(part_grad * part_grad) for part_grad in owned])
    gains = jnp.sum((gains_far + gains_own).reshape(2, 8, LANES // head_dim, head_dim), axis=(1, 2))
    packed = jnp.concatenate(
        [gain_one, gain_two, gains.reshape(-1), jnp.broadcast_to(own_square, (LANES,))]
    ).reshape(-1, LANES)
    for axis, size in (("mp", ways), ("dp", devices)):
        for bit in bits_of(size):
            packed = packed + swap(packed, axis, bit)
    flat = packed.reshape(-1)
    norm_sum = flat[: 2 * width].reshape(2, width)
    head_sum = flat[2 * width : 2 * width + 2 * head_dim].reshape(2, head_dim)
    square_sum = flat[2 * width + 2 * head_dim]
    clip_value = jnp.sqrt(square_sum + jnp.sum(norm_sum * norm_sum) + jnp.sum(head_sum * head_sum))
    limit = math.sqrt(2 * D * H * HD + 2 * D * KV * HD + 3 * D * FF + 2 * D + 2 * HD)
    factor = jnp.minimum(1.0, limit / clip_value)

    owned_parts = (
        own_qkv[:, :query_cols],
        own_qkv[:, query_cols:].reshape(-1, 2, key_cols),
        own_output.T,
        jnp.stack([own_gate, own_up], axis=1),
        own_down.T,
    )
    starts = (start_query, start_keyval, start_output, start_gateup, start_down)
    masters = (master_query, master_keyval, master_output, master_gateup, master_down)
    moments = [0.5 * begin + factor * part_grad for begin, part_grad in zip(starts, owned_parts)]
    nexts = [held - step * moved for held, moved in zip(masters, moments)]
    moment_norms = 0.5 * start_norms + factor * norm_sum
    moment_heads = 0.5 * start_heads + factor * head_sum
    next_norms = norm_gains - step * moment_norms
    next_heads = head_gains - step * moment_heads

    order = places_of(devices, device)

    def spread(own):
        return pick(gather_dp(own.astype(LOW), devices), order)

    all_qkv = spread(own_qkv).reshape(width, -1)
    all_output = spread(own_output).reshape(width, -1)
    all_gateup = spread(owned_parts[3]).reshape(width, 2, hidden)
    all_down = spread(owned_parts[4])
    pull = step * factor

    def finish(ahead_part, gradient):
        return (ahead_part.astype(FULL) - pull * gradient.astype(FULL)).astype(LOW)

    done_small = finish(ahead_small, jnp.concatenate([all_qkv, all_output], axis=1))
    weights = (
        done_small[:, :query_cols],
        done_small[:, query_cols : query_cols + 2 * key_cols].reshape(width, 2, key_cols),
        done_small[:, query_cols + 2 * key_cols :].T,
        finish(ahead_gateup, all_gateup),
        finish(ahead_down, all_down).transpose(1, 0, 2).reshape(hidden, width),
    )
    return (
        output,
        input_grad,
        clip_value.reshape(1),
        *moments,
        moment_norms,
        moment_heads,
        *nexts,
        next_norms,
        next_heads,
        *weights,
    )


def solution(mesh):
    in_specs = (
        P("dp", None),
        P("dp", None),
        P("dp", None),
        P(),
        P(None, "mp"),
        P(None, None, "mp"),
        P("mp", None),
        P(None, None, "mp"),
        P("mp", None),
        P(),
        P(),
        P("dp", "mp"),
        P("dp", None, "mp"),
        P("mp", "dp"),
        P("dp", None, "mp"),
        P("mp", "dp"),
        P("dp", "mp"),
        P("dp", None, "mp"),
        P("mp", "dp"),
        P("dp", None, "mp"),
        P("mp", "dp"),
        P(),
        P(),
        P(),
    )
    out_specs = (
        P("dp", None),
        P("dp", None),
        P(),
        P("dp", "mp"),
        P("dp", None, "mp"),
        P("mp", "dp"),
        P("dp", None, "mp"),
        P("mp", "dp"),
        P(),
        P(),
        P("dp", "mp"),
        P("dp", None, "mp"),
        P("mp", "dp"),
        P("dp", None, "mp"),
        P("mp", "dp"),
        P(),
        P(),
        P(None, "mp"),
        P(None, None, "mp"),
        P("mp", None),
        P(None, None, "mp"),
        P("mp", None),
    )
    return jax.shard_map(local, mesh=mesh, in_specs=in_specs, out_specs=out_specs, check_vma=False)
```

time: 1590 us -> 830 us (0.52)
  waiting for transfers between devices: 958 us -> 257 us
  Pallas kernels: 0 us -> 205 us
  matrix products: 209 us -> 40.9 us
  blocking collectives: 135 us -> 0 us
  starting transfers between devices: 24 us -> 80.7 us
  local copies, waits for them, and re-layouts: 111 us -> 88.5 us
    reduce_scatter x5 -> x0, waiting for transfers between devices: 462 us -> none  [the longest x1 165 us: local(): lax.psum_scatter(summed[3], 'dp', scatter_dimension=0, tiled=True)]
    all_to_all x4, waiting for transfers between devices: 268 us -> 21.5 us  [across_dp(): return lax.all_to_all(values, 'dp', split_axis=0, concat_axis=0, tiled=True)]
    ppermute x0 -> x63, waiting for transfers between devices: none -> 236 us  [swap(): lax.ppermute(values, axis, [(place, place ^ bit) for place in range(size)])]
    psum x3 -> x0, waiting for transfers between devices: 227 us -> none  [the longest x1 112 us: local(): lax.psum(jnp.dot(inner, w_down, preferred_element_type=jnp.float32).astyp...]
    pallas_call x0 -> x22, Pallas kernels: none -> 205 us  [the longest x2 75.1 us: feed(): pl.pallas_call(functools.partial(feed_body, hidden // 3), grid=(2,), in_s...]
    dot_general x52 -> x11, matrix products: 207 us -> 40.9 us  [dot(): lax.dot_general(left, right, (((left_dim,), (right_dim,)), ((), ())), pre...]
    all_gather x3 -> x0, blocking collectives: 95.8 us -> none  [the longest x1 35.1 us: local(): lax.all_gather(nexts[0].astype(jnp.bfloat16), 'dp', axis=0, tiled=True)]
    ppermute x0 -> x63, starting transfers between devices: none -> 58 us  [swap(): lax.ppermute(values, axis, [(place, place ^ bit) for place in range(size)])]
  transfers between devices with their start and end apart: 14 -> 70, of which waited for: 11 -> 23; matrix products, arithmetic and copies ran while one was open for 16% -> 29% of each run, Pallas kernels for 0% -> 21%
where the time goes in v1:
time: 830 us; the launch traced here: 823 us
  waiting for transfers between devices  257 us (31%)
  Pallas kernels  205 us (25%)
  other arithmetic  128 us (15%)
  local copies, waits for them, and re-layouts  88.5 us (11%)
  starting transfers between devices  80.7 us (10%)
  matrix products  40.9 us (5%)
  between operations  22.6 us (3%)
    ppermute x63, waiting for transfers between devices, swap(): lax.ppermute(values, axis, [(place, place ^ bit) for place in range(size)])  236 us
    pallas_call x2, Pallas kernels, feed(): pl.pallas_call(functools.partial(feed_body, hidden // 3), grid=(2,), in_s...  75.1 us
    ppermute x63, starting transfers between devices, swap(): lax.ppermute(values, axis, [(place, place ^ bit) for place in range(size)])  58 us
    pallas_call x2, Pallas kernels, attend_back(): pl.pallas_call(functools.partial(attend_back_body, last, dims), in_specs=...  44.4 us
    dot_general x11, matrix products, dot(): lax.dot_general(left, right, (((left_dim,), (right_dim,)), ((), ())), pre...  40.9 us
    pallas_call x11, Pallas kernels, pick(): pl.pallas_call(pick_body, in_specs=[SMEM, HELD], out_specs=VMEM, out_shap...  35.2 us
    unnamed x211, local copies, waits for them, and re-layouts  35 us
    pallas_call x2, Pallas kernels, attend(): pl.pallas_call(functools.partial(attend_body, last, dims), in_specs=[SMEM...  29.6 us
  transfers between devices with their start and end apart: 70, of which 23 were waited for; matrix products, arithmetic and copies ran while one was open for 29% of the time, Pallas kernels for 21%

profile of v1, /device:TPU:0, one launch (start us, length us, event | category | flops | bytes accessed | tf_op | source)
XLA Modules:
  0.0 822.7 jit_solution(9161194998619623525)
XLA Ops:
  11.7 7.4 all-to-all-start
  28.5 10.6 %fusion.48 = (bf16[1024,1,1152]{2,1,0:T(2,128)(2,1)}, bf16[1024,1,1152]{2,1,0:T(2,128)(2,1)}) fusion(bf16[1024,2,1152]{2,1,0:T(2,128)(2,1)} %param.32), kind=kLoop, calls=%fused_computation.209 | loop fusion | bytes 9437184 | tf_op jit(solution)/shard_map/slice | solution.py:637
  48.1 6.8 copy_bitcast_fusion
  61.2 13.0 %collective-permute-done.3.second = bf16[4,72,1024]{2,1,0:T(8,128)(2,1)S(1)} collective-permute-done((bf16[4,72,1024]{2,1,0:T(8,128)(2,1)}, bf16[4,72,1024]{2,1,0:T(8,128)(2,1)S(1)}, u32[]{:S(2)}, u32[]{:S(2)}) %collective-permute-start.3) | collective-permute-done | bytes 589856 | tf_op jit(solution)/shard_map/ppermute | solution.py:33
  84.6 5.7 all-to-all-start.1
  92.8 13.9 %shard_map.412 = (bf16[1152,256]{1,0:T(8,128)(2,1)}, bf16[1152,384]{1,0:T(8,128)(2,1)}, f32[2,1152,128]{2,1,0:T(8,128)}, bf16[2,1152,128]{2,1,0:T(8,128)(2,1)}, ...) custom-call(s32[1]{0:T(128)} %bitcast.refs_0_.member, ...), custom_call_target="tpu_custom_call" | custom-call | flops 12000000000 | bytes 12000000 | tf_op jit(solution)/shard_map/pallas_call | solution.py:692
  106.7 12.9 %all-to-all-done.1.source.first.second = bf16[8,72,1024]{2,1,0:T(8,128)(2,1)S(1)} async-done(((bf16[8,72,1024]{2,1,0:T(8,128)(2,1)}), bf16[8,72,1024]{2,1,0:T(8,128)(2,1)S(1)}, u32[]{:S(2)}, u32[]{:S(2)}) %all-to-all-start.1) | async-done | bytes 1179680 | tf_op jit(solution)/shard_map/all_to_all | solution.py:420
  119.5 15.7 %shard_map.413 = (bf16[1152,256]{1,0:T(8,128)(2,1)}, bf16[1152,384]{1,0:T(8,128)(2,1)}, f32[2,1152,128]{2,1,0:T(8,128)}, bf16[2,1152,128]{2,1,0:T(8,128)(2,1)}, ...) custom-call(s32[1]{0:T(128)} %bitcast.refs_0_.member, ...), custom_call_target="tpu_custom_call" | custom-call | flops 12000000000 | bytes 12000000 | tf_op jit(solution)/shard_map/pallas_call | solution.py:692
  138.8 15.4 %collective-permute-done.7.second = bf16[4,72,1024]{2,1,0:T(8,128)(2,1)S(1)} collective-permute-done((bf16[4,72,1024]{2,1,0:T(8,128)(2,1)}, bf16[4,72,1024]{2,1,0:T(8,128)(2,1)S(1)}, u32[]{:S(2)}, u32[]{:S(2)}) %collective-permute-start.7) | collective-permute-done | bytes 589856 | tf_op jit(solution)/shard_map/ppermute | solution.py:33
  170.0 35.2 %collective-permute-done.13.first = bf16[4,72,1024]{2,1,0:T(8,128)(2,1)} collective-permute-done((bf16[4,72,1024]{2,1,0:T(8,128)(2,1)}, bf16[4,72,1024]{2,1,0:T(8,128)(2,1)}, u32[]{:S(2)}, u32[]{:S(2)}) %collective-permute-start.13) | collective-permute-done | bytes 589856 | tf_op jit(solution)/shard_map/ppermute | solution.py:33
  209.5 31.2 %shard_map.416 = (bf16[2304,1152]{1,0:T(8,128)(2,1)}, bf16[2304,1152]{1,0:T(8,128)(2,1)}, bf16[2304,1152]{1,0:T(8,128)(2,1)}, bf16[2304,1024]{1,0:T(8,128)(2,1)}...) custom-call(bf16[576,1024]{1,0:T(8,128)(2,1)} %multiply_convert_fusion.n_own, ...), custom_call_target="tpu_custom_call" | custom-call | flops 16307453952 | bytes 28311552 | tf_op jit(solution)/shard_map/pallas_call | solution.py:364
  240.8 43.9 %shard_map.419 = (bf16[2304,1152]{1,0:T(8,128)(2,1)}, bf16[2304,1152]{1,0:T(8,128)(2,1)}, bf16[2304,1152]{1,0:T(8,128)(2,1)}, bf16[2304,1024]{1,0:T(8,128)(2,1)}...) custom-call(bf16[576,1024]{1,0:T(8,128)(2,1)} %collective-permute-do, ...), custom_call_target="tpu_custom_call", output_to_operand_aliasing={{0}: (7, {}), {1}: (8, {}), {2}: (9, {}), {3}: (10, {}), {4... | custom-call | flops 16307453952 | bytes 28311552 | tf_op jit(solution)/shard_map/pallas_call | solution.py:364
  297.1 10.6 %convolution_convert_fusion.1 = bf16[1024,1152]{1,0:T(8,128)(2,1)S(1)} fusion(bf16[2304,1024]{1,0:T(8,128)(2,1)} %get-tuple-element.148, bf16[2304,1152]{1,0:T(8,128)(2,1)} %get-tuple-element.149), kind=kOutput, calls=%fused_computation.7 | convolution fusion | flops 5436997632 | bytes 12386304 | tf_op jit(solution)/shard_map/dot_general | solution.py:26
  307.8 6.8 convolution_convert_fusion
  314.8 9.2 %convolution_convert_fusion.2 = bf16[1024,1152]{1,0:T(8,128)(2,1)S(1)} fusion(bf16[2304,1024]{1,0:T(8,128)(2,1)} %get-tuple-element.146, bf16[2304,1152]{1,0:T(8,128)(2,1)S(1)} %bitcast.248), kind=kOutput, calls=%fused_computation.8 | convolution fusion | flops 5436997632 | bytes 12386304 | tf_op jit(solution)/shard_map/dot_general | solution.py:26
  346.7 20.1 %shard_map.420 = (bf16[1152,512]{1,0:T(8,128)(2,1)}, f32[16,128]{1,0:T(8,128)}) custom-call(s32[1]{0:T(128)} %bitcast.refs_0_.member, bf16[576,1024]{1,0:T(8,128)(2,1)} %copy-done.41, bf16[576,1024]{1,0:T(8,128)(2,1)} %copy-done.85, bf16[256,1024]{1,0:T(8,128)(2,1)} %collective-permute-done.2.refs_10_.refs_3_, bf16[1152,256]{1,0:T(8,128)(2,1)} %get-tuple-element.153.refs_4_, ...), custom_call_target="tpu_custom_call" | custom-call | flops 20000000000 | bytes 14000000 | tf_op jit(solution)/shard_map/pallas_call | solution.py:729
  366.8 13.2 %collective-permute-done.19 = bf16[4,128,1152]{2,1,0:T(8,128)(2,1)} collective-permute-done((bf16[4,128,1152]{2,1,0:T(8,128)(2,1)}, bf16[4,128,1152]{2,1,0:T(8,128)(2,1)}, u32[]{:S(2)}, u32[]{:S(2)}) %collective-permute-start.19) | collective-permute-done | bytes 1179680 | tf_op jit(solution)/shard_map/ppermute | solution.py:33
  380.0 25.3 %collective-permute-done.20 = bf16[4,128,1152]{2,1,0:T(8,128)(2,1)} collective-permute-done((bf16[4,128,1152]{2,1,0:T(8,128)(2,1)}, bf16[4,128,1152]{2,1,0:T(8,128)(2,1)}, u32[]{:S(2)}, u32[]{:S(2)}) %collective-permute-start.20) | collective-permute-done | bytes 1179680 | tf_op jit(solution)/shard_map/ppermute | solution.py:33
  425.5 24.3 %shard_map.421 = (bf16[1152,512]{1,0:T(8,128)(2,1)}, f32[16,128]{1,0:T(8,128)}, bf16[576,1024]{1,0:T(8,128)(2,1)}, bf16[576,1024]{1,0:T(8,128)(2,1)}) custom-call(s32[1]{0:T(128)} %bitcast.refs_0_.member, bf16[576,1024]{1,0:T(8,128)(2,1)} %copy-done.41, bf16[576,1024]{1,0:T(8,128)(2,1)} %copy-done.85, bf16[256,1024]{1,0:T(8,128)(2,1)} %refs_3_.1, ...), custom_call_target="tpu_custom_call" | custom-call | flops 20000000000 | bytes 14000000 | tf_op jit(solution)/shard_map/pallas_call | solution.py:729
  490.2 29.5 %collective-permute-done.42 = bf16[1,128,1152]{2,1,0:T(8,128)(2,1)S(1)} collective-permute-done((bf16[1,128,1152]{2,1,0:T(8,128)(2,1)S(1)}, bf16[1,128,1152]{2,1,0:T(8,128)(2,1)S(1)}, u32[]{:S(2)}, u32[]{:S(2)}) %collective-permute-start.42) | collective-permute-done | bytes 294944 | tf_op jit(solution)/shard_map/ppermute | solution.py:33
  529.6 10.7 %collective-permute-done.41 = bf16[1,128,256]{2,1,0:T(8,128)(2,1)S(1)} collective-permute-done((bf16[1,128,256]{2,1,0:T(8,128)(2,1)S(1)}, bf16[1,128,256]{2,1,0:T(8,128)(2,1)S(1)}, u32[]{:S(2)}, u32[]{:S(2)}) %collective-permute-start.41) | collective-permute-done | bytes 65568 | tf_op jit(solution)/shard_map/ppermute | solution.py:33
  556.4 6.4 collective-permute-done.44
  586.2 16.4 %collective-permute-done.38 = bf16[1,128,512]{2,1,0:T(8,128)(2,1)S(1)} collective-permute-done((bf16[1,128,512]{2,1,0:T(8,128)(2,1)S(1)}, bf16[1,128,512]{2,1,0:T(8,128)(2,1)S(1)}, u32[]{:S(2)}, u32[]{:S(2)}) %collective-permute-start.38) | collective-permute-done | bytes 131104 | tf_op jit(solution)/shard_map/ppermute | solution.py:33
  618.9 20.5 %collective-permute-done.48 = f32[18,128]{1,0:T(8,128)S(1)} collective-permute-done((f32[18,128]{1,0:T(8,128)S(1)}, f32[18,128]{1,0:T(8,128)S(1)}, u32[]{:S(2)}, u32[]{:S(2)}) %collective-permute-start.48) | collective-permute-done | bytes 9248 | tf_op jit(solution)/shard_map/ppermute | solution.py:33
  667.0 24.9 %collective-permute-done.52 = bf16[2,128,512]{2,1,0:T(8,128)(2,1)S(1)} collective-permute-done((bf16[2,128,512]{2,1,0:T(8,128)(2,1)S(1)}, bf16[2,128,512]{2,1,0:T(8,128)(2,1)S(1)}, u32[]{:S(2)}, u32[]{:S(2)}) %collective-permute-start.52) | collective-permute-done | bytes 262176 | tf_op jit(solution)/shard_map/ppermute | solution.py:33
  697.0 5.5 pad_maximum_fusion.1
  759.7 8.6 %all-to-all-done.3.refs_0_ = bf16[8,72,1024]{2,1,0:T(8,128)(2,1)S(1)} async-done(((bf16[8,72,1024]{2,1,0:T(8,128)(2,1)}), bf16[8,72,1024]{2,1,0:T(8,128)(2,1)S(1)}, u32[]{:S(2)}, u32[]{:S(2)}) %all-to-all-start.3) | async-done | bytes 1179680 | tf_op jit(solution)/shard_map/all_to_all | solution.py:420
  769.4 5.5 shard_map.423
  774.9 7.1 pad_maximum_fusion.source
  792.7 6.7 convert_multiply_fusion
  799.4 8.8 %fusion = bf16[1024,2,1152]{2,1,0:T(2,128)(2,1)} fusion(f32[8,128,2,1152]{3,2,1,0:T(2,128)} %bitcast.201, bf16[1024,2,1152]{2,1,0:T(2,128)(2,1)} %all-gather.7.cloned.1.call-done), kind=kLoop, calls=%fused_computation.1 | loop fusion | flops 7077888 | bytes 18874368 | tf_op jit(solution)/shard_map/convert_element_type | solution.py:892
  809.3 5.5 shard_map.425
  (508 shorter events, 322.9 us)
Async XLA Ops:
  11.7 44.5 %all-to-all-start = ((bf16[8,72,1024]{2,1,0:T(8,128)(2,1)}), bf16[8,72,1024]{2,1,0:T(8,128)(2,1)S(1)}, u32[]{:S(2)}, u32[]{:S(2)}) async-start(bf16[8,72,1024]{2,1,0:T(8,128)(2,1)} %shard_map.408), calls=%async_computation | async-start | bytes 2359296 | tf_op jit(solution)/shard_map/all_to_all | solution.py:420
  19.1 37.1 %collective-permute-start = (bf16[1024,256]{1,0:T(8,128)(2,1)}, bf16[1024,256]{1,0:T(8,128)(2,1)}, u32[]{:S(2)}, u32[]{:S(2)}) collective-permute-start(bf16[1024,256]{1,0:T(8,128)(2,1)} %refs_17_), channel_id=1, source_target_pairs={{0,2},{1,3},{2,0},{3,1},{4,6},{5,7},{6,4},{7,5},{8,10},{9,11},{10,... | collective-permute-start | bytes 1572872 | tf_op jit(solution)/shard_map/ppermute | solution.py:33
  90.3 640.9 %all-gather.5.cloned.1.call-start = ((), (), s32[]{:S(2)}) async-start(), calls=%async_computation.4 | async-start | bytes 1769472 | tf_op jit(solution)/shard_map/all_gather | solution.py:659
  135.4 611.2 %all-gather.9.cloned.1.call-start = ((), (), s32[]{:S(2)}) async-start(), calls=%async_computation.6 | async-start | bytes 2654208 | tf_op jit(solution)/shard_map/all_gather | solution.py:661
  164.7 44.4 %collective-permute-start.11 = (bf16[576,1024]{1,0:T(8,128)(2,1)}, bf16[576,1024]{1,0:T(8,128)(2,1)}, u32[]{:S(2)}, u32[]{:S(2)}) collective-permute-start(bf16[576,1024]{1,0:T(8,128)(2,1)} %multiply_convert_fusion.n_own), channel_id=1, source_target_pairs={{0,2},{1,3},{2,0},{3,1},{4,6},{5,7},{6,4},{7,5},{8,10},{9,11},{10,... | collective-permute-start | bytes 3538952 | tf_op jit(solution)/shard_map/ppermute | solution.py:33
  165.1 44.4 %collective-permute-start.8 = (bf16[576,1024]{1,0:T(8,128)(2,1)}, bf16[576,1024]{1,0:T(8,128)(2,1)}, u32[]{:S(2)}, u32[]{:S(2)}) collective-permute-start(bf16[576,1024]{1,0:T(8,128)(2,1)} %bitcast.18.c_own), channel_id=1, source_target_pairs={{0,1},{1,0},{2,3},{3,2},{4,5},{5,4},{6,7},{7,6},{8,9},{9,8},{10,11... | collective-permute-start | bytes 3538952 | tf_op jit(solution)/shard_map/ppermute | solution.py:33
  165.1 44.4 %collective-permute-start.6 = (bf16[576,1024]{1,0:T(8,128)(2,1)}, bf16[576,1024]{1,0:T(8,128)(2,1)}, u32[]{:S(2)}, u32[]{:S(2)}) collective-permute-start(bf16[576,1024]{1,0:T(8,128)(2,1)} %multiply_convert_fusion.n_own), channel_id=1, source_target_pairs={{0,1},{1,0},{2,3},{3,2},{4,5},{5,4},{6,7},{7,6},{8,9},{9,8},{10,11... | collective-permute-start | bytes 3538952 | tf_op jit(solution)/shard_map/ppermute | solution.py:33
  168.3 36.9 %collective-permute-start.13 = (bf16[4,72,1024]{2,1,0:T(8,128)(2,1)}, bf16[4,72,1024]{2,1,0:T(8,128)(2,1)}, u32[]{:S(2)}, u32[]{:S(2)}) collective-permute-start(bf16[4,72,1024]{2,1,0:T(8,128)(2,1)} %shard_map.417), channel_id=1, source_target_pairs={{0,2},{1,3},{2,0},{3,1},{4,6},{5,7},{6,4},{7,5},{8,10},{9,11},{10,... | collective-permute-start | bytes 1769480 | tf_op jit(solution)/shard_map/ppermute | solution.py:33
  169.9 629.5 %all-gather.7.cloned.1.call-start = ((), (), s32[]{:S(2)}) async-start(), calls=%async_computation.5 | async-start | bytes 5308416 | tf_op jit(solution)/shard_map/all_gather | solution.py:660
  334.2 83.7 %collective-permute-start.9 = (bf16[576,1024]{1,0:T(8,128)(2,1)}, bf16[576,1024]{1,0:T(8,128)(2,1)}, u32[]{:S(2)}, u32[]{:S(2)}) collective-permute-start(bf16[576,1024]{1,0:T(8,128)(2,1)} %slice.113), channel_id=1, source_target_pairs={{0,1},{1,0},{2,3},{3,2},{4,5},{5,4},{6,7},{7,6},{8,9},{9,8},{10,11... | collective-permute-start | bytes 3538952 | tf_op jit(solution)/shard_map/ppermute | solution.py:33
  335.7 44.3 %collective-permute-start.19 = (bf16[4,128,1152]{2,1,0:T(8,128)(2,1)}, bf16[4,128,1152]{2,1,0:T(8,128)(2,1)}, u32[]{:S(2)}, u32[]{:S(2)}) collective-permute-start(bf16[4,128,1152]{2,1,0:T(8,128)(2,1)} %dynamic-slice_bitcast_fusion.2), channel_id=1, source_target_pairs={{0,4},{4,0},{8,12},{12,8},{16,20},{20,16},{24,28},{28,24},{1,5},{5... | collective-permute-start | bytes 3538952 | tf_op jit(solution)/shard_map/ppermute | solution.py:33
  338.1 67.2 %collective-permute-start.20 = (bf16[4,128,1152]{2,1,0:T(8,128)(2,1)}, bf16[4,128,1152]{2,1,0:T(8,128)(2,1)}, u32[]{:S(2)}, u32[]{:S(2)}) collective-permute-start(bf16[4,128,1152]{2,1,0:T(8,128)(2,1)} %dynamic-slice_bitcast_fusion.1), channel_id=1, source_target_pairs={{0,4},{4,0},{8,12},{12,8},{16,20},{20,16},{24,28},{28,24},{1,5},{5... | collective-permute-start | bytes 3538952 | tf_op jit(solution)/shard_map/ppermute | solution.py:33
  338.9 66.4 %collective-permute-start.21 = (bf16[576,1024]{1,0:T(8,128)(2,1)}, bf16[576,1024]{1,0:T(8,128)(2,1)}, u32[]{:S(2)}, u32[]{:S(2)}) collective-permute-start(bf16[576,1024]{1,0:T(8,128)(2,1)} %add_convert_fusion.2), channel_id=1, source_target_pairs={{0,2},{1,3},{2,0},{3,1},{4,6},{5,7},{6,4},{7,5},{8,10},{9,11},{10,... | collective-permute-start | bytes 3538952 | tf_op jit(solution)/shard_map/ppermute | solution.py:33
  345.2 114.5 %collective-permute-start.24 = (bf16[4,128,1152]{2,1,0:T(8,128)(2,1)}, bf16[4,128,1152]{2,1,0:T(8,128)(2,1)}, u32[]{:S(2)}, u32[]{:S(2)}) collective-permute-start(bf16[4,128,1152]{2,1,0:T(8,128)(2,1)} %dynamic-slice_bitcast_fusion), channel_id=1, source_target_pairs={{0,4},{4,0},{8,12},{12,8},{16,20},{20,16},{24,28},{28,24},{1,5},{5... | collective-permute-start | bytes 3538952 | tf_op jit(solution)/shard_map/ppermute | solution.py:33
  411.6 49.5 %collective-permute-start.22 = (bf16[2,128,1152]{1,2,0:T(8,128)(2,1)}, bf16[2,128,1152]{1,2,0:T(8,128)(2,1)}, u32[]{:S(2)}, u32[]{:S(2)}) collective-permute-start(bf16[2,128,1152]{1,2,0:T(8,128)(2,1)} %bitcast.236), channel_id=1, source_target_pairs={{0,8},{4,12},{8,0},{12,4},{16,24},{20,28},{24,16},{28,20},{1,9},{5... | collective-permute-start | bytes 1769480 | tf_op jit(solution)/shard_map/ppermute | solution.py:33
  417.2 43.9 %collective-permute-start.23 = (bf16[2,128,1152]{2,1,0:T(8,128)(2,1)}, bf16[2,128,1152]{2,1,0:T(8,128)(2,1)}, u32[]{:S(2)}, u32[]{:S(2)}) collective-permute-start(bf16[2,128,1152]{2,1,0:T(8,128)(2,1)} %fusion.7), channel_id=1, source_target_pairs={{0,8},{4,12},{8,0},{12,4},{16,24},{20,28},{24,16},{28,20},{1,9},{5... | collective-permute-start | bytes 1769480 | tf_op jit(solution)/shard_map/ppermute | solution.py:33
  421.4 39.7 %collective-permute-start.25 = (bf16[288,1024]{1,0:T(8,128)(2,1)}, bf16[288,1024]{1,0:T(8,128)(2,1)}, u32[]{:S(2)}, u32[]{:S(2)}) collective-permute-start(bf16[288,1024]{1,0:T(8,128)(2,1)} %get-tuple-element.345), channel_id=1, source_target_pairs={{0,2},{1,3},{2,0},{3,1},{4,6},{5,7},{6,4},{7,5},{8,10},{9,11},{10,... | collective-permute-start | bytes 1769480 | tf_op jit(solution)/shard_map/ppermute | solution.py:33
  459.7 67.6 %collective-permute-start.35 = (bf16[1024,512]{1,0:T(8,128)(2,1)}, bf16[1024,512]{1,0:T(8,128)(2,1)}, u32[]{:S(2)}, u32[]{:S(2)}) collective-permute-start(bf16[1024,512]{1,0:T(8,128)(2,1)} %add_convert_fusion.4), channel_id=1, source_target_pairs={{0,2},{1,3},{2,0},{3,1},{4,6},{5,7},{6,4},{7,5},{8,10},{9,11},{10,... | collective-permute-start | bytes 3145736 | tf_op jit(solution)/shard_map/ppermute | solution.py:33
  466.5 228.7 %all-to-all-start.2 = ((bf16[8,72,1024]{2,1,0:T(8,128)(2,1)}), bf16[8,72,1024]{2,1,0:T(8,128)(2,1)}, u32[]{:S(2)}, u32[]{:S(2)}) async-start(bf16[8,72,1024]{2,1,0:T(8,128)(2,1)} %shard_map.422), calls=%async_computation.2 | async-start | bytes 2359296 | tf_op jit(solution)/shard_map/all_to_all | solution.py:420
  471.2 111.4 %collective-permute-start.30 = (bf16[576,1024]{1,0:T(8,128)(2,1)}, bf16[576,1024]{1,0:T(8,128)(2,1)}, u32[]{:S(2)}, u32[]{:S(2)}) collective-permute-start(bf16[576,1024]{1,0:T(8,128)(2,1)} %get-tuple-element.181), channel_id=1, source_target_pairs={{0,1},{1,0},{2,3},{3,2},{4,5},{5,4},{6,7},{7,6},{8,9},{9,8},{10,11... | collective-permute-start | bytes 3538952 | tf_op jit(solution)/shard_map/ppermute | solution.py:33
  476.4 43.4 %collective-permute-start.42 = (bf16[1,128,1152]{2,1,0:T(8,128)(2,1)S(1)}, bf16[1,128,1152]{2,1,0:T(8,128)(2,1)S(1)}, u32[]{:S(2)}, u32[]{:S(2)}) collective-permute-start(bf16[1,128,1152]{2,1,0:T(8,128)(2,1)S(1)} %dynamic-slice_convert_fusion.3), channel_id=1, source_target_pairs={{0,16},{4,20},{8,24},{12,28},{16,0},{20,4},{24,8},{28,12},{1,17},{... | collective-permute-start | bytes 884744 | tf_op jit(solution)/shard_map/ppermute | solution.py:33
  480.4 66.0 %collective-permute-start.43 = (bf16[2,128,1152]{2,1,0:T(8,128)(2,1)S(1)}, bf16[2,128,1152]{2,1,0:T(8,128)(2,1)S(1)}, u32[]{:S(2)}, u32[]{:S(2)}) collective-permute-start(bf16[2,128,1152]{2,1,0:T(8,128)(2,1)S(1)} %fusion.8), channel_id=1, source_target_pairs={{0,8},{4,12},{8,0},{12,4},{16,24},{20,28},{24,16},{28,20},{1,9},{5... | collective-permute-start | bytes 1769480 | tf_op jit(solution)/shard_map/ppermute | solution.py:33
  550.3 57.9 %collective-permute-start.61 = (bf16[2,1152,128]{2,1,0:T(8,128)(2,1)}, bf16[2,1152,128]{2,1,0:T(8,128)(2,1)}, u32[]{:S(2)}, u32[]{:S(2)}) collective-permute-start(bf16[2,1152,128]{2,1,0:T(8,128)(2,1)} %pad_maximum_fusion.9), channel_id=1, source_target_pairs={{0,8},{4,12},{8,0},{12,4},{16,24},{20,28},{24,16},{28,20},{1,9},{5... | collective-permute-start | bytes 1769480 | tf_op jit(solution)/shard_map/ppermute | solution.py:33
  568.8 87.2 %collective-permute-start.57 = (bf16[1,128,2,1152]{3,2,1,0:T(2,128)(2,1)}, bf16[1,128,2,1152]{3,2,1,0:T(2,128)(2,1)}, u32[]{:S(2)}, u32[]{:S(2)}) collective-permute-start(bf16[1,128,2,1152]{3,2,1,0:T(2,128)(2,1)} %pad_maximum_fusion.8), channel_id=1, source_target_pairs={{0,16},{4,20},{8,24},{12,28},{16,0},{20,4},{24,8},{28,12},{1,17},{... | collective-permute-start | bytes 1769480 | tf_op jit(solution)/shard_map/ppermute | solution.py:33
  610.5 129.1 %collective-permute-start.62 = (bf16[4,1152,128]{2,1,0:T(8,128)(2,1)}, bf16[4,1152,128]{2,1,0:T(8,128)(2,1)}, u32[]{:S(2)}, u32[]{:S(2)}) collective-permute-start(bf16[4,1152,128]{2,1,0:T(8,128)(2,1)} %pad_maximum_fusion.6), channel_id=1, source_target_pairs={{0,4},{4,0},{8,12},{12,8},{16,20},{20,16},{24,28},{28,24},{1,5},{5... | collective-permute-start | bytes 3538952 | tf_op jit(solution)/shard_map/ppermute | solution.py:33
  640.5 72.4 %collective-permute-start.31 = (bf16[288,1024]{1,0:T(8,128)(2,1)}, bf16[288,1024]{1,0:T(8,128)(2,1)}, u32[]{:S(2)}, u32[]{:S(2)}) collective-permute-start(bf16[288,1024]{1,0:T(8,128)(2,1)} %get-tuple-element.343), channel_id=1, source_target_pairs={{0,2},{1,3},{2,0},{3,1},{4,6},{5,7},{6,4},{7,5},{8,10},{9,11},{10,... | collective-permute-start | bytes 1769480 | tf_op jit(solution)/shard_map/ppermute | solution.py:33
  659.9 37.1 %collective-permute-start.58 = (bf16[2,128,2,1152]{3,2,1,0:T(2,128)(2,1)}, bf16[2,128,2,1152]{3,2,1,0:T(2,128)(2,1)S(1)}, u32[]{:S(2)}, u32[]{:S(2)}) collective-permute-start(bf16[2,128,2,1152]{3,2,1,0:T(2,128)(2,1)} %pad_maximum_fusion.5), channel_id=1, source_target_pairs={{0,8},{4,12},{8,0},{12,4},{16,24},{20,28},{24,16},{28,20},{1,9},{5... | collective-permute-start | bytes 3538952 | tf_op jit(solution)/shard_map/ppermute | solution.py:33
  695.3 38.5 %collective-permute-start.27 = (bf16[8,72,1024]{2,1,0:T(8,128)(2,1)}, bf16[8,72,1024]{2,1,0:T(8,128)(2,1)}, u32[]{:S(2)}, u32[]{:S(2)}) collective-permute-start(bf16[8,72,1024]{2,1,0:T(8,128)(2,1)} %all-to-all-done.2.refs_0_), channel_id=1, source_target_pairs={{0,2},{1,3},{2,0},{3,1},{4,6},{5,7},{6,4},{7,5},{8,10},{9,11},{10,... | collective-permute-start | bytes 3538952 | tf_op jit(solution)/shard_map/ppermute | solution.py:33
  702.5 72.4 %collective-permute-start.59 = (bf16[4,128,2,1152]{3,2,1,0:T(2,128)(2,1)}, bf16[4,128,2,1152]{3,2,1,0:T(2,128)(2,1)}, u32[]{:S(2)}, u32[]{:S(2)}) collective-permute-start(bf16[4,128,2,1152]{3,2,1,0:T(2,128)(2,1)} %pad_maximum_fusion.1), channel_id=1, source_target_pairs={{0,4},{4,0},{8,12},{12,8},{16,20},{20,16},{24,28},{28,24},{1,5},{5... | collective-permute-start | bytes 7077896 | tf_op jit(solution)/shard_map/ppermute | solution.py:33
  718.5 49.8 %all-to-all-start.3 = ((bf16[8,72,1024]{2,1,0:T(8,128)(2,1)}), bf16[8,72,1024]{2,1,0:T(8,128)(2,1)S(1)}, u32[]{:S(2)}, u32[]{:S(2)}) async-start(bf16[8,72,1024]{2,1,0:T(8,128)(2,1)} %shard_map.424), calls=%async_computation.3 | async-start | bytes 2359296 | tf_op jit(solution)/shard_map/all_to_all | solution.py:420
  723.7 45.7 %collective-permute-start.28 = (bf16[8,72,1024]{2,1,0:T(8,128)(2,1)}, bf16[8,72,1024]{2,1,0:T(8,128)(2,1)}, u32[]{:S(2)}, u32[]{:S(2)}) collective-permute-start(bf16[8,72,1024]{2,1,0:T(8,128)(2,1)} %all-to-all-done.2.refs_0_), channel_id=1, source_target_pairs={{0,1},{1,0},{2,3},{3,2},{4,5},{5,4},{6,7},{7,6},{8,9},{9,8},{10,11... | collective-permute-start | bytes 3538952 | tf_op jit(solution)/shard_map/ppermute | solution.py:33
  769.3 38.9 %collective-permute-start.33 = (bf16[8,72,1024]{2,1,0:T(8,128)(2,1)S(1)}, bf16[8,72,1024]{2,1,0:T(8,128)(2,1)}, u32[]{:S(2)}, u32[]{:S(2)}) collective-permute-start(bf16[8,72,1024]{2,1,0:T(8,128)(2,1)S(1)} %all-to-all-done.3.refs_0_), channel_id=1, source_target_pairs={{0,1},{1,0},{2,3},{3,2},{4,5},{5,4},{6,7},{7,6},{8,9},{9,8},{10,11... | collective-permute-start | bytes 3538952 | tf_op jit(solution)/shard_map/ppermute | solution.py:33
  (137 other events, 1897.7 us)
Sparse Core Ops, SparseCore 0:
  135.5 43.5 all-gather.4
  181.3 50.2 all-gather.8
  293.0 95.3 all-gather.6

commit v2 on v1

--- a/solution.py
+++ b/solution.py
@@ -302,68 +302,59 @@
     gains[8:, :] = gain_sums[1]
 
 
-def feed_body(chunk, n_own, n_near, c_own, c_near, w_gate, w_up, w_down, *refs):
-    refs = refs[-7:]
-    (inner, d_gate, d_up, n_all, c_all, d_norm, partial) = refs
-    step = pl.program_id(0)
-
-    def run(n_ref, c_ref):
-        n_rows = n_ref[...]
-        c_rows = c_ref[...]
-        n_all[...] = n_rows
-        c_all[...] = c_rows
-        hidden = w_gate.shape[1]
-        total_n = None
-        total_y = None
-        for begin in range(0, hidden, chunk):
-            cols = slice(begin, begin + chunk)
-            gate = dot(n_rows, w_gate[:, cols])
-            up_part = dot(n_rows, w_up[:, cols])
-            d_inner = dot(c_rows, w_down[cols, :], 1, 1)
-            sigma = 1.0 / (1.0 + jnp.exp(-gate))
-            held = gate * sigma
-            inner_low = (held * up_part).astype(LOW)
-            d_gate_low = (d_inner * up_part * sigma * (1.0 + gate * (1.0 - sigma))).astype(LOW)
-            d_up_low = (d_inner * held).astype(LOW)
-            inner[:, cols] = inner_low
-            d_gate[:, cols] = d_gate_low
-            d_up[:, cols] = d_up_low
-            more_n = dot(d_gate_low, w_gate[:, cols], 1, 1) + dot(d_up_low, w_up[:, cols], 1, 1)
-            more_y = dot(inner_low, w_down[cols, :])
-            total_n = more_n if total_n is None else total_n + more_n
-            total_y = more_y if total_y is None else total_y + more_y
-        d_norm[...] = total_n.astype(LOW)
-        partial[...] = total_y.astype(LOW)
-
-    @pl.when(step == 0)
+def feed_body(n_own, n_near, c_own, c_near, w_gate, w_up, w_down, *refs):
+    (inner, d_gate, d_up, n_all, c_all, d_own, d_near, y_own, y_near) = refs[-9:]
+    mine = pl.program_id(0) < pl.num_programs(0) // 2
+    n_rows = jnp.where(mine, n_own[...], n_near[...])
+    c_rows = jnp.where(mine, c_own[...], c_near[...])
+    n_all[...] = n_rows
+    c_all[...] = c_rows
+    gate = dot(n_rows, w_gate[...])
+    up_part = dot(n_rows, w_up[...])
+    d_inner = dot(c_rows, w_down[...], 1, 1)
+    sigma = 1.0 / (1.0 + jnp.exp(-gate))
+    held = gate * sigma
+    inner[...] = (held * up_part).astype(LOW)
+    d_gate[...] = (d_inner * up_part * sigma * (1.0 + gate * (1.0 - sigma))).astype(LOW)
+    d_up[...] = (d_inner * held).astype(LOW)
+    total = dot(d_gate[...], w_gate[...], 1, 1) + dot(d_up[...], w_up[...], 1, 1)
+    product = dot(inner[...], w_down[...])
+
+    @pl.when(mine)
     def _():
-        run(n_own, c_own)
-
-    @pl.when(step == 1)
+        d_own[...] = total.astype(LOW)
+        y_own[...] = product.astype(LOW)
+
+    @pl.when(jnp.logical_not(mine))
     def _():
-        run(n_near, c_near)
+        d_near[...] = total.astype(LOW)
+        y_near[...] = product.astype(LOW)
 
 
 def feed(half, kept, n_own, n_near, c_own, c_near, w_gate, w_up, w_down):
     rows, width = n_own.shape
     hidden = w_gate.shape[1]
-    whole = lambda shape: pl.BlockSpec(shape, lambda i: (0, 0))
-    part = lambda cols: pl.BlockSpec((rows, cols), lambda i: (i + 2 * half, 0))
-    in_specs = [whole(v.shape) for v in (n_own, n_near, c_own, c_near, w_gate, w_up, w_down)]
-    all_rows = [
+    block = rows // 2
+    steps = 4
+    first = pl.BlockSpec((block, width), lambda i: (jnp.minimum(i, 1), 0))
+    second = pl.BlockSpec((block, width), lambda i: (jnp.maximum(i - 2, 0), 0))
+    whole = lambda values: pl.BlockSpec(values.shape, lambda i: (0, 0))
+    part = lambda cols: pl.BlockSpec((block, cols), lambda i: (i + steps * half, 0))
+    in_specs = [first, second, first, second] + [whole(v) for v in (w_gate, w_up, w_down)]
+    outs = [
         jax.ShapeDtypeStruct((4 * rows, cols), LOW) for cols in (hidden, hidden, hidden, width, width)
     ]
-    outs = all_rows + [jax.ShapeDtypeStruct((2 * rows, width), LOW)] * 2
+    outs += [jax.ShapeDtypeStruct((rows, width), LOW)] * 4
     out_specs = [part(hidden)] * 3 + [part(width)] * 2
-    out_specs += [pl.BlockSpec((rows, width), lambda i: (i, 0))] * 2
+    out_specs += [first, second, first, second]
     aliases = {}
     if half:
         in_specs += [pl.BlockSpec(memory_space=pl.ANY)] * 5
         aliases = {7 + index: index for index in range(5)}
     work = 2 * rows * width * hidden * 2 * 6
     return pl.pallas_call(
-        functools.partial(feed_body, hidden // 3),
-        grid=(2,),
+        feed_body,
+        grid=(steps,),
         in_specs=in_specs,
         out_specs=out_specs,
         out_shape=outs,
@@ -478,6 +469,63 @@
     return pieces.reshape(count * 4 * part_rows, width)
 
 
+def kernel_params():
+    return pltpu.CompilerParams(vmem_limit_bytes=VMEM_BYTES)
+
+
+def finish_down_body(pull, ahead, gradient, weight):
+    value = ahead[0].astype(FULL) - pull[0] * gradient[0].astype(FULL)
+    weight[...] = value.astype(LOW)
+
+
+def finish_down(pull, ahead, gradient):
+    count, rows, cols = ahead.shape
+    if cols % LANES:
+        value = ahead.astype(FULL) - pull * gradient.astype(FULL)
+        return value.astype(LOW).transpose(1, 0, 2).reshape(rows, count * cols)
+    shard = pl.BlockSpec((1, rows, cols), lambda i: (i, 0, 0))
+    return pl.pallas_call(
+        finish_down_body,
+        grid=(count,),
+        in_specs=[SMEM, shard, shard],
+        out_specs=pl.BlockSpec((rows, cols), lambda i: (0, i)),
+        out_shape=jax.ShapeDtypeStruct((rows, count * cols), LOW),
+        compiler_params=kernel_params(),
+    )(pull, ahead, gradient)
+
+
+def finish_small_body(pull, ahead, gradient, query, keyval, output):
+    value = ahead[0].astype(FULL) - pull[0] * gradient[0].astype(FULL)
+    first = query.shape[1]
+    second = first + keyval.shape[1]
+    query[...] = value[:, :first].astype(LOW)
+    keyval[...] = value[:, first:second].astype(LOW)
+    output[...] = value[:, second:].T.astype(LOW)
+
+
+def finish_small(pull, ahead, gradient, first, second):
+    count, rows, cols = ahead.shape
+    if rows % LANES:
+        value = (ahead.astype(FULL) - pull * gradient.astype(FULL)).astype(LOW)
+        value = value.reshape(count * rows, cols)
+        return value[:, :first], value[:, first:second], value[:, second:].T
+    shard = pl.BlockSpec((1, rows, cols), lambda i: (i, 0, 0))
+    shapes = [(count * rows, first), (count * rows, second - first), (cols - second, count * rows)]
+    specs = [
+        pl.BlockSpec((rows, first), lambda i: (i, 0)),
+        pl.BlockSpec((rows, second - first), lambda i: (i, 0)),
+        pl.BlockSpec((cols - second, rows), lambda i: (0, i)),
+    ]
+    return pl.pallas_call(
+        finish_small_body,
+        grid=(count,),
+        in_specs=[SMEM, shard, shard],
+        out_specs=specs,
+        out_shape=[jax.ShapeDtypeStruct(shape, LOW) for shape in shapes],
+        compiler_params=kernel_params(),
+    )(pull, ahead, gradient)
+
+
 def fence(*values):
     return lax.optimization_barrier(values)
 
@@ -494,29 +542,8 @@
     return first.astype(FULL) + second.astype(FULL)
 
 
-def reduce_rest(kept, got, steps, device):
-    for step in steps:
-        kept, got = reduce_step(add(kept, got), step, device)
-    return add(kept, got)[0]
-
-
 def by_device(product, devices):
     return product.reshape((devices, product.shape[0] // devices) + product.shape[1:])
-
-
-def gather_dp(own, devices):
-    held = own[None]
-    for step in reversed(bits_of(devices)):
-        held = jnp.concatenate([held, swap(held, "dp", step)], axis=0)
-    return held
-
-
-def places_of(devices, device):
-    apart = jnp.arange(devices, dtype=jnp.int32) ^ device
-    place = jnp.zeros_like(apart)
-    for index, step in enumerate(bits_of(devices)):
-        place = place + ((apart // step) & 1) * (devices // 2 // step)
-    return place
 
 
 def row_norm(values, gain_row):
@@ -629,10 +656,7 @@
     gain_k = jnp.tile(head_gains[1:2], (1, LANES // head_dim))
 
     w_keyval_flat = w_keyval.reshape(width, 2 * key_cols)
-    groups = (
-        (w_query, w_keyval_flat, w_output),
-        (far(w_query), far(w_keyval_flat), far(w_output)),
-    )
+    far_query, far_keyval = far(w_query), far(w_keyval_flat)
     w_gate = w_gateup[:, 0]
     w_up = w_gateup[:, 1]
 
@@ -650,20 +674,27 @@
     part_gateup = ahead(master_gateup, start_gateup)
     part_down = ahead(master_down, start_down)
 
-    early = fence(x_got, small, part_gateup, part_down, cosine, sine, w_gate, w_up, groups)
-    x_got, small, part_gateup, part_down, cosine, sine, w_gate, w_up, groups = early
+    early = fence(
+        (x_got, far_query, far_keyval, cosine, sine, w_gate, w_up),
+        (small, part_gateup, part_down, cotangent, w_output),
+    )
+    x_got, far_query, far_keyval, cosine, sine, w_gate, w_up = early[0]
+    small, part_gateup, part_down, cotangent, w_output = early[1]
     x_other = far(pick(x_got, other_source))
-    cotangent, _ = fence(cotangent, x_got)
     c_got = deal_in(cotangent)
+    x_other, w_output = fence(x_other, w_output)
+    groups = (
+        (w_query, w_keyval_flat, w_output),
+        (far_query, far_keyval, far(w_output)),
+    )
     x_own = rows_of(join(x_got, own_source, x_other, in_order))
-    ahead_small = lax.all_gather(small, "dp", axis=0, tiled=True)
-    ahead_gateup = lax.all_gather(part_gateup, "dp", axis=0, tiled=True)
-    ahead_down = lax.all_gather(part_down, "dp", axis=0, tiled=False)
 
     x_full = x_own.astype(FULL)
     norm_one_f, inv_one = row_norm(x_full, norm_gains[0])
     norm_own = norm_one_f.astype(LOW)
     norm_near = near(norm_own)
+    stepped = fence(norm_near, c_got, small, part_gateup, part_down)
+    norm_near, c_got, small, part_gateup, part_down = stepped
 
     dims = (slot_rows, slot_pieces, part_rows, slot_rows // 6, head_dim, heads)
     shape = jax.ShapeDtypeStruct
@@ -746,48 +777,58 @@
         )(*arguments)
 
     first_kept = attend(False, groups[0], ())
-    c_got, first_kept = fence(c_got, first_kept)
     c_own_far = far(pick(c_got, other_source))
     c_other_far = far(pick(c_got, own_source))
+    ahead_down = lax.all_gather(part_down, "dp", axis=0, tiled=False)
+    ahead_gateup = lax.all_gather(part_gateup, "dp", axis=0, tiled=True)
+    ahead_small = lax.all_gather(small, "dp", axis=0, tiled=False)
     *second_kept, attn_own, attn_near = attend(
         True, groups[1], (groups[1][2], groups[0][2], first_kept[0])
     )
+    attn_got = near(attn_near)
+    attn_got, attn_own, c_own_far = fence(attn_got, attn_own, c_own_far)
     c_own = rows_of(join(c_got, own_source, c_own_far, in_order))
     c_near = near(c_own)
-    attn_sum = add(attn_own, near(attn_near))
-    hidden_one = x_full + attn_sum
+    hidden_one = x_full + add(attn_own, attn_got)
     norm_two_f, inv_two = row_norm(hidden_one, norm_gains[1])
     two_own = norm_two_f.astype(LOW)
     two_near = near(two_own)
+    two_near, two_own, c_near, c_other_far = fence(two_near, two_own, c_near, c_other_far)
     two_far = far(two_own)
+
+    *kept, d_own, d_near, y_own, y_near = feed(
+        0, (), two_own, two_near, c_own, c_near, w_gate, w_up, w_down
+    )
+    stepped = fence(two_far, d_own, d_near, c_other_far, y_near, ahead_down)
+    two_far, d_own, d_near, c_other_far, y_near, ahead_down = stepped
     two_across = near(two_far)
     c_far = rows_of(join(c_other_far, in_order, c_got, other_source))
     c_across = near(c_far)
-
-    *kept, d_two_own, ffn_own = feed(0, (), two_own, two_near, c_own, c_near, w_gate, w_up, w_down)
-    near_own = near(d_two_own[half_rows:])
-    *kept, d_two_far, ffn_far = feed(
+    d_got = near(d_near)
+    y_got = near(y_near)
+    *kept, far_own, far_near, far_y_own, far_y_near = feed(
         1, kept, two_far, two_across, c_far, c_across, w_gate, w_up, w_down
     )
-    near_far = near(d_two_far[half_rows:])
-    pair_far = add(d_two_far[:half_rows], near_far).astype(LOW)
-    pair_far, kept, ffn_far = fence(pair_far, kept, ffn_far)
+    far_got = near(far_near)
+    pair_far = add(far_own, far_got).astype(LOW)
+    pair_far, kept, far_y_near = fence(pair_far, kept, far_y_near)
     inner, d_gate, d_up, two_all, c_all = kept
     pair_got = far(pair_far)
+    far_y_got = near(far_y_near)
+    steps = bits_of(devices)
     grad_down = dot(c_all, inner, 0, 0).astype(LOW)
+    down_kept, down_got = reduce_step(by_device(grad_down, devices), steps[0], device)
     grad_gate = dot(two_all, d_gate, 0, 0).astype(LOW)
+    gate_kept, gate_got = reduce_step(by_device(grad_gate, devices), steps[0], device)
+    y_pair = add(y_own, y_got) + hidden_one
+    far_y_pair = add(far_y_own, far_y_got)
+    y_leaving = jnp.concatenate([y_pair[quarter_rows:], far_y_pair[:quarter_rows]]).astype(LOW)
     grad_up = dot(two_all, d_up, 0, 0).astype(LOW)
-    ffn_pair_far = add(ffn_far[:half_rows], near(ffn_far[half_rows:])).astype(LOW)
-    ffn_pair_own = add(ffn_own[:half_rows], near(ffn_own[half_rows:]))
-    stepped = fence(pair_got, grad_down, grad_gate, grad_up, ffn_pair_far)
-    pair_got, grad_down, grad_gate, grad_up, ffn_pair_far = stepped
-    steps = bits_of(devices)
-    down_kept, down_got = reduce_step(by_device(grad_down, devices), steps[0], device)
-    gate_kept, gate_got = reduce_step(by_device(grad_gate, devices), steps[0], device)
     up_kept, up_got = reduce_step(by_device(grad_up, devices), steps[0], device)
-    ffn_got = far(ffn_pair_far)
-
-    d_norm_two = add(d_two_own[:half_rows], near_own) + pair_got.astype(FULL)
+    pair_got, gate_kept, up_kept, y_leaving = fence(pair_got, gate_kept, up_kept, y_leaving)
+    y_arrived = far(y_leaving)
+
+    d_norm_two = add(d_own, d_got) + pair_got.astype(FULL)
     d_hidden_part, gain_two = row_norm_back(d_norm_two, hidden_one, inv_two, norm_gains[1])
     d_hidden = c_own.astype(FULL) + d_hidden_part
     dh_own = d_hidden.astype(LOW)
@@ -797,12 +838,22 @@
         return dot(own, values[:half_rows], 0, 0) + dot(other, values[half_rows:], 0, 0)
 
     d_raw_far, gains_far = attend_back(False, groups[1], second_kept, dh_own, dh_near, ())
-    stepped = fence(d_raw_far, down_got, gate_got, ffn_got)
-    d_raw_far, down_got, gate_got, ffn_got = stepped
+    d_raw_far, down_got, y_arrived = fence(d_raw_far, down_got, y_arrived)
+
+    out_order = (place_from + (slot_count - slot) * slot_pieces) % pieces_dev
+
+    def deal_out(mine, other):
+        rows = jnp.concatenate([mine, other], axis=0)
+        return across_dp(pick(rows.reshape(pieces_dev, part_rows, width), out_order))
+
+    def settle(got, got_far):
+        return place_pieces((got, got_far, near(got), near(got_far)), target, member_ref)
+
+    out_got = deal_out(
+        (y_pair[:quarter_rows] + y_arrived[quarter_rows:].astype(FULL)).astype(LOW),
+        (far_y_pair[quarter_rows:] + y_arrived[:quarter_rows].astype(FULL)).astype(LOW),
+    )
     down_kept, down_got = reduce_step(add(down_kept, down_got), steps[1], device)
-    gate_kept, gate_got = reduce_step(add(gate_kept, gate_got), steps[1], device)
-    out_own = (hidden_one + ffn_pair_own + ffn_got.astype(FULL)).astype(LOW)
-    out_other = far(out_own[quarter_rows:])
     grad_output_got = far(over_rows(dh_own, dh_near, second_kept[0]).astype(LOW))
     grad_qkv_got = far(over_rows(norm_own, norm_near, d_raw_far).astype(LOW))
     grad_output_mine = over_rows(dh_own, dh_near, first_kept[0])
@@ -814,37 +865,49 @@
         dh_near,
         (groups[0][0], groups[0][1], groups[1][0], groups[1][1], d_raw_far),
     )
-    stepped = fence(d_raw_own, d_one_near, down_got, gate_got, up_got, out_other, grad_output_got)
-    d_raw_own, d_one_near, down_got, gate_got, up_got, out_other, grad_output_got = stepped
-    d_norm_one = add(d_one_own, near(d_one_near))
+    stepped = fence(d_raw_own, d_one_near, down_got, gate_got, up_got, out_got, ahead_gateup)
+    d_raw_own, d_one_near, down_got, gate_got, up_got, out_got, ahead_gateup = stepped
+
+    d_one_got = near(d_one_near)
+    down_kept, down_got = reduce_step(add(down_kept, down_got), steps[2], device)
+    gate_kept, gate_got = reduce_step(add(gate_kept, gate_got), steps[1], device)
+    d_one_got, down_kept, gate_kept = fence(d_one_got, down_kept, gate_kept)
+    d_norm_one = add(d_one_own, d_one_got)
     d_input_part, gain_one = row_norm_back(d_norm_one, x_full, inv_one, norm_gains[0])
     dx_own = (d_hidden + d_input_part).astype(LOW)
-
-    own_down = reduce_rest(down_kept, down_got, steps[2:], device)
-    own_gate = reduce_rest(gate_kept, gate_got, steps[2:], device)
-    own_up = reduce_rest(up_kept, up_got, steps[1:], device)
-    grad_output = add(grad_output_mine, grad_output_got)
-    grad_qkv = add(over_rows(norm_own, norm_near, d_raw_own), grad_qkv_got)
-    own_output = reduce_rest(
-        *reduce_step(by_device(grad_output, devices), steps[0], device), steps[1:], device
-    )
-    own_qkv = reduce_rest(
-        *reduce_step(by_device(grad_qkv, devices), steps[0], device), steps[1:], device
-    )
-
-    def deal_out(values, other):
-        mine = values[:quarter_rows].reshape(slot_pieces, part_rows, width)
-        other = other.reshape(slot_pieces, part_rows, width)
-        held = jnp.concatenate([mine, other], axis=0)
-        order = (place_from + (slot_count - slot) * slot_pieces) % pieces_dev
-        got = across_dp(pick(held, order))
-        got_far = far(got)
-        return place_pieces((got, got_far, near(got), near(got_far)), target, member_ref)
-
-    output = deal_out(out_own, out_other)
-    input_grad = deal_out(dx_own, far(dx_own[quarter_rows:]))
-
-    owned = (own_qkv, own_output, own_gate, own_up, own_down)
+    dx_other = far(dx_own[quarter_rows:])
+    up_kept, up_got = reduce_step(add(up_kept, up_got), steps[1], device)
+    grad_qkv_mine = over_rows(norm_own, norm_near, d_raw_own)
+    grad_small = jnp.concatenate(
+        [add(grad_qkv_mine, grad_qkv_got), add(grad_output_mine, grad_output_got)], axis=1
+    )
+    small_kept, small_got = reduce_step(by_device(grad_small, devices), steps[0], device)
+
+    down_got, up_kept, gate_got = fence(down_got, up_kept, gate_got)
+    own_down = add(down_kept, down_got)[0]
+    owned_down = own_down.T
+    gate_kept, gate_got = reduce_step(add(gate_kept, gate_got), steps[2], device)
+    up_got, gate_kept, owned_down = fence(up_got, gate_kept, owned_down)
+    up_kept, up_got = reduce_step(add(up_kept, up_got), steps[2], device)
+    all_down = lax.all_gather(owned_down.astype(LOW), "dp", axis=0, tiled=False)
+    small_got, up_kept = fence(small_got, up_kept)
+    small_kept, small_got = reduce_step(add(small_kept, small_got), steps[1], device)
+    gate_got, up_got, dx_other, dx_own, small_kept = fence(
+        gate_got, up_got, dx_other, dx_own, small_kept
+    )
+    own_gate = add(gate_kept, gate_got)[0]
+    own_up = add(up_kept, up_got)[0]
+    owned_gateup = jnp.stack([own_gate, own_up], axis=1)
+    all_gateup = lax.all_gather(owned_gateup.astype(LOW), "dp", axis=0, tiled=True)
+    dx_got = deal_out(dx_own[:quarter_rows], dx_other)
+    out_far = far(out_got)
+    small_got, owned_gateup = fence(small_got, owned_gateup)
+    small_kept, small_got = reduce_step(add(small_kept, small_got), steps[2], device)
+    small_got, small_kept = fence(small_got, small_kept)
+    own_small = add(small_kept, small_got)[0]
+    all_small = lax.all_gather(own_small.astype(LOW), "dp", axis=0, tiled=False)
+
+    owned = (own_small, own_gate, own_up, own_down)
     own_square = sum([jnp.sum(part_grad * part_grad) for part_grad in owned])
     gains = jnp.sum((gains_far + gains_own).reshape(2, 8, LANES // head_dim, head_dim), axis=(1, 2))
     packed = jnp.concatenate(
@@ -861,12 +924,15 @@
     limit = math.sqrt(2 * D * H * HD + 2 * D * KV * HD + 3 * D * FF + 2 * D + 2 * HD)
     factor = jnp.minimum(1.0, limit / clip_value)
 
+    dx_far = far(dx_got)
+
+    qkv_cols = query_cols + 2 * key_cols
     owned_parts = (
-        own_qkv[:, :query_cols],
-        own_qkv[:, query_cols:].reshape(-1, 2, key_cols),
-        own_output.T,
-        jnp.stack([own_gate, own_up], axis=1),
-        own_down.T,
+        own_small[:, :query_cols],
+        own_small[:, query_cols:qkv_cols].reshape(-1, 2, key_cols),
+        own_small[:, qkv_cols:].T,
+        owned_gateup,
+        owned_down,
     )
     starts = (start_query, start_keyval, start_output, start_gateup, start_down)
     masters = (master_query, master_keyval, master_output, master_gateup, master_down)
@@ -877,27 +943,19 @@
     next_norms = norm_gains - step * moment_norms
     next_heads = head_gains - step * moment_heads
 
-    order = places_of(devices, device)
-
-    def spread(own):
-        return pick(gather_dp(own.astype(LOW), devices), order)
-
-    all_qkv = spread(own_qkv).reshape(width, -1)
-    all_output = spread(own_output).reshape(width, -1)
-    all_gateup = spread(owned_parts[3]).reshape(width, 2, hidden)
-    all_down = spread(owned_parts[4])
-    pull = step * factor
-
-    def finish(ahead_part, gradient):
-        return (ahead_part.astype(FULL) - pull * gradient.astype(FULL)).astype(LOW)
-
-    done_small = finish(ahead_small, jnp.concatenate([all_qkv, all_output], axis=1))
+    pull = (step * factor).reshape(1)
+    output = settle(out_got, out_far)
+    input_grad = settle(dx_got, dx_far)
+    done_query, done_keyval, done_output = finish_small(
+        pull, ahead_small, all_small, query_cols, qkv_cols
+    )
+    done_gateup = ahead_gateup.astype(FULL) - pull[0] * all_gateup.astype(FULL)
     weights = (
-        done_small[:, :query_cols],
-        done_small[:, query_cols : query_cols + 2 * key_cols].reshape(width, 2, key_cols),
-        done_small[:, query_cols + 2 * key_cols :].T,
-        finish(ahead_gateup, all_gateup),
-        finish(ahead_down, all_down).transpose(1, 0, 2).reshape(hidden, width),
+        done_query,
+        done_keyval.reshape(width, 2, key_cols),
+        done_output,
+        done_gateup.astype(LOW),
+        finish_down(pull, ahead_down, all_down),
     )
     return (
         output,

time: 830 us -> 714 us (0.86)
  waiting for transfers between devices: 257 us -> 215 us
  other arithmetic: 128 us -> 88.9 us
  starting transfers between devices: 80.7 us -> 52.4 us
  Pallas kernels: 205 us -> 181 us
  local copies, waits for them, and re-layouts: 88.5 us -> 110 us
    ppermute x63 -> x47, waiting for transfers between devices: 236 us -> 127 us  [swap(): lax.ppermute(values, axis, [(place, place ^ bit) for place in range(size)])]
    all_gather x1 -> x4, waiting for transfers between devices: 0.01 us -> 36.4 us  [the longest x1 36.4 us: local(): lax.all_gather(owned_gateup.astype(LOW), 'dp', axis=0, tiled=True)]
    all_to_all x4, waiting for transfers between devices: 21.5 us -> 50.8 us  [across_dp(): return lax.all_to_all(values, 'dp', split_axis=0, concat_axis=0, tiled=True)]
    concatenate x14 -> x4, other arithmetic: 33.5 us -> 5.21 us  [the longest x2 2.2 us: deal_out(): rows = jnp.concatenate([mine, other], axis=0)]
    ppermute x63 -> x47, starting transfers between devices: 58 us -> 30.9 us  [swap(): lax.ppermute(values, axis, [(place, place ^ bit) for place in range(size)])]
    pallas_call x11 -> x7, Pallas kernels: 35.2 us -> 20.2 us  [pick(): pl.pallas_call(pick_body, in_specs=[SMEM, HELD], out_specs=VMEM, out_shap...]
    pallas_call x2 -> x4, Pallas kernels: 75.1 us -> 66.6 us  [the longest x2 54 us: feed(): pl.pallas_call(feed_body, grid=(steps,), in_specs=in_specs, out_specs=out...]
    unnamed x211 -> x201, local copies, waits for them, and re-layouts: 35 us -> 41.5 us
  transfers between devices with their start and end apart: 70 -> 57, of which waited for: 23 -> 25; matrix products, arithmetic and copies ran while one was open for 29% -> 29% of each run, Pallas kernels for 21% -> 25%
where the time goes in v2:
time: 714 us; the launch traced here: 707 us
  waiting for transfers between devices  215 us (30%)
  Pallas kernels  181 us (25%)
  local copies, waits for them, and re-layouts  110 us (15%)
  other arithmetic  88.9 us (12%)
  starting transfers between devices  52.4 us (7%)
  matrix products  37.3 us (5%)
  between operations  22.1 us (3%)
    ppermute x47, waiting for transfers between devices, swap(): lax.ppermute(values, axis, [(place, place ^ bit) for place in range(size)])  127 us
    pallas_call x2, Pallas kernels, feed(): pl.pallas_call(feed_body, grid=(steps,), in_specs=in_specs, out_specs=out...  54 us
    all_to_all x4, waiting for transfers between devices, across_dp(): return lax.all_to_all(values, 'dp', split_axis=0, concat_axis=0, tiled=True)  50.8 us
    pallas_call x2, Pallas kernels, attend_back(): pl.pallas_call(functools.partial(attend_back_body, last, dims), in_specs=...  44.5 us
    unnamed x201, local copies, waits for them, and re-layouts  41.5 us
    dot_general x11, matrix products, dot(): lax.dot_general(left, right, (((left_dim,), (right_dim,)), ((), ())), pre...  37.3 us
    all_gather x1, waiting for transfers between devices, local(): lax.all_gather(owned_gateup.astype(LOW), 'dp', axis=0, tiled=True)  36.4 us
    ppermute x47, starting transfers between devices, swap(): lax.ppermute(values, axis, [(place, place ^ bit) for place in range(size)])  30.9 us
  transfers between devices with their start and end apart: 57, of which 25 were waited for; matrix products, arithmetic and copies ran while one was open for 29% of the time, Pallas kernels for 25%

profile of v2, /device:TPU:0, one launch (start us, length us, event | category | flops | bytes accessed | tf_op | source)
XLA Modules:
  0.0 707.1 jit_solution(16423369762284136887)
XLA Ops:
  12.3 7.4 %all-to-all-start = ((bf16[8,72,1024]{2,1,0:T(8,128)(2,1)}), bf16[8,72,1024]{2,1,0:T(8,128)(2,1)S(1)}, u32[]{:S(2)}, u32[]{:S(2)}) async-start(bf16[8,72,1024]{2,1,0:T(8,128)(2,1)} %shard_map.408), calls=%async_computation | async-start | bytes 2359296 | tf_op jit(solution)/shard_map/all_to_all | solution.py:411
  28.3 10.6 %fusion.47 = (bf16[1024,1,1152]{2,1,0:T(2,128)(2,1)}, bf16[1024,1,1152]{2,1,0:T(2,128)(2,1)}) fusion(bf16[1024,2,1152]{2,1,0:T(2,128)(2,1)} %param.32), kind=kLoop, calls=%fused_computation.187 | loop fusion | bytes 9437184 | tf_op jit(solution)/shard_map/slice | solution.py:661
  50.8 6.9 copy_bitcast_fusion
  67.3 6.0 all-to-all-start.1
  86.3 14.5 %all-to-all-done.1.source.first.second = bf16[8,72,1024]{2,1,0:T(8,128)(2,1)S(1)} async-done(((bf16[8,72,1024]{2,1,0:T(8,128)(2,1)}), bf16[8,72,1024]{2,1,0:T(8,128)(2,1)S(1)}, u32[]{:S(2)}, u32[]{:S(2)}) %all-to-all-start.1) | async-done | bytes 1179680 | tf_op jit(solution)/shard_map/all_to_all | solution.py:411
  108.4 14.0 %shard_map.412 = (bf16[1152,256]{1,0:T(8,128)(2,1)}, bf16[1152,384]{1,0:T(8,128)(2,1)}, f32[2,1152,128]{2,1,0:T(8,128)}, bf16[2,1152,128]{2,1,0:T(8,128)(2,1)}, ...) custom-call(s32[1]{0:T(128)} %bitcast.refs_0_.member, ...), custom_call_target="tpu_custom_call" | custom-call | flops 12000000000 | bytes 12000000 | tf_op jit(solution)/shard_map/pallas_call | solution.py:723
  123.2 15.3 %shard_map.413 = (bf16[1152,256]{1,0:T(8,128)(2,1)}, bf16[1152,384]{1,0:T(8,128)(2,1)}, f32[2,1152,128]{2,1,0:T(8,128)}, bf16[2,1152,128]{2,1,0:T(8,128)(2,1)}, ...) custom-call(s32[1]{0:T(128)} %bitcast.refs_0_.member, ...), custom_call_target="tpu_custom_call" | custom-call | flops 12000000000 | bytes 12000000 | tf_op jit(solution)/shard_map/pallas_call | solution.py:723
  143.0 14.4 %collective-permute-done.6.second = bf16[4,72,1024]{2,1,0:T(8,128)(2,1)S(1)} collective-permute-done((bf16[4,72,1024]{2,1,0:T(8,128)(2,1)}, bf16[4,72,1024]{2,1,0:T(8,128)(2,1)S(1)}, u32[]{:S(2)}, u32[]{:S(2)}) %collective-permute-start.6) | collective-permute-done | bytes 589856 | tf_op jit(solution)/shard_map/ppermute | solution.py:33
  171.7 14.0 %collective-permute-done.9.first = bf16[4,72,1024]{2,1,0:T(8,128)(2,1)} collective-permute-done((bf16[4,72,1024]{2,1,0:T(8,128)(2,1)}, bf16[4,72,1024]{2,1,0:T(8,128)(2,1)}, u32[]{:S(2)}, u32[]{:S(2)}) %collective-permute-start.9) | collective-permute-done | bytes 589856 | tf_op jit(solution)/shard_map/ppermute | solution.py:33
  187.3 27.1 %shard_map.417 = (bf16[2304,1152]{1,0:T(8,128)(2,1)}, bf16[2304,1152]{1,0:T(8,128)(2,1)}, bf16[2304,1152]{1,0:T(8,128)(2,1)}, bf16[2304,1024]{1,0:T(8,128)(2,1)}...) custom-call(bf16[576,1024]{1,0:T(8,128)(2,1)} %multiply_convert_fusi, ...), custom_call_target="tpu_custom_call" | custom-call | flops 16307453952 | bytes 28311552 | tf_op jit(solution)/shard_map/pallas_call | solution.py:355
  223.3 26.9 %shard_map.419 = (bf16[2304,1152]{1,0:T(8,128)(2,1)}, bf16[2304,1152]{1,0:T(8,128)(2,1)}, bf16[2304,1152]{1,0:T(8,128)(2,1)}, bf16[2304,1024]{1,0:T(8,128)(2,1)}...) custom-call(bf16[576,1024]{1,0:T(8,128)(2,1)} %collective-permute-do, ...), custom_call_target="tpu_custom_call", output_to_operand_aliasing={{0}: (7, {}), {1}: (8, {}), {2}: (9, {}), {3}: (10, {}), {4... | custom-call | flops 16307453952 | bytes 28311552 | tf_op jit(solution)/shard_map/pallas_call | solution.py:355
  260.0 9.1 %convolution_convert_fusion.1 = bf16[1024,1152]{1,0:T(8,128)(2,1)S(1)} fusion(bf16[2304,1024]{1,0:T(8,128)(2,1)} %get-tuple-element.188, bf16[2304,1152]{1,0:T(8,128)(2,1)S(1)} %copy-done.84), kind=kOutput, calls=%fused_computation.2 | convolution fusion | flops 5436997632 | bytes 12386304 | tf_op jit(solution)/shard_map/dot_general | solution.py:26
  269.2 6.8 convolution_convert_fusion.2
  281.5 6.0 collective-permute-done.15
  292.8 7.2 %convolution_convert_fusion = bf16[1024,1152]{1,0:T(8,128)(2,1)S(1)} fusion(bf16[2304,1024]{1,0:T(8,128)(2,1)S(1)} %bitcast.191, bf16[2304,1152]{1,0:T(8,128)(2,1)S(1)} %bitcast.185), kind=kOutput, calls=%fused_computation.1 | convolution fusion | flops 5436997632 | bytes 12386304 | tf_op jit(solution)/shard_map/dot_general | solution.py:26
  307.8 20.2 %shard_map.420 = (bf16[1152,512]{1,0:T(8,128)(2,1)}, f32[16,128]{1,0:T(8,128)}) custom-call(s32[1]{0:T(128)} %bitcast.refs_0_.member, bf16[576,1024]{1,0:T(8,128)(2,1)} %copy-done.4, bf16[576,1024]{1,0:T(8,128)(2,1)} %copy-done.18, bf16[256,1024]{1,0:T(8,128)(2,1)} %copy-done.81, bf16[1152,256]{1,0:T(8,128)(2,1)} %get-tuple-element.203.refs_4_, ...), custom_call_target="tpu_custom_call" | custom-call | flops 20000000000 | bytes 14000000 | tf_op jit(solution)/shard_map/pallas_call | solution.py:760
  354.7 24.3 %shard_map.421 = (bf16[1152,512]{1,0:T(8,128)(2,1)}, f32[16,128]{1,0:T(8,128)}, bf16[576,1024]{1,0:T(8,128)(2,1)}, bf16[576,1024]{1,0:T(8,128)(2,1)}) custom-call(s32[1]{0:T(128)} %bitcast.refs_0_.member, bf16[576,1024]{1,0:T(8,128)(2,1)} %copy-done.4, bf16[576,1024]{1,0:T(8,128)(2,1)} %copy-done.18, bf16[256,1024]{1,0:T(8,128)(2,1)} %refs_3_.2, ...), custom_call_target="tpu_custom_call" | custom-call | flops 20000000000 | bytes 14000000 | tf_op jit(solution)/shard_map/pallas_call | solution.py:760
  411.4 5.6 reshape_reshape.15
  430.7 4.8 copy.146
  439.0 7.4 %collective-permute-done.31 = bf16[2,128,1152]{2,1,0:T(8,128)(2,1)} collective-permute-done((bf16[2,128,1152]{2,1,0:T(8,128)(2,1)}, bf16[2,128,1152]{2,1,0:T(8,128)(2,1)}, u32[]{:S(2)}, u32[]{:S(2)}) %collective-permute-start.31) | collective-permute-done | bytes 589856 | tf_op jit(solution)/shard_map/ppermute | solution.py:33
  458.9 17.2 %collective-permute-done.32 = bf16[1,128,1152]{2,1,0:T(8,128)(2,1)S(1)} collective-permute-done((bf16[1,128,1152]{2,1,0:T(8,128)(2,1)S(1)}, bf16[1,128,1152]{2,1,0:T(8,128)(2,1)S(1)}, u32[]{:S(2)}, u32[]{:S(2)}) %collective-permute-start.32) | collective-permute-done | bytes 294944 | tf_op jit(solution)/shard_map/ppermute | solution.py:33
  476.0 6.2 collective-permute-done.30
  485.1 11.4 %collective-permute-done.41 = bf16[1,128,768]{2,1,0:T(8,128)(2,1)S(1)} collective-permute-done((bf16[1,128,768]{2,1,0:T(8,128)(2,1)S(1)}, bf16[1,128,768]{2,1,0:T(8,128)(2,1)S(1)}, u32[]{:S(2)}, u32[]{:S(2)}) %collective-permute-start.41) | collective-permute-done | bytes 196640 | tf_op jit(solution)/shard_map/ppermute | solution.py:33
  539.9 34.6 %all-to-all-done.3.refs_0_ = bf16[8,72,1024]{2,1,0:T(8,128)(2,1)S(1)} async-done(((bf16[8,72,1024]{2,1,0:T(8,128)(2,1)}), bf16[8,72,1024]{2,1,0:T(8,128)(2,1)S(1)}, u32[]{:S(2)}, u32[]{:S(2)}) %all-to-all-start.3) | async-done | bytes 1179680 | tf_op jit(solution)/shard_map/all_to_all | solution.py:411
  583.9 15.0 %collective-permute-done.37.refs_1_ = bf16[8,72,1024]{2,1,0:T(8,128)(2,1)} collective-permute-done((bf16[8,72,1024]{2,1,0:T(8,128)(2,1)S(1)}, bf16[8,72,1024]{2,1,0:T(8,128)(2,1)}, u32[]{:S(2)}, u32[]{:S(2)}) %collective-permute-start.37) | collective-permute-done | bytes 1179680 | tf_op jit(solution)/shard_map/ppermute | solution.py:33
  615.8 5.6 shard_map.423
  621.4 6.0 shard_map.426
  633.7 6.5 shard_map.427
  640.2 5.5 shard_map.425
  645.8 36.4 %all-gather.14.cloned.1.call-done = bf16[1024,2,1152]{2,0,1:T(8,128)(2,1)} async-done(((bf16[128,2,1152]{2,0,1:T(8,128)(2,1)}), bf16[1024,2,1152]{2,0,1:T(8,128)(2,1)}) %all-gather.14.cloned.1.call-update) | async-done | bytes 4718608 | tf_op jit(solution)/shard_map/all_gather | solution.py:901
  682.1 7.4 %subtract_convert_fusion = bf16[1024,2,1152]{2,0,1:T(8,128)(2,1)} fusion(bf16[1024,2,1152]{2,0,1:T(8,128)(2,1)} %all-gather.14.cloned.1.call-done, bf16[1024,2,1152]{2,0,1:T(8,128)(2,1)} %all-gather.10.cloned.1.call-done, f32[]{:T(128)} %mul.566), kind=kLoop, calls=%fused_computation | loop fusion | flops 11796480 | bytes 14155780 | tf_op jit(solution)/shard_map/convert_element_type | solution.py:957
  689.6 9.4 %copy.162 = bf16[1024,2,1152]{2,1,0:T(2,128)(2,1)} copy(bf16[1024,2,1152]{2,0,1:T(8,128)(2,1)} %subtract_convert_fusion) | data formatting | bytes 9437184
  (460 shorter events, 275.4 us)
Async XLA Ops:
  12.3 46.7 %all-to-all-start = ((bf16[8,72,1024]{2,1,0:T(8,128)(2,1)}), bf16[8,72,1024]{2,1,0:T(8,128)(2,1)S(1)}, u32[]{:S(2)}, u32[]{:S(2)}) async-start(bf16[8,72,1024]{2,1,0:T(8,128)(2,1)} %shard_map.408), calls=%async_computation | async-start | bytes 2359296 | tf_op jit(solution)/shard_map/all_to_all | solution.py:411
  20.6 38.4 %collective-permute-start.1 = (bf16[1024,256]{1,0:T(8,128)(2,1)}, bf16[1024,256]{1,0:T(8,128)(2,1)}, u32[]{:S(2)}, u32[]{:S(2)}) collective-permute-start(bf16[1024,256]{1,0:T(8,128)(2,1)} %bitcast.137.refs_4_.refs_18_), channel_id=1, source_target_pairs={{0,2},{1,3},{2,0},{3,1},{4,6},{5,7},{6,4},{7,5},{8,10},{9,11},{10,... | collective-permute-start | bytes 1572872 | tf_op jit(solution)/shard_map/ppermute | solution.py:33
  22.1 36.9 %collective-permute-start = (bf16[1024,256]{1,0:T(8,128)(2,1)}, bf16[1024,256]{1,0:T(8,128)(2,1)}, u32[]{:S(2)}, u32[]{:S(2)}) collective-permute-start(bf16[1024,256]{1,0:T(8,128)(2,1)} %refs_17_.1), channel_id=1, source_target_pairs={{0,2},{1,3},{2,0},{3,1},{4,6},{5,7},{6,4},{7,5},{8,10},{9,11},{10,... | collective-permute-start | bytes 1572872 | tf_op jit(solution)/shard_map/ppermute | solution.py:33
  67.3 33.4 %all-to-all-start.1 = ((bf16[8,72,1024]{2,1,0:T(8,128)(2,1)}), bf16[8,72,1024]{2,1,0:T(8,128)(2,1)S(1)}, u32[]{:S(2)}, u32[]{:S(2)}) async-start(bf16[8,72,1024]{2,1,0:T(8,128)(2,1)} %shard_map.411), calls=%async_computation.1 | async-start | bytes 2359296 | tf_op jit(solution)/shard_map/all_to_all | solution.py:411
  73.3 141.2 %all-gather.16.cloned.1.call-start = ((), (), s32[]{:S(2)}) async-start(), calls=%async_computation.7 | async-start | bytes 2654208 | tf_op jit(solution)/shard_map/all_gather | solution.py:782
  100.8 289.6 %all-gather.10.cloned.1.call-start = ((), (), s32[]{:S(2)}) async-start(), calls=%async_computation.4 | async-start | bytes 5308416 | tf_op jit(solution)/shard_map/all_gather | solution.py:783
  138.5 438.3 %all-gather.18.cloned.1.call-start = ((), (), s32[]{:S(2)}) async-start(), calls=%async_computation.8 | async-start | bytes 1769472 | tf_op jit(solution)/shard_map/all_gather | solution.py:784
  185.8 28.7 %collective-permute-start.10 = (bf16[576,1024]{1,0:T(8,128)(2,1)}, bf16[576,1024]{1,0:T(8,128)(2,1)}, u32[]{:S(2)}, u32[]{:S(2)}) collective-permute-start(bf16[576,1024]{1,0:T(8,128)(2,1)} %multiply_convert_fusion.n_own), channel_id=1, source_target_pairs={{0,2},{1,3},{2,0},{3,1},{4,6},{5,7},{6,4},{7,5},{8,10},{9,11},{10,... | collective-permute-start | bytes 3538952 | tf_op jit(solution)/shard_map/ppermute | solution.py:33
  218.9 33.8 %collective-permute-start.16 = (bf16[576,1024]{1,0:T(8,128)(2,1)}, bf16[576,1024]{1,0:T(8,128)(2,1)}, u32[]{:S(2)}, u32[]{:S(2)}) collective-permute-start(bf16[576,1024]{1,0:T(8,128)(2,1)} %get-tuple-element.192), channel_id=1, source_target_pairs={{0,1},{1,0},{2,3},{3,2},{4,5},{5,4},{6,7},{7,6},{8,9},{9,8},{10,11... | collective-permute-start | bytes 3538952 | tf_op jit(solution)/shard_map/ppermute | solution.py:33
  252.2 35.3 %collective-permute-start.11 = (bf16[576,1024]{1,0:T(8,128)(2,1)}, bf16[576,1024]{1,0:T(8,128)(2,1)S(1)}, u32[]{:S(2)}, u32[]{:S(2)}) collective-permute-start(bf16[576,1024]{1,0:T(8,128)(2,1)} %get-tuple-element.171), channel_id=1, source_target_pairs={{0,1},{1,0},{2,3},{3,2},{4,5},{5,4},{6,7},{7,6},{8,9},{9,8},{10,11... | collective-permute-start | bytes 3538952 | tf_op jit(solution)/shard_map/ppermute | solution.py:33
  259.3 28.2 %collective-permute-start.15 = (bf16[576,1024]{1,0:T(8,128)(2,1)S(1)}, bf16[576,1024]{1,0:T(8,128)(2,1)S(1)}, u32[]{:S(2)}, u32[]{:S(2)}) collective-permute-start(bf16[576,1024]{1,0:T(8,128)(2,1)S(1)} %add_convert_fusion.1), channel_id=1, source_target_pairs={{0,2},{1,3},{2,0},{3,1},{4,6},{5,7},{6,4},{7,5},{8,10},{9,11},{10,... | collective-permute-start | bytes 3538952 | tf_op jit(solution)/shard_map/ppermute | solution.py:33
  301.1 29.2 %collective-permute-start.19 = (bf16[4,128,1152]{2,1,0:T(8,128)(2,1)}, bf16[4,128,1152]{2,1,0:T(8,128)(2,1)}, u32[]{:S(2)}, u32[]{:S(2)}) collective-permute-start(bf16[4,128,1152]{2,1,0:T(8,128)(2,1)} %dynamic-slice_bitcast_fusion.4), channel_id=1, source_target_pairs={{0,4},{4,0},{8,12},{12,8},{16,20},{20,16},{24,28},{28,24},{1,5},{5... | collective-permute-start | bytes 3538952 | tf_op jit(solution)/shard_map/ppermute | solution.py:33
  302.5 83.3 %collective-permute-start.23 = (bf16[4,128,1152]{2,1,0:T(8,128)(2,1)}, bf16[4,128,1152]{2,1,0:T(8,128)(2,1)}, u32[]{:S(2)}, u32[]{:S(2)}) collective-permute-start(bf16[4,128,1152]{2,1,0:T(8,128)(2,1)} %get-tuple-element.375), channel_id=1, source_target_pairs={{0,4},{4,0},{8,12},{12,8},{16,20},{20,16},{24,28},{28,24},{1,5},{5... | collective-permute-start | bytes 3538952 | tf_op jit(solution)/shard_map/ppermute | solution.py:33
  303.2 87.2 %collective-permute-start.22 = (bf16[4,128,1152]{2,1,0:T(8,128)(2,1)}, bf16[4,128,1152]{2,1,0:T(8,128)(2,1)}, u32[]{:S(2)}, u32[]{:S(2)}) collective-permute-start(bf16[4,128,1152]{2,1,0:T(8,128)(2,1)} %get-tuple-element.377), channel_id=1, source_target_pairs={{0,4},{4,0},{8,12},{12,8},{16,20},{20,16},{24,28},{28,24},{1,5},{5... | collective-permute-start | bytes 3538952 | tf_op jit(solution)/shard_map/ppermute | solution.py:33
  337.7 54.3 %all-to-all-start.2 = ((bf16[8,72,1024]{2,1,0:T(8,128)(2,1)}), bf16[8,72,1024]{2,1,0:T(8,128)(2,1)S(1)}, u32[]{:S(2)}, u32[]{:S(2)}) async-start(bf16[8,72,1024]{2,1,0:T(8,128)(2,1)} %shard_map.422), calls=%async_computation.2 | async-start | bytes 2359296 | tf_op jit(solution)/shard_map/all_to_all | solution.py:411
  341.3 280.1 %all-gather.12.cloned.1.call-start = ((), (), s32[]{:S(2)}) async-start(), calls=%async_computation.5 | async-start | bytes 1769472 | tf_op jit(solution)/shard_map/all_gather | solution.py:908
  344.3 46.0 %collective-permute-start.21 = (bf16[2,128,1152]{2,1,0:T(8,128)(2,1)}, bf16[2,128,1152]{2,1,0:T(8,128)(2,1)}, u32[]{:S(2)}, u32[]{:S(2)}) collective-permute-start(bf16[2,128,1152]{2,1,0:T(8,128)(2,1)} %fusion.5), channel_id=1, source_target_pairs={{0,8},{4,12},{8,0},{12,4},{16,24},{20,28},{24,16},{28,20},{1,9},{5... | collective-permute-start | bytes 1769480 | tf_op jit(solution)/shard_map/ppermute | solution.py:33
  350.6 56.0 %collective-permute-start.34 = (bf16[1024,512]{0,1:T(8,128)(2,1)}, bf16[1024,512]{0,1:T(8,128)(2,1)}, u32[]{:S(2)}, u32[]{:S(2)}) collective-permute-start(bf16[1024,512]{0,1:T(8,128)(2,1)} %add_convert_fusion.2), channel_id=1, source_target_pairs={{0,2},{1,3},{2,0},{3,1},{4,6},{5,7},{6,4},{7,5},{8,10},{9,11},{10,... | collective-permute-start | bytes 3145736 | tf_op jit(solution)/shard_map/ppermute | solution.py:33
  353.3 31.2 %collective-permute-start.35 = (bf16[1024,256]{0,1:T(8,128)(2,1)}, bf16[1024,256]{0,1:T(8,128)(2,1)S(1)}, u32[]{:S(2)}, u32[]{:S(2)}) collective-permute-start(bf16[1024,256]{0,1:T(8,128)(2,1)} %fusion.1), channel_id=1, source_target_pairs={{0,2},{1,3},{2,0},{3,1},{4,6},{5,7},{6,4},{7,5},{8,10},{9,11},{10,... | collective-permute-start | bytes 1572872 | tf_op jit(solution)/shard_map/ppermute | solution.py:33
  396.0 39.6 %collective-permute-start.29 = (bf16[2,128,1152]{2,1,0:T(8,128)(2,1)}, bf16[2,128,1152]{2,1,0:T(8,128)(2,1)}, u32[]{:S(2)}, u32[]{:S(2)}) collective-permute-start(bf16[2,128,1152]{2,1,0:T(8,128)(2,1)} %fusion.6), channel_id=1, source_target_pairs={{0,8},{4,12},{8,0},{12,4},{16,24},{20,28},{24,16},{28,20},{1,9},{5... | collective-permute-start | bytes 1769480 | tf_op jit(solution)/shard_map/ppermute | solution.py:33
  398.1 37.5 %collective-permute-start.28 = (bf16[1,128,1152]{2,1,0:T(8,128)(2,1)}, bf16[1,128,1152]{2,1,0:T(8,128)(2,1)}, u32[]{:S(2)}, u32[]{:S(2)}) collective-permute-start(bf16[1,128,1152]{2,1,0:T(8,128)(2,1)} %dynamic-slice_convert_fusion.5), channel_id=1, source_target_pairs={{0,16},{4,20},{8,24},{12,28},{16,0},{20,4},{24,8},{28,12},{1,17},{... | collective-permute-start | bytes 884744 | tf_op jit(solution)/shard_map/ppermute | solution.py:33
  399.9 35.7 %collective-permute-start.27 = (bf16[576,1024]{1,0:T(8,128)(2,1)}, bf16[576,1024]{1,0:T(8,128)(2,1)}, u32[]{:S(2)}, u32[]{:S(2)}) collective-permute-start(bf16[576,1024]{1,0:T(8,128)(2,1)} %get-tuple-element.222), channel_id=1, source_target_pairs={{0,1},{1,0},{2,3},{3,2},{4,5},{5,4},{6,7},{7,6},{8,9},{9,8},{10,11... | collective-permute-start | bytes 3538952 | tf_op jit(solution)/shard_map/ppermute | solution.py:33
  451.5 30.7 %collective-permute-start.33 = (bf16[288,1024]{1,0:T(8,128)(2,1)S(1)}, bf16[288,1024]{1,0:T(8,128)(2,1)S(1)}, u32[]{:S(2)}, u32[]{:S(2)}) collective-permute-start(bf16[288,1024]{1,0:T(8,128)(2,1)S(1)} %slice.122), channel_id=1, source_target_pairs={{0,2},{1,3},{2,0},{3,1},{4,6},{5,7},{6,4},{7,5},{8,10},{9,11},{10,... | collective-permute-start | bytes 1769480 | tf_op jit(solution)/shard_map/ppermute | solution.py:33
  455.1 27.1 %collective-permute-start.30 = (bf16[1,128,1152]{2,1,0:T(8,128)(2,1)S(1)}, bf16[1,128,1152]{2,1,0:T(8,128)(2,1)S(1)}, u32[]{:S(2)}, u32[]{:S(2)}) collective-permute-start(bf16[1,128,1152]{2,1,0:T(8,128)(2,1)S(1)} %dynamic-slice_convert_fusion.4), channel_id=1, source_target_pairs={{0,16},{4,20},{8,24},{12,28},{16,0},{20,4},{24,8},{28,12},{1,17},{... | collective-permute-start | bytes 884744 | tf_op jit(solution)/shard_map/ppermute | solution.py:33
  497.2 132.2 %all-gather.20.cloned.1.call-start = ((), (), s32[]{:S(2)}) async-start(), calls=%async_computation.9 | async-start | bytes 2654208 | tf_op jit(solution)/shard_map/all_gather | solution.py:892
  530.3 151.9 %all-gather.14.cloned.1.call-start = ((), (), s32[]{:S(2)}) async-start(), calls=%async_computation.6 | async-start | bytes 5308416 | tf_op jit(solution)/shard_map/all_gather | solution.py:901
  535.6 38.9 %all-to-all-start.3 = ((bf16[8,72,1024]{2,1,0:T(8,128)(2,1)}), bf16[8,72,1024]{2,1,0:T(8,128)(2,1)S(1)}, u32[]{:S(2)}, u32[]{:S(2)}) async-start(bf16[8,72,1024]{2,1,0:T(8,128)(2,1)} %shard_map.424), calls=%async_computation.3 | async-start | bytes 2359296 | tf_op jit(solution)/shard_map/all_to_all | solution.py:411
  539.3 40.2 %collective-permute-start.24 = (bf16[8,72,1024]{2,1,0:T(8,128)(2,1)S(1)}, bf16[8,72,1024]{2,1,0:T(8,128)(2,1)}, u32[]{:S(2)}, u32[]{:S(2)}) collective-permute-start(bf16[8,72,1024]{2,1,0:T(8,128)(2,1)S(1)} %copy-done.16), channel_id=1, source_target_pairs={{0,2},{1,3},{2,0},{3,1},{4,6},{5,7},{6,4},{7,5},{8,10},{9,11},{10,... | collective-permute-start | bytes 3538952 | tf_op jit(solution)/shard_map/ppermute | solution.py:33
  579.5 36.3 %collective-permute-start.25 = (bf16[8,72,1024]{2,1,0:T(8,128)(2,1)S(1)}, bf16[8,72,1024]{2,1,0:T(8,128)(2,1)}, u32[]{:S(2)}, u32[]{:S(2)}) collective-permute-start(bf16[8,72,1024]{2,1,0:T(8,128)(2,1)S(1)} %copy-done.16), channel_id=1, source_target_pairs={{0,1},{1,0},{2,3},{3,2},{4,5},{5,4},{6,7},{7,6},{8,9},{9,8},{10,11... | collective-permute-start | bytes 3538952 | tf_op jit(solution)/shard_map/ppermute | solution.py:33
  579.5 36.3 %collective-permute-start.26 = (bf16[8,72,1024]{2,1,0:T(8,128)(2,1)}, bf16[8,72,1024]{2,1,0:T(8,128)(2,1)}, u32[]{:S(2)}, u32[]{:S(2)}) collective-permute-start(bf16[8,72,1024]{2,1,0:T(8,128)(2,1)} %collective-permute-done.24.refs_1_), channel_id=1, source_target_pairs={{0,1},{1,0},{2,3},{3,2},{4,5},{5,4},{6,7},{7,6},{8,9},{9,8},{10,11... | collective-permute-start | bytes 3538952 | tf_op jit(solution)/shard_map/ppermute | solution.py:33
  583.9 56.3 %collective-permute-start.38 = (bf16[8,72,1024]{2,1,0:T(8,128)(2,1)S(1)}, bf16[8,72,1024]{2,1,0:T(8,128)(2,1)}, u32[]{:S(2)}, u32[]{:S(2)}) collective-permute-start(bf16[8,72,1024]{2,1,0:T(8,128)(2,1)S(1)} %all-to-all-done.3.refs_0_), channel_id=1, source_target_pairs={{0,1},{1,0},{2,3},{3,2},{4,5},{5,4},{6,7},{7,6},{8,9},{9,8},{10,11... | collective-permute-start | bytes 3538952 | tf_op jit(solution)/shard_map/ppermute | solution.py:33
  598.9 41.3 %collective-permute-start.39 = (bf16[8,72,1024]{2,1,0:T(8,128)(2,1)}, bf16[8,72,1024]{2,1,0:T(8,128)(2,1)}, u32[]{:S(2)}, u32[]{:S(2)}) collective-permute-start(bf16[8,72,1024]{2,1,0:T(8,128)(2,1)} %collective-permute-done.37.refs_1_), channel_id=1, source_target_pairs={{0,1},{1,0},{2,3},{3,2},{4,5},{5,4},{6,7},{7,6},{8,9},{9,8},{10,11... | collective-permute-start | bytes 3538952 | tf_op jit(solution)/shard_map/ppermute | solution.py:33
  (118 other events, 1081.2 us)
Sparse Core Ops, SparseCore 0:
  100.9 49.9 all-gather.15
  153.1 78.4 all-gather.9
  252.3 43.6 all-gather.17
  497.4 41.3 all-gather.11
  540.8 60.8 all-gather.19
  603.7 78.3 all-gather.13

commit v3 on v2

--- a/solution.py
+++ b/solution.py
@@ -5,6 +5,7 @@
 import jax.numpy as jnp
 from jax import lax
 from jax.experimental import pallas as pl
+from jax.experimental.layout import Layout, with_layout_constraint
 from jax.experimental.pallas import tpu as pltpu
 from jax.sharding import PartitionSpec as P
 
@@ -31,6 +32,10 @@
 def swap(values, axis, bit):
     size = lax.axis_size(axis)
     return lax.ppermute(values, axis, [(place, place ^ bit) for place in range(size)])
+
+
+def row_major(values):
+    return with_layout_constraint(values, Layout(tuple(range(values.ndim))))
 
 
 def far(values):
@@ -303,7 +308,8 @@
 
 
 def feed_body(n_own, n_near, c_own, c_near, w_gate, w_up, w_down, *refs):
-    (inner, d_gate, d_up, n_all, c_all, d_own, d_near, y_own, y_near) = refs[-9:]
+    (inner, d_both, n_all, c_all, d_own, d_near, y_own, y_near) = refs[-8:]
+    hidden = w_gate.shape[1]
     mine = pl.program_id(0) < pl.num_programs(0) // 2
     n_rows = jnp.where(mine, n_own[...], n_near[...])
     c_rows = jnp.where(mine, c_own[...], c_near[...])
@@ -315,9 +321,10 @@
     sigma = 1.0 / (1.0 + jnp.exp(-gate))
     held = gate * sigma
     inner[...] = (held * up_part).astype(LOW)
-    d_gate[...] = (d_inner * up_part * sigma * (1.0 + gate * (1.0 - sigma))).astype(LOW)
-    d_up[...] = (d_inner * held).astype(LOW)
-    total = dot(d_gate[...], w_gate[...], 1, 1) + dot(d_up[...], w_up[...], 1, 1)
+    d_both[:, :hidden] = (d_inner * up_part * sigma * (1.0 + gate * (1.0 - sigma))).astype(LOW)
+    d_both[:, hidden:] = (d_inner * held).astype(LOW)
+    total = dot(d_both[:, :hidden], w_gate[...], 1, 1)
+    total = total + dot(d_both[:, hidden:], w_up[...], 1, 1)
     product = dot(inner[...], w_down[...])
 
     @pl.when(mine)
@@ -342,15 +349,15 @@
     part = lambda cols: pl.BlockSpec((block, cols), lambda i: (i + steps * half, 0))
     in_specs = [first, second, first, second] + [whole(v) for v in (w_gate, w_up, w_down)]
     outs = [
-        jax.ShapeDtypeStruct((4 * rows, cols), LOW) for cols in (hidden, hidden, hidden, width, width)
+        jax.ShapeDtypeStruct((4 * rows, cols), LOW) for cols in (hidden, 2 * hidden, width, width)
     ]
     outs += [jax.ShapeDtypeStruct((rows, width), LOW)] * 4
-    out_specs = [part(hidden)] * 3 + [part(width)] * 2
+    out_specs = [part(hidden), part(2 * hidden)] + [part(width)] * 2
     out_specs += [first, second, first, second]
     aliases = {}
     if half:
-        in_specs += [pl.BlockSpec(memory_space=pl.ANY)] * 5
-        aliases = {7 + index: index for index in range(5)}
+        in_specs += [pl.BlockSpec(memory_space=pl.ANY)] * 4
+        aliases = {7 + index: index for index in range(4)}
     work = 2 * rows * width * hidden * 2 * 6
     return pl.pallas_call(
         feed_body,
@@ -469,81 +476,215 @@
     return pieces.reshape(count * 4 * part_rows, width)
 
 
+def finish_down_body(device, pull, ahead, held, more, weight, gradient, arrived):
+    apart = places_apart(ahead.shape[0])
+    copies = placing(apart, device, held, more, gradient, arrived)
+    fetch(copies)
+    cols = ahead.shape[2]
+    for index in range(ahead.shape[0]):
+        value = ahead[index].astype(FULL) - pull[0] * gradient[index].astype(FULL)
+        weight[:, index * cols : (index + 1) * cols] = value.astype(LOW)
+
+
+def finish_small_body(device, pull, ahead, held, more, query, keyval, output, gradient, arrived):
+    apart = places_apart(ahead.shape[0])
+    fetch(placing(apart, device, held, more, gradient, arrived))
+    rows = ahead.shape[1]
+    first = query.shape[1]
+    second = first + keyval.shape[1]
+    for index in range(ahead.shape[0]):
+        value = ahead[index].astype(FULL) - pull[0] * gradient[index].astype(FULL)
+        here = slice(index * rows, (index + 1) * rows)
+        query[here, :] = value[:, :first].astype(LOW)
+        keyval[here, :] = value[:, first:second].astype(LOW)
+        output[:, here] = value[:, second:].T.astype(LOW)
+
+
+def places_apart(count):
+    apart = [0]
+    for step in reversed(bits_of(count)):
+        apart = apart + [other + step for other in apart]
+    return apart
+
+
+def placing(apart, device, held, more, target, arrived):
+    half = len(apart) // 2
+    copies = []
+    for index, distance in enumerate(apart):
+        source = held.at[index] if index < half else more.at[index - half]
+
+        def copy_of(_, index=index, distance=distance, source=source):
+            return pltpu.make_async_copy(
+                source, target.at[device[0] ^ distance], arrived.at[index]
+            )
+
+        copies.append((1, copy_of))
+    return copies
+
+
+def place_shards_body(device, *refs):
+    *sources, target, arrived = refs
+    apart = places_apart(target.shape[0])
+    half = len(apart) // 2
+    rows = sources[0].shape[1]
+    copies = []
+    for chunk in range(len(sources) // 2):
+        held, more = sources[2 * chunk : 2 * chunk + 2]
+        for index, distance in enumerate(apart):
+            source = held.at[index] if index < half else more.at[index - half]
+
+            def copy_of(_, index=index, distance=distance, source=source, chunk=chunk):
+                there = target.at[device[0] ^ distance, pl.ds(chunk * rows, rows)]
+                return pltpu.make_async_copy(source, there, arrived.at[chunk, index])
+
+            copies.append((1, copy_of))
+    fetch(copies)
+
+
 def kernel_params():
     return pltpu.CompilerParams(vmem_limit_bytes=VMEM_BYTES)
 
 
-def finish_down_body(pull, ahead, gradient, weight):
-    value = ahead[0].astype(FULL) - pull[0] * gradient[0].astype(FULL)
-    weight[...] = value.astype(LOW)
-
-
-def finish_down(pull, ahead, gradient):
+def place_shards(device, devices, *chunks):
+    shape = (devices, len(chunks) * chunks[0][0].shape[1]) + chunks[0][0].shape[2:]
+    sources = [part for chunk in chunks for part in chunk]
+    return pl.pallas_call(
+        place_shards_body,
+        in_specs=[SMEM] + [HELD] * len(sources),
+        out_specs=VMEM,
+        out_shape=jax.ShapeDtypeStruct(shape, LOW),
+        scratch_shapes=[pltpu.SemaphoreType.DMA((len(chunks), devices))],
+        compiler_params=kernel_params(),
+    )(device, *sources)
+
+
+def finish_down(device, pull, ahead, held, more):
     count, rows, cols = ahead.shape
     if cols % LANES:
+        gradient = place_shards(device, count, (held, more))
         value = ahead.astype(FULL) - pull * gradient.astype(FULL)
         return value.astype(LOW).transpose(1, 0, 2).reshape(rows, count * cols)
-    shard = pl.BlockSpec((1, rows, cols), lambda i: (i, 0, 0))
     return pl.pallas_call(
         finish_down_body,
-        grid=(count,),
-        in_specs=[SMEM, shard, shard],
-        out_specs=pl.BlockSpec((rows, cols), lambda i: (0, i)),
+        in_specs=[SMEM, SMEM, VMEM, HELD, HELD],
+        out_specs=VMEM,
         out_shape=jax.ShapeDtypeStruct((rows, count * cols), LOW),
+        scratch_shapes=[pltpu.VMEM(ahead.shape, LOW), pltpu.SemaphoreType.DMA((count,))],
         compiler_params=kernel_params(),
-    )(pull, ahead, gradient)
-
-
-def finish_small_body(pull, ahead, gradient, query, keyval, output):
-    value = ahead[0].astype(FULL) - pull[0] * gradient[0].astype(FULL)
-    first = query.shape[1]
-    second = first + keyval.shape[1]
-    query[...] = value[:, :first].astype(LOW)
-    keyval[...] = value[:, first:second].astype(LOW)
-    output[...] = value[:, second:].T.astype(LOW)
-
-
-def finish_small(pull, ahead, gradient, first, second):
+    )(device, pull, ahead, held, more)
+
+
+def finish_small(device, pull, ahead, held, more, first, second):
     count, rows, cols = ahead.shape
     if rows % LANES:
+        gradient = place_shards(device, count, (held, more))
         value = (ahead.astype(FULL) - pull * gradient.astype(FULL)).astype(LOW)
         value = value.reshape(count * rows, cols)
         return value[:, :first], value[:, first:second], value[:, second:].T
-    shard = pl.BlockSpec((1, rows, cols), lambda i: (i, 0, 0))
-    shapes = [(count * rows, first), (count * rows, second - first), (cols - second, count * rows)]
-    specs = [
-        pl.BlockSpec((rows, first), lambda i: (i, 0)),
-        pl.BlockSpec((rows, second - first), lambda i: (i, 0)),
-        pl.BlockSpec((cols - second, rows), lambda i: (0, i)),
+    shapes = [
+        (count * rows, first),
+        (count * rows, second - first),
+        (cols - second, count * rows),
     ]
     return pl.pallas_call(
         finish_small_body,
-        grid=(count,),
-        in_specs=[SMEM, shard, shard],
-        out_specs=specs,
+        in_specs=[SMEM, SMEM, VMEM, HELD, HELD],
+        out_specs=[VMEM] * 3,
         out_shape=[jax.ShapeDtypeStruct(shape, LOW) for shape in shapes],
+        scratch_shapes=[pltpu.VMEM(ahead.shape, LOW), pltpu.SemaphoreType.DMA((count,))],
         compiler_params=kernel_params(),
-    )(pull, ahead, gradient)
+    )(device, pull, ahead, held, more)
 
 
 def fence(*values):
     return lax.optimization_barrier(values)
 
 
-def reduce_step(total, step, device):
-    bit = (device // step) & 1
-    split = total.reshape((total.shape[0] // 2, 2) + total.shape[1:])
-    sent = lax.dynamic_index_in_dim(split, 1 - bit, 1, keepdims=False).astype(LOW)
-    kept = lax.dynamic_index_in_dim(split, bit, 1, keepdims=False)
-    return (kept, swap(sent, "dp", step))
-
-
 def add(first, second):
     return first.astype(FULL) + second.astype(FULL)
 
 
-def by_device(product, devices):
-    return product.reshape((devices, product.shape[0] // devices) + product.shape[1:])
+def halve_body(pairs, bit, kept, got, leaving, staying):
+    for index, (base, stride) in enumerate(pairs):
+        there = base + bit[0] * stride
+        total = kept[there].astype(FULL) + got[there].astype(FULL)
+        staying[index] = total
+        there = base + (1 - bit[0]) * stride
+        total = kept[there].astype(FULL) + got[there].astype(FULL)
+        leaving[index] = total.astype(LOW)
+
+
+def pairs_of(count, stride):
+    return [(index, stride) for index in range(count) if not (index // stride) % 2]
+
+
+class Halving:
+    def __init__(self, product, device, devices, order):
+        rows = product.shape[0] // devices
+        self.device = device
+        self.left = list(reversed(range(len(bits_of(devices)))))
+        self.order = list(order)
+        place, bit, stride = self.next()
+        split = product.reshape((-1, 2, stride, rows) + product.shape[1:])
+        shape = (devices // 2, rows) + product.shape[1:]
+        leaving = lax.dynamic_index_in_dim(split, 1 - bit, 1, keepdims=False).reshape(shape)
+        self.kept = lax.dynamic_index_in_dim(split, bit, 1, keepdims=False).reshape(shape)
+        self.got = swap(leaving.astype(LOW), "dp", 1 << place)
+
+    def next(self):
+        place = self.order.pop(0)
+        stride = 1 << (len(self.left) - 1 - self.left.index(place))
+        self.left.remove(place)
+        return place, (self.device >> place) & 1, stride
+
+    def go(self):
+        place, bit, stride = self.next()
+        count = self.kept.shape[0]
+        shape = (count // 2,) + self.kept.shape[1:]
+        leaving, self.kept = pl.pallas_call(
+            functools.partial(halve_body, pairs_of(count, stride)),
+            in_specs=[SMEM, VMEM, VMEM],
+            out_specs=[VMEM, VMEM],
+            out_shape=[jax.ShapeDtypeStruct(shape, LOW), jax.ShapeDtypeStruct(shape, FULL)],
+            compiler_params=kernel_params(),
+        )(bit.reshape(1).astype(jnp.int32), self.kept, self.got)
+        self.got = swap(leaving, "dp", 1 << place)
+
+    def own(self):
+        while self.order:
+            self.go()
+        return add(self.kept, self.got)[0]
+
+
+def small_body(pairs, size, bit, *refs):
+    (first, first_got, second, second_got, leaving, staying) = refs
+    wide = first.shape[1]
+    for index, (base, stride) in enumerate(pairs):
+        for target, side in ((leaving, 1 - bit[0]), (staying, bit[0])):
+            rows = pl.ds(pl.multiple_of((base + side * stride) * size, size), size)
+            total = first[rows, :].astype(FULL) + first_got[rows, :].astype(FULL)
+            target[index, :, :wide] = total.astype(target.dtype)
+            total = second[rows, :].astype(FULL) + second_got[rows, :].astype(FULL)
+            target[index, :, wide:] = total.astype(target.dtype)
+
+
+def small_halving(parts, device, devices, order):
+    self = Halving.__new__(Halving)
+    self.device = device
+    self.left = list(reversed(range(len(bits_of(devices)))))
+    self.order = list(order)
+    place, bit, stride = self.next()
+    size = parts[0].shape[0] // devices
+    shape = (devices // 2, size, parts[0].shape[1] + parts[2].shape[1])
+    leaving, self.kept = pl.pallas_call(
+        functools.partial(small_body, pairs_of(devices, stride), size),
+        in_specs=[SMEM] + [VMEM] * 4,
+        out_specs=[VMEM, VMEM],
+        out_shape=[jax.ShapeDtypeStruct(shape, LOW), jax.ShapeDtypeStruct(shape, FULL)],
+        compiler_params=kernel_params(),
+    )(bit.reshape(1).astype(jnp.int32), *parts)
+    self.got = swap(leaving, "dp", 1 << place)
+    return self
 
 
 def row_norm(values, gain_row):
@@ -660,42 +801,35 @@
     w_gate = w_gateup[:, 0]
     w_up = w_gateup[:, 1]
 
-    def ahead(master, begin):
-        return (master - 0.5 * step * begin).astype(LOW)
+    masters = (master_query, master_keyval, master_output, master_gateup, master_down)
+    starts = (start_query, start_keyval, start_output, start_gateup, start_down)
+    early = fence(
+        (x_got, far_query, far_keyval, cosine, sine, w_gate, w_up), cotangent, w_output, masters
+    )
+    (x_got, far_query, far_keyval, cosine, sine, w_gate, w_up), cotangent, w_output, held = early
+
+    def ahead(index):
+        return (held[index] - 0.5 * step * starts[index]).astype(LOW)
 
     small = jnp.concatenate(
-        [
-            ahead(master_query, start_query),
-            ahead(master_keyval, start_keyval).reshape(-1, 2 * key_cols),
-            ahead(master_output, start_output).T,
-        ],
-        axis=1,
-    )
-    part_gateup = ahead(master_gateup, start_gateup)
-    part_down = ahead(master_down, start_down)
-
-    early = fence(
-        (x_got, far_query, far_keyval, cosine, sine, w_gate, w_up),
-        (small, part_gateup, part_down, cotangent, w_output),
-    )
-    x_got, far_query, far_keyval, cosine, sine, w_gate, w_up = early[0]
-    small, part_gateup, part_down, cotangent, w_output = early[1]
+        [ahead(0), ahead(1).reshape(-1, 2 * key_cols), ahead(2).T], axis=1
+    )
+    part_gateup = row_major(ahead(3))
+    part_down = ahead(4)
     x_other = far(pick(x_got, other_source))
     c_got = deal_in(cotangent)
     x_other, w_output = fence(x_other, w_output)
     groups = (
         (w_query, w_keyval_flat, w_output),
-        (far_query, far_keyval, far(w_output)),
-    )
+        (far_query, far_keyval),
+    )
+    far_output = far(w_output)
     x_own = rows_of(join(x_got, own_source, x_other, in_order))
 
     x_full = x_own.astype(FULL)
     norm_one_f, inv_one = row_norm(x_full, norm_gains[0])
     norm_own = norm_one_f.astype(LOW)
     norm_near = near(norm_own)
-    stepped = fence(norm_near, c_got, small, part_gateup, part_down)
-    norm_near, c_got, small, part_gateup, part_down = stepped
-
     dims = (slot_rows, slot_pieces, part_rows, slot_rows // 6, head_dim, heads)
     shape = jax.ShapeDtypeStruct
 
@@ -732,7 +866,9 @@
             ],
             compiler_params=pltpu.CompilerParams(vmem_limit_bytes=VMEM_BYTES),
             cost_estimate=pl.CostEstimate(
-                flops=12_000_000_000, bytes_accessed=12_000_000, transcendentals=0
+                flops=12_000_000_000 if last else 1_000_000_000,
+                bytes_accessed=12_000_000 if last else 1_000_000,
+                transcendentals=0,
             ),
         )(*arguments)
 
@@ -777,32 +913,38 @@
         )(*arguments)
 
     first_kept = attend(False, groups[0], ())
-    c_own_far = far(pick(c_got, other_source))
-    c_other_far = far(pick(c_got, own_source))
+    stepped = fence(first_kept, c_got, small, part_gateup, part_down, far_output)
+    first_kept, c_got, small, part_gateup, part_down, far_output = stepped
+    groups = (groups[0], groups[1] + (far_output,))
+    c_first, c_second = pick(c_got, other_source), pick(c_got, own_source)
+    first_kept, c_first, c_second = fence(first_kept, c_first, c_second)
+    c_own_far, c_other_far = far(c_first), far(c_second)
+    ahead_gateup = lax.all_gather(part_gateup, "dp", axis=0, tiled=True)
     ahead_down = lax.all_gather(part_down, "dp", axis=0, tiled=False)
-    ahead_gateup = lax.all_gather(part_gateup, "dp", axis=0, tiled=True)
     ahead_small = lax.all_gather(small, "dp", axis=0, tiled=False)
     *second_kept, attn_own, attn_near = attend(
         True, groups[1], (groups[1][2], groups[0][2], first_kept[0])
     )
+    attn_own, attn_near, c_own_far = fence(attn_own, attn_near, c_own_far)
     attn_got = near(attn_near)
-    attn_got, attn_own, c_own_far = fence(attn_got, attn_own, c_own_far)
     c_own = rows_of(join(c_got, own_source, c_own_far, in_order))
+    attn_got, c_own = fence(attn_got, c_own)
     c_near = near(c_own)
     hidden_one = x_full + add(attn_own, attn_got)
     norm_two_f, inv_two = row_norm(hidden_one, norm_gains[1])
     two_own = norm_two_f.astype(LOW)
+    two_own, c_other_far = fence(two_own, c_other_far)
     two_near = near(two_own)
-    two_near, two_own, c_near, c_other_far = fence(two_near, two_own, c_near, c_other_far)
+    two_near, c_near = fence(two_near, c_near)
     two_far = far(two_own)
+    c_far = rows_of(join(c_other_far, in_order, c_got, other_source))
 
     *kept, d_own, d_near, y_own, y_near = feed(
         0, (), two_own, two_near, c_own, c_near, w_gate, w_up, w_down
     )
-    stepped = fence(two_far, d_own, d_near, c_other_far, y_near, ahead_down)
-    two_far, d_own, d_near, c_other_far, y_near, ahead_down = stepped
+    stepped = fence(two_far, d_own, d_near, y_near, ahead_gateup)
+    two_far, d_own, d_near, y_near, ahead_gateup = stepped
     two_across = near(two_far)
-    c_far = rows_of(join(c_other_far, in_order, c_got, other_source))
     c_across = near(c_far)
     d_got = near(d_near)
     y_got = near(y_near)
@@ -812,20 +954,20 @@
     far_got = near(far_near)
     pair_far = add(far_own, far_got).astype(LOW)
     pair_far, kept, far_y_near = fence(pair_far, kept, far_y_near)
-    inner, d_gate, d_up, two_all, c_all = kept
+    inner, d_both, two_all, c_all = kept
     pair_got = far(pair_far)
     far_y_got = near(far_y_near)
-    steps = bits_of(devices)
+    places = list(range(len(bits_of(devices))))
+    grad_both = dot(two_all, d_both, 0, 0).astype(LOW)
+    gate = Halving(grad_both[:, :hidden], device, devices, places[1:] + places[:1])
+    up = Halving(grad_both[:, hidden:], device, devices, places)
     grad_down = dot(c_all, inner, 0, 0).astype(LOW)
-    down_kept, down_got = reduce_step(by_device(grad_down, devices), steps[0], device)
-    grad_gate = dot(two_all, d_gate, 0, 0).astype(LOW)
-    gate_kept, gate_got = reduce_step(by_device(grad_gate, devices), steps[0], device)
+    down = Halving(grad_down, device, devices, places)
     y_pair = add(y_own, y_got) + hidden_one
     far_y_pair = add(far_y_own, far_y_got)
     y_leaving = jnp.concatenate([y_pair[quarter_rows:], far_y_pair[:quarter_rows]]).astype(LOW)
-    grad_up = dot(two_all, d_up, 0, 0).astype(LOW)
-    up_kept, up_got = reduce_step(by_device(grad_up, devices), steps[0], device)
-    pair_got, gate_kept, up_kept, y_leaving = fence(pair_got, gate_kept, up_kept, y_leaving)
+    stepped = fence(pair_got, y_leaving, down.kept, gate.kept, up.kept)
+    pair_got, y_leaving, down.kept, gate.kept, up.kept = stepped
     y_arrived = far(y_leaving)
 
     d_norm_two = add(d_own, d_got) + pair_got.astype(FULL)
@@ -838,22 +980,19 @@
         return dot(own, values[:half_rows], 0, 0) + dot(other, values[half_rows:], 0, 0)
 
     d_raw_far, gains_far = attend_back(False, groups[1], second_kept, dh_own, dh_near, ())
-    d_raw_far, down_got, y_arrived = fence(d_raw_far, down_got, y_arrived)
+    stepped = fence(d_raw_far, down.got, gate.got, ahead_down, y_arrived)
+    d_raw_far, down.got, gate.got, ahead_down, y_arrived = stepped
+    gate.go()
+    down.go()
 
     out_order = (place_from + (slot_count - slot) * slot_pieces) % pieces_dev
 
-    def deal_out(mine, other):
-        rows = jnp.concatenate([mine, other], axis=0)
-        return across_dp(pick(rows.reshape(pieces_dev, part_rows, width), out_order))
-
-    def settle(got, got_far):
-        return place_pieces((got, got_far, near(got), near(got_far)), target, member_ref)
-
-    out_got = deal_out(
-        (y_pair[:quarter_rows] + y_arrived[quarter_rows:].astype(FULL)).astype(LOW),
-        (far_y_pair[quarter_rows:] + y_arrived[:quarter_rows].astype(FULL)).astype(LOW),
-    )
-    down_kept, down_got = reduce_step(add(down_kept, down_got), steps[1], device)
+    def to_send(rows):
+        return pick(rows.reshape(pieces_dev, part_rows, width), out_order)
+
+    y_mine = y_pair[:quarter_rows] + y_arrived[quarter_rows:].astype(FULL)
+    y_other = far_y_pair[quarter_rows:] + y_arrived[:quarter_rows].astype(FULL)
+    out_rows = jnp.concatenate([y_mine, y_other], axis=0).astype(LOW)
     grad_output_got = far(over_rows(dh_own, dh_near, second_kept[0]).astype(LOW))
     grad_qkv_got = far(over_rows(norm_own, norm_near, d_raw_far).astype(LOW))
     grad_output_mine = over_rows(dh_own, dh_near, first_kept[0])
@@ -865,57 +1004,96 @@
         dh_near,
         (groups[0][0], groups[0][1], groups[1][0], groups[1][1], d_raw_far),
     )
-    stepped = fence(d_raw_own, d_one_near, down_got, gate_got, up_got, out_got, ahead_gateup)
-    d_raw_own, d_one_near, down_got, gate_got, up_got, out_got, ahead_gateup = stepped
+    stepped = fence(
+        (d_raw_own, d_one_near, down.got, gate.got, up.got), out_rows, grad_output_got, ahead_small
+    )
+    (d_raw_own, d_one_near, down.got, gate.got, up.got), *stepped = stepped
+    out_rows, grad_output_got, ahead_small = stepped
 
     d_one_got = near(d_one_near)
-    down_kept, down_got = reduce_step(add(down_kept, down_got), steps[2], device)
-    gate_kept, gate_got = reduce_step(add(gate_kept, gate_got), steps[1], device)
-    d_one_got, down_kept, gate_kept = fence(d_one_got, down_kept, gate_kept)
+    down.go()
+    gate.go()
+    up.go()
+    stepped = fence(d_one_got, down.kept, gate.kept, up.kept, d_raw_own, out_rows)
+    d_one_got, down.kept, gate.kept, up.kept, d_raw_own, out_rows = stepped
     d_norm_one = add(d_one_own, d_one_got)
     d_input_part, gain_one = row_norm_back(d_norm_one, x_full, inv_one, norm_gains[0])
     dx_own = (d_hidden + d_input_part).astype(LOW)
+    stepped = fence(dx_own, up.got, down.got, gate.got, out_rows)
+    dx_own, up.got, down.got, gate.got, out_rows = stepped
+
+    def grown(held, got):
+        return jnp.concatenate([held, got], axis=0)
+
+    def first_steps(own):
+        held = own.astype(LOW)[None]
+        for bit in reversed(bits_of(devices)[3:]):
+            held = grown(held, swap(held, "dp", bit))
+        return held
+
     dx_other = far(dx_own[quarter_rows:])
-    up_kept, up_got = reduce_step(add(up_kept, up_got), steps[1], device)
-    grad_qkv_mine = over_rows(norm_own, norm_near, d_raw_own)
-    grad_small = jnp.concatenate(
-        [add(grad_qkv_mine, grad_qkv_got), add(grad_output_mine, grad_output_got)], axis=1
-    )
-    small_kept, small_got = reduce_step(by_device(grad_small, devices), steps[0], device)
-
-    down_got, up_kept, gate_got = fence(down_got, up_kept, gate_got)
-    own_down = add(down_kept, down_got)[0]
+    up.go()
+    own_down = down.own()
     owned_down = own_down.T
-    gate_kept, gate_got = reduce_step(add(gate_kept, gate_got), steps[2], device)
-    up_got, gate_kept, owned_down = fence(up_got, gate_kept, owned_down)
-    up_kept, up_got = reduce_step(add(up_kept, up_got), steps[2], device)
-    all_down = lax.all_gather(owned_down.astype(LOW), "dp", axis=0, tiled=False)
-    small_got, up_kept = fence(small_got, up_kept)
-    small_kept, small_got = reduce_step(add(small_kept, small_got), steps[1], device)
-    gate_got, up_got, dx_other, dx_own, small_kept = fence(
-        gate_got, up_got, dx_other, dx_own, small_kept
-    )
-    own_gate = add(gate_kept, gate_got)[0]
-    own_up = add(up_kept, up_got)[0]
+    held_down = first_steps(owned_down)
+    down_more = swap(held_down, "dp", 4)
+    own_gate = gate.own()
+    grad_qkv_mine = over_rows(norm_own, norm_near, d_raw_own).astype(LOW)
+    small_parts = (grad_qkv_mine, grad_qkv_got, grad_output_mine, grad_output_got)
+    rest = small_halving(small_parts, device, devices, places)
+    stepped = fence(up.got, rest.got, dx_own, dx_other, down_more, own_gate, out_rows)
+    up.got, rest.got, dx_own, dx_other, down_more, own_gate, out_rows = stepped
+
+    own_up = up.own()
     owned_gateup = jnp.stack([own_gate, own_up], axis=1)
-    all_gateup = lax.all_gather(owned_gateup.astype(LOW), "dp", axis=0, tiled=True)
-    dx_got = deal_out(dx_own[:quarter_rows], dx_other)
-    out_far = far(out_got)
-    small_got, owned_gateup = fence(small_got, owned_gateup)
-    small_kept, small_got = reduce_step(add(small_kept, small_got), steps[2], device)
-    small_got, small_kept = fence(small_got, small_kept)
-    own_small = add(small_kept, small_got)[0]
-    all_small = lax.all_gather(own_small.astype(LOW), "dp", axis=0, tiled=False)
-
+    held_gateup = first_steps(row_major(owned_gateup.astype(LOW)))
+    gateup_more = swap(held_gateup, "dp", 4)
+    rest.go()
+    held_down = grown(held_down, down_more)
+    down_more = swap(held_down, "dp", 2)
+    dx_sent = to_send(jnp.concatenate([dx_own[:quarter_rows], dx_other], axis=0))
+    out_sent = to_send(out_rows)
+    stepped = fence(rest.got, down_more, gateup_more, dx_sent, out_sent)
+    rest.got, down_more, gateup_more, dx_sent, out_sent = stepped
+
+    held_gateup = grown(held_gateup, gateup_more)
+    gateup_more = swap(held_gateup, "dp", 2)
+    held_down = grown(held_down, down_more)
+    down_more = swap(held_down, "dp", 1)
+    rest.go()
+    rest.got, down_more, gateup_more, out_sent = fence(rest.got, down_more, gateup_more, out_sent)
+
+    held_gateup = grown(held_gateup, gateup_more)
+    half_shard = held_gateup.shape[1] // 2
+    held_lower, held_upper = held_gateup[:, :half_shard], held_gateup[:, half_shard:]
+    lower_more = swap(held_lower, "dp", 1)
+    out_got = across_dp(out_sent)
+    own_small = rest.own()
+    held_small = first_steps(own_small)
+    small_more = swap(held_small, "dp", 4)
     owned = (own_small, own_gate, own_up, own_down)
     own_square = sum([jnp.sum(part_grad * part_grad) for part_grad in owned])
     gains = jnp.sum((gains_far + gains_own).reshape(2, 8, LANES // head_dim, head_dim), axis=(1, 2))
     packed = jnp.concatenate(
         [gain_one, gain_two, gains.reshape(-1), jnp.broadcast_to(own_square, (LANES,))]
     ).reshape(-1, LANES)
-    for axis, size in (("mp", ways), ("dp", devices)):
-        for bit in bits_of(size):
-            packed = packed + swap(packed, axis, bit)
+    for bit in bits_of(ways):
+        packed = packed + swap(packed, "mp", bit)
+    stepped = fence(lower_more, out_got, small_more, own_small, held_upper, dx_sent, packed)
+    lower_more, out_got, small_more, own_small, held_upper, dx_sent, packed = stepped
+
+    for bit in bits_of(devices):
+        packed = packed + swap(packed, "dp", bit)
+    stepped = fence(held_upper, dx_sent, out_got, small_more, packed)
+    held_upper, dx_sent, out_got, small_more, packed = stepped
+    upper_more = swap(held_upper, "dp", 1)
+    dx_got = across_dp(dx_sent)
+    out_far = far(out_got)
+    held_small = grown(held_small, small_more)
+    small_more = swap(held_small, "dp", 2)
+    upper_more, dx_got, out_far, small_more = fence(upper_more, dx_got, out_far, small_more)
+    dx_far = far(dx_got)
+
     flat = packed.reshape(-1)
     norm_sum = flat[: 2 * width].reshape(2, width)
     head_sum = flat[2 * width : 2 * width + 2 * head_dim].reshape(2, head_dim)
@@ -924,7 +1102,8 @@
     limit = math.sqrt(2 * D * H * HD + 2 * D * KV * HD + 3 * D * FF + 2 * D + 2 * HD)
     factor = jnp.minimum(1.0, limit / clip_value)
 
-    dx_far = far(dx_got)
+    held_small = grown(held_small, small_more)
+    small_more = swap(held_small, "dp", 1)
 
     qkv_cols = query_cols + 2 * key_cols
     owned_parts = (
@@ -934,8 +1113,6 @@
         owned_gateup,
         owned_down,
     )
-    starts = (start_query, start_keyval, start_output, start_gateup, start_down)
-    masters = (master_query, master_keyval, master_output, master_gateup, master_down)
     moments = [0.5 * begin + factor * part_grad for begin, part_grad in zip(starts, owned_parts)]
     nexts = [held - step * moved for held, moved in zip(masters, moments)]
     moment_norms = 0.5 * start_norms + factor * norm_sum
@@ -944,18 +1121,26 @@
     next_heads = head_gains - step * moment_heads
 
     pull = (step * factor).reshape(1)
-    output = settle(out_got, out_far)
-    input_grad = settle(dx_got, dx_far)
+    output = place_pieces((out_got, out_far, near(out_got), near(out_far)), target, member_ref)
+    device_ref = device.reshape(1).astype(jnp.int32)
+    all_gateup = place_shards(
+        device_ref, devices, (held_lower, lower_more), (held_upper, upper_more)
+    ).reshape(ahead_gateup.shape)
+    done_gateup = (ahead_gateup.astype(FULL) - pull[0] * all_gateup.astype(FULL)).astype(LOW)
+    done_down = finish_down(device_ref, pull, ahead_down, held_down, down_more)
+    near_got = near(dx_got)
+    stepped = fence(dx_far, small_more, near_got, output, done_gateup, done_down, moments, nexts)
+    dx_far, small_more, near_got, output, done_gateup, done_down, moments, nexts = stepped
+    input_grad = place_pieces((dx_got, dx_far, near_got, near(dx_far)), target, member_ref)
     done_query, done_keyval, done_output = finish_small(
-        pull, ahead_small, all_small, query_cols, qkv_cols
-    )
-    done_gateup = ahead_gateup.astype(FULL) - pull[0] * all_gateup.astype(FULL)
+        device_ref, pull, ahead_small, held_small, small_more, query_cols, qkv_cols
+    )
     weights = (
         done_query,
         done_keyval.reshape(width, 2, key_cols),
         done_output,
-        done_gateup.astype(LOW),
-        finish_down(pull, ahead_down, all_down),
+        done_gateup,
+        done_down,
     )
     return (
         output,

time: 714 us -> 662 us (0.927)
  waiting for transfers between devices: 215 us -> 159 us
  local copies, waits for them, and re-layouts: 110 us -> 57.3 us
  Pallas kernels: 181 us -> 209 us
  starting transfers between devices: 52.4 us -> 74.7 us
    all_to_all x4, waiting for transfers between devices: 50.8 us -> 3.39 us  [across_dp(): return lax.all_to_all(values, 'dp', split_axis=0, concat_axis=0, tiled=True)]
    all_gather x3 -> x0, waiting for transfers between devices: 36.4 us -> none  [the longest x1 36.4 us: local(): lax.all_gather(owned_gateup.astype(LOW), 'dp', axis=0, tiled=True)]
    unnamed x201 -> x210, local copies, waits for them, and re-layouts: 41.5 us -> 13.3 us
    pallas_call x2 -> x12, Pallas kernels: 12.5 us -> 39.9 us  [the longest x8 21.2 us: go(): pl.pallas_call(functools.partial(halve_body, pairs_of(count, stride)), in...]
    ppermute x47 -> x57, starting transfers between devices: 30.9 us -> 50.4 us  [swap(): lax.ppermute(values, axis, [(place, place ^ bit) for place in range(size)])]
    ppermute x47 -> x57, waiting for transfers between devices: 127 us -> 140 us  [swap(): lax.ppermute(values, axis, [(place, place ^ bit) for place in range(size)])]
    add x10 -> x1, other arithmetic: 12.3 us -> 0.45 us  [add(): return first.astype(FULL) + second.astype(FULL)]
    concatenate x4 -> x9, other arithmetic: 5.68 us -> 17 us  [the longest x6 13.1 us: grown(): return jnp.concatenate([held, got], axis=0)]
  transfers between devices with their start and end apart: 57 -> 64, of which waited for: 25 -> 24; matrix products, arithmetic and copies ran while one was open for 29% -> 26% of each run, Pallas kernels for 25% -> 30%
where the time goes in v3:
time: 662 us; the launch traced here: 652 us
  Pallas kernels  209 us (32%)
  waiting for transfers between devices  159 us (24%)
  other arithmetic  86.9 us (13%)
  starting transfers between devices  74.7 us (11%)
  local copies, waits for them, and re-layouts  57.3 us (9%)
  matrix products  43.2 us (7%)
  between operations  22.1 us (3%)
    ppermute x57, waiting for transfers between devices, swap(): lax.ppermute(values, axis, [(place, place ^ bit) for place in range(size)])  140 us
    pallas_call x2, Pallas kernels, feed(): pl.pallas_call(feed_body, grid=(steps,), in_specs=in_specs, out_specs=out...  53.8 us
    ppermute x57, starting transfers between devices, swap(): lax.ppermute(values, axis, [(place, place ^ bit) for place in range(size)])  50.4 us
    pallas_call x2, Pallas kernels, attend_back(): pl.pallas_call(functools.partial(attend_back_body, last, dims), in_specs=...  44.4 us
    dot_general x10, matrix products, dot(): lax.dot_general(left, right, (((left_dim,), (right_dim,)), ((), ())), pre...  43.2 us
    pallas_call x2, Pallas kernels, attend(): pl.pallas_call(functools.partial(attend_body, last, dims), in_specs=[SMEM...  29.7 us
    all_to_all x4, starting transfers between devices, across_dp(): return lax.all_to_all(values, 'dp', split_axis=0, concat_axis=0, tiled=True)  23.6 us
    pallas_call x8, Pallas kernels, go(): pl.pallas_call(functools.partial(halve_body, pairs_of(count, stride)), in...  21.2 us
  transfers between devices with their start and end apart: 64, of which 24 were waited for; matrix products, arithmetic and copies ran while one was open for 26% of the time, Pallas kernels for 30%

profile of v3, /device:TPU:0, one launch (start us, length us, event | category | flops | bytes accessed | tf_op | source)
XLA Modules:
  0.0 651.7 jit_solution(722560916415562203)
XLA Ops:
  12.2 7.4 %all-to-all-start = ((bf16[8,72,1024]{2,1,0:T(8,128)(2,1)}), bf16[8,72,1024]{2,1,0:T(8,128)(2,1)S(1)}, u32[]{:S(2)}, u32[]{:S(2)}) async-start(bf16[8,72,1024]{2,1,0:T(8,128)(2,1)} %shard_map.408), calls=%async_computation | async-start | bytes 2359296 | tf_op jit(solution)/shard_map/all_to_all | solution.py:418
  22.1 10.5 %fusion.39 = (bf16[1024,1,1152]{2,1,0:T(2,128)(2,1)}, bf16[1024,1,1152]{2,1,0:T(2,128)(2,1)}) fusion(bf16[1024,2,1152]{2,1,0:T(2,128)(2,1)} %param.32), kind=kLoop, calls=%fused_computation.160 | loop fusion | bytes 9437184 | tf_op jit(solution)/shard_map/slice | solution.py:802
  33.9 6.8 %copy_bitcast_fusion = (bf16[1024,1152]{1,0:T(8,128)(2,1)}, bf16[1024,1152]{1,0:T(8,128)(2,1)}) fusion(bf16[1024,1,1152]{2,1,0:T(2,128)(2,1)} %get-tuple-element.533, bf16[1024,1,1152]{2,1,0:T(2,128)(2,1)} %get-tuple-element.534), kind=kLoop, calls=%fused_computation.6 | loop fusion | bytes 9437184 | tf_op jit(solution)/shard_map/squeeze | solution.py:802
  56.6 5.5 all-to-all-start.1
  80.1 14.0 %shard_map.411 = (bf16[1152,256]{1,0:T(8,128)(2,1)}, bf16[1152,384]{1,0:T(8,128)(2,1)}, f32[2,1152,128]{2,1,0:T(8,128)}, bf16[2,1152,128]{2,1,0:T(8,128)(2,1)}, ...) custom-call(s32[1]{0:T(128)} %bitcast.1.refs_0_.member, ...), custom_call_target="tpu_custom_call" | custom-call | flops 1000000000 | bytes 1000000 | tf_op jit(solution)/shard_map/pallas_call | solution.py:857
  101.2 15.7 %shard_map.415 = (bf16[1152,256]{1,0:T(8,128)(2,1)}, bf16[1152,384]{1,0:T(8,128)(2,1)}, f32[2,1152,128]{2,1,0:T(8,128)}, bf16[2,1152,128]{2,1,0:T(8,128)(2,1)}, ...) custom-call(s32[1]{0:T(128)} %bitcast.1.refs_0_.member, ...), custom_call_target="tpu_custom_call" | custom-call | flops 12000000000 | bytes 12000000 | tf_op jit(solution)/shard_map/pallas_call | solution.py:857
  138.9 26.9 %shard_map.417 = (bf16[2304,1152]{1,0:T(8,128)(2,1)}, bf16[2304,2304]{1,0:T(8,128)(2,1)}, bf16[2304,1024]{1,0:T(8,128)(2,1)}, bf16[2304,1024]{1,0:T(8,128)(2,1)}...) custom-call(bf16[576,1024]{1,0:T(8,128)(2,1)} %multiply_convert_fusi, ...), custom_call_target="tpu_custom_call" | custom-call | flops 16307453952 | bytes 28311552 | tf_op jit(solution)/shard_map/pallas_call | solution.py:362
  165.9 8.2 %all-gather.6.cloned.1.call-done = bf16[1024,2,1152]{2,1,0:T(2,128)(2,1)} async-done(((bf16[128,2,1152]{2,1,0:T(2,128)(2,1)}), bf16[1024,2,1152]{2,1,0:T(2,128)(2,1)}) %all-gather.6.cloned.1.call-update) | async-done | bytes 4718608 | tf_op jit(solution)/shard_map/all_gather | solution.py:922
  177.3 26.9 %shard_map.419 = (bf16[2304,1152]{1,0:T(8,128)(2,1)}, bf16[2304,2304]{1,0:T(8,128)(2,1)}, bf16[2304,1024]{1,0:T(8,128)(2,1)}, bf16[2304,1024]{1,0:T(8,128)(2,1)}...) custom-call(bf16[576,1024]{1,0:T(8,128)(2,1)} %collective-permute-do, ...), custom_call_target="tpu_custom_call", output_to_operand_aliasing={{0}: (7, {}), {1}: (8, {}), {2}: (9, {}), {3}: (10, {})} | custom-call | flops 16307453952 | bytes 28311552 | tf_op jit(solution)/shard_map/pallas_call | solution.py:362
  213.0 15.0 %convolution_convert_fusion = bf16[1024,2304]{1,0:T(8,128)(2,1)S(1)} fusion(bf16[2304,1024]{1,0:T(8,128)(2,1)S(1)} %copy-done.95, bf16[2304,2304]{1,0:T(8,128)(2,1)} %get-tuple-element.293), kind=kOutput, calls=%fused_computation.3 | convolution fusion | flops 10873995264 | bytes 20054016 | tf_op jit(solution)/shard_map/dot_general | solution.py:27
  228.0 6.9 %convolution_convert_fusion.1 = bf16[1024,1152]{1,0:T(8,128)(2,1)S(1)} fusion(bf16[2304,1024]{1,0:T(8,128)(2,1)S(1)} %bitcast.168, bf16[2304,1152]{1,0:T(8,128)(2,1)S(1)} %bitcast.166), kind=kOutput, calls=%fused_computation.4 | convolution fusion | flops 5436997632 | bytes 12386304 | tf_op jit(solution)/shard_map/dot_general | solution.py:27
  255.0 20.3 %shard_map.420 = (bf16[1152,512]{1,0:T(8,128)(2,1)}, f32[16,128]{1,0:T(8,128)}) custom-call(s32[1]{0:T(128)} %bitcast.1.refs_0_.member, bf16[576,1024]{1,0:T(8,128)(2,1)} %get-tuple-element.526.refs_1_, bf16[576,1024]{1,0:T(8,128)(2,1)} %collective-permute-done.18.refs_2_, bf16[256,1024]{1,0:T(8,128)(2,1)} %copy-done.90, ...), custom_call_target="tpu_custom_call" | custom-call | flops 20000000000 | bytes 14000000 | tf_op jit(solution)/shard_map/pallas_call | solution.py:896
  275.3 7.5 %all-gather.8.cloned.1.call-done = bf16[9216,128]{1,0:T(8,128)(2,1)} async-done(((bf16[1152,128]{1,0:T(8,128)(2,1)}), bf16[9216,128]{1,0:T(8,128)(2,1)}) %all-gather.8.cloned.1.call-update) | async-done | bytes 2359312 | tf_op jit(solution)/shard_map/all_gather | solution.py:923
  282.8 11.2 %collective-permute-done.20.got = bf16[4,128,1152]{2,1,0:T(8,128)(2,1)} collective-permute-done((bf16[4,128,1152]{2,1,0:T(8,128)(2,1)S(1)}, bf16[4,128,1152]{2,1,0:T(8,128)(2,1)}, u32[]{:S(2)}, u32[]{:S(2)}) %collective-permute-start.20) | collective-permute-done | bytes 1179680 | tf_op jit(solution)/shard_map/ppermute | solution.py:34
  309.2 24.1 %shard_map.421 = (bf16[1152,512]{1,0:T(8,128)(2,1)}, f32[16,128]{1,0:T(8,128)}, bf16[576,1024]{1,0:T(8,128)(2,1)}, bf16[576,1024]{1,0:T(8,128)(2,1)}) custom-call(s32[1]{0:T(128)} %bitcast.1.refs_0_.member, bf16[576,1024]{1,0:T(8,128)(2,1)} %get-tuple-element.526.refs_1_, bf16[576,1024]{1,0:T(8,128)(2,1)} %collective-permute-done.18.refs_2_, ...), custom_call_target="tpu_custom_call" | custom-call | flops 20000000000 | bytes 14000000 | tf_op jit(solution)/shard_map/pallas_call | solution.py:896
  388.3 20.6 %collective-permute-done.34 = bf16[1,1152,128]{2,1,0:T(8,128)(2,1)S(1)} collective-permute-done((bf16[1,1152,128]{2,1,0:T(8,128)(2,1)S(1)}, bf16[1,1152,128]{2,1,0:T(8,128)(2,1)S(1)}, u32[]{:S(2)}, u32[]{:S(2)}) %collective-permute-start.34) | collective-permute-done | bytes 294944 | tf_op jit(solution)/shard_map/ppermute | solution.py:34
  408.8 11.7 %collective-permute-done.30 = bf16[1,128,1152]{2,0,1:T(2,128)(2,1)S(1)} collective-permute-done((bf16[1,128,1152]{2,0,1:T(2,128)(2,1)S(1)}, bf16[1,128,1152]{2,0,1:T(2,128)(2,1)S(1)}, u32[]{:S(2)}, u32[]{:S(2)}) %collective-permute-start.30) | collective-permute-done | bytes 294944 | tf_op jit(solution)/shard_map/ppermute | solution.py:34
  438.9 21.7 %collective-permute-done.35.got = bf16[2,128,768]{2,1,0:T(8,128)(2,1)} collective-permute-done((bf16[2,128,768]{2,1,0:T(8,128)(2,1)}, bf16[2,128,768]{2,1,0:T(8,128)(2,1)}, u32[]{:S(2)}, u32[]{:S(2)}) %collective-permute-start.35) | collective-permute-done | bytes 393248 | tf_op jit(solution)/shard_map/ppermute | solution.py:34
  472.5 20.5 %collective-permute-done.38 = bf16[1,128,768]{2,1,0:T(8,128)(2,1)S(1)} collective-permute-done((bf16[1,128,768]{2,1,0:T(8,128)(2,1)}, bf16[1,128,768]{2,1,0:T(8,128)(2,1)S(1)}, u32[]{:S(2)}, u32[]{:S(2)}) %collective-permute-start.38) | collective-permute-done | bytes 196640 | tf_op jit(solution)/shard_map/ppermute | solution.py:34
  495.1 4.3 all-to-all-start.2
  499.4 5.3 pad_maximum_fusion
  520.3 14.0 %collective-permute-done.42 = bf16[1,128,768]{2,1,0:T(8,128)(2,1)S(1)} collective-permute-done((bf16[1,128,768]{2,1,0:T(8,128)(2,1)S(1)}, bf16[1,128,768]{2,1,0:T(8,128)(2,1)S(1)}, u32[]{:S(2)}, u32[]{:S(2)}) %collective-permute-start.42) | collective-permute-done | bytes 196640 | tf_op jit(solution)/shard_map/ppermute | solution.py:34
  534.3 5.0 collective-permute-done.41.refs_1_
  557.6 6.4 all-to-all-start.3
  572.7 5.6 shard_map.435
  584.8 9.4 %collective-permute-done.50 = bf16[2,128,768]{2,1,0:T(8,128)(2,1)S(1)} collective-permute-done((bf16[2,128,768]{2,1,0:T(8,128)(2,1)}, bf16[2,128,768]{2,1,0:T(8,128)(2,1)S(1)}, u32[]{:S(2)}, u32[]{:S(2)}) %collective-permute-start.50) | collective-permute-done | bytes 393248 | tf_op jit(solution)/shard_map/ppermute | solution.py:34
  598.8 5.0 shard_map.434
  607.9 9.2 %fusion = bf16[1024,2,1152]{2,1,0:T(2,128)(2,1)} fusion(f32[8,128,2,1152]{3,2,1,0:T(2,128)S(1)} %bitcast.133, bf16[1024,2,1152]{2,1,0:T(2,128)(2,1)S(1)} %bitcast.146), kind=kLoop, calls=%fused_computation.1 | loop fusion | flops 7077888 | bytes 18874368 | tf_op jit(solution)/shard_map/convert_element_type | solution.py:1129
  617.2 5.7 shard_map.433
  622.9 4.5 collective-permute-done.52.more
  629.0 4.5 shard_map.437
  638.1 5.5 shard_map.436
  (472 shorter events, 263.8 us)
Async XLA Ops:
  12.2 36.0 %all-to-all-start = ((bf16[8,72,1024]{2,1,0:T(8,128)(2,1)}), bf16[8,72,1024]{2,1,0:T(8,128)(2,1)S(1)}, u32[]{:S(2)}, u32[]{:S(2)}) async-start(bf16[8,72,1024]{2,1,0:T(8,128)(2,1)} %shard_map.408), calls=%async_computation | async-start | bytes 2359296 | tf_op jit(solution)/shard_map/all_to_all | solution.py:418
  56.6 37.6 %all-to-all-start.1 = ((bf16[8,72,1024]{2,1,0:T(8,128)(2,1)}), bf16[8,72,1024]{2,1,0:T(8,128)(2,1)S(1)}, u32[]{:S(2)}, u32[]{:S(2)}) async-start(bf16[8,72,1024]{2,1,0:T(8,128)(2,1)} %shard_map.412), calls=%async_computation.1 | async-start | bytes 2359296 | tf_op jit(solution)/shard_map/all_to_all | solution.py:418
  62.1 112.0 %all-gather.6.cloned.1.call-start = ((), (), s32[]{:S(2)}) async-start(), calls=%async_computation.4 | async-start | bytes 5308416 | tf_op jit(solution)/shard_map/all_gather | solution.py:922
  94.2 155.1 %all-gather.10.cloned.1.call-start = ((), (), s32[]{:S(2)}) async-start(), calls=%async_computation.6 | async-start | bytes 1769472 | tf_op jit(solution)/shard_map/all_gather | solution.py:924
  133.5 32.3 %collective-permute-start.8 = (bf16[576,1024]{1,0:T(8,128)(2,1)}, bf16[576,1024]{1,0:T(8,128)(2,1)}, u32[]{:S(2)}, u32[]{:S(2)}) collective-permute-start(bf16[576,1024]{1,0:T(8,128)(2,1)} %multiply_convert_fusion.n_own), channel_id=1, source_target_pairs={{0,2},{1,3},{2,0},{3,1},{4,6},{5,7},{6,4},{7,5},{8,10},{9,11},{10,... | collective-permute-start | bytes 3538952 | tf_op jit(solution)/shard_map/ppermute | solution.py:34
  138.8 36.4 %collective-permute-start.13 = (bf16[576,1024]{1,0:T(8,128)(2,1)}, bf16[576,1024]{1,0:T(8,128)(2,1)}, u32[]{:S(2)}, u32[]{:S(2)}) collective-permute-start(bf16[576,1024]{1,0:T(8,128)(2,1)} %bitcast.153), channel_id=1, source_target_pairs={{0,1},{1,0},{2,3},{3,2},{4,5},{5,4},{6,7},{7,6},{8,9},{9,8},{10,11... | collective-permute-start | bytes 3538952 | tf_op jit(solution)/shard_map/ppermute | solution.py:34
  174.1 108.7 %all-gather.8.cloned.1.call-start = ((), (), s32[]{:S(2)}) async-start(), calls=%async_computation.5 | async-start | bytes 2654208 | tf_op jit(solution)/shard_map/all_gather | solution.py:923
  174.6 30.2 %collective-permute-start.16 = (bf16[576,1024]{1,0:T(8,128)(2,1)}, bf16[576,1024]{1,0:T(8,128)(2,1)}, u32[]{:S(2)}, u32[]{:S(2)}) collective-permute-start(bf16[576,1024]{1,0:T(8,128)(2,1)} %get-tuple-element.287), channel_id=1, source_target_pairs={{0,1},{1,0},{2,3},{3,2},{4,5},{5,4},{6,7},{7,6},{8,9},{9,8},{10,11... | collective-permute-start | bytes 3538952 | tf_op jit(solution)/shard_map/ppermute | solution.py:34
  204.4 38.1 %collective-permute-start.11 = (bf16[576,1024]{1,0:T(8,128)(2,1)}, bf16[576,1024]{1,0:T(8,128)(2,1)S(1)}, u32[]{:S(2)}, u32[]{:S(2)}) collective-permute-start(bf16[576,1024]{1,0:T(8,128)(2,1)} %get-tuple-element.271), channel_id=1, source_target_pairs={{0,1},{1,0},{2,3},{3,2},{4,5},{5,4},{6,7},{7,6},{8,9},{9,8},{10,11... | collective-permute-start | bytes 3538952 | tf_op jit(solution)/shard_map/ppermute | solution.py:34
  211.2 29.0 %collective-permute-start.17 = (bf16[576,1024]{1,0:T(8,128)(2,1)S(1)}, bf16[576,1024]{1,0:T(8,128)(2,1)S(1)}, u32[]{:S(2)}, u32[]{:S(2)}) collective-permute-start(bf16[576,1024]{1,0:T(8,128)(2,1)S(1)} %copy-done.87), channel_id=1, source_target_pairs={{0,1},{1,0},{2,3},{3,2},{4,5},{5,4},{6,7},{7,6},{8,9},{9,8},{10,11... | collective-permute-start | bytes 3538952 | tf_op jit(solution)/shard_map/ppermute | solution.py:34
  211.4 31.1 %collective-permute-start.15 = (bf16[576,1024]{1,0:T(8,128)(2,1)S(1)}, bf16[576,1024]{1,0:T(8,128)(2,1)S(1)}, u32[]{:S(2)}, u32[]{:S(2)}) collective-permute-start(bf16[576,1024]{1,0:T(8,128)(2,1)S(1)} %add_convert_fusion.1), channel_id=1, source_target_pairs={{0,2},{1,3},{2,0},{3,1},{4,6},{5,7},{6,4},{7,5},{8,10},{9,11},{10,... | collective-permute-start | bytes 3538952 | tf_op jit(solution)/shard_map/ppermute | solution.py:34
  252.1 41.9 %collective-permute-start.20 = (bf16[4,128,1152]{2,1,0:T(8,128)(2,1)S(1)}, bf16[4,128,1152]{2,1,0:T(8,128)(2,1)}, u32[]{:S(2)}, u32[]{:S(2)}) collective-permute-start(bf16[4,128,1152]{2,1,0:T(8,128)(2,1)S(1)} %bitcast.152), channel_id=1, source_target_pairs={{0,8},{4,12},{8,0},{12,4},{16,24},{20,28},{24,16},{28,20},{1,9},{5... | collective-permute-start | bytes 3538952 | tf_op jit(solution)/shard_map/ppermute | solution.py:34
  252.6 41.3 %collective-permute-start.19 = (bf16[4,128,1152]{2,1,0:T(8,128)(2,1)S(1)}, bf16[4,128,1152]{2,1,0:T(8,128)(2,1)}, u32[]{:S(2)}, u32[]{:S(2)}) collective-permute-start(bf16[4,128,1152]{2,1,0:T(8,128)(2,1)S(1)} %copy-done.29), channel_id=1, source_target_pairs={{0,4},{4,0},{8,12},{12,8},{16,20},{20,16},{24,28},{28,24},{1,5},{5... | collective-permute-start | bytes 3538952 | tf_op jit(solution)/shard_map/ppermute | solution.py:34
  253.3 83.1 %collective-permute-start.24 = (bf16[4,128,1152]{2,1,0:T(8,128)(2,1)}, bf16[4,128,1152]{2,1,0:T(8,128)(2,1)}, u32[]{:S(2)}, u32[]{:S(2)}) collective-permute-start(bf16[4,128,1152]{2,1,0:T(8,128)(2,1)} %get-tuple-element.537), channel_id=1, source_target_pairs={{0,4},{4,0},{8,12},{12,8},{16,20},{20,16},{24,28},{28,24},{1,5},{5... | collective-permute-start | bytes 3538952 | tf_op jit(solution)/shard_map/ppermute | solution.py:34
  254.7 39.3 %collective-permute-start.21 = (bf16[576,1024]{1,0:T(8,128)(2,1)}, bf16[576,1024]{1,0:T(8,128)(2,1)}, u32[]{:S(2)}, u32[]{:S(2)}) collective-permute-start(bf16[576,1024]{1,0:T(8,128)(2,1)} %pad_maximum_fusion.1), channel_id=1, source_target_pairs={{0,2},{1,3},{2,0},{3,1},{4,6},{5,7},{6,4},{7,5},{8,10},{9,11},{10,... | collective-permute-start | bytes 3538952 | tf_op jit(solution)/shard_map/ppermute | solution.py:34
  298.7 37.7 %collective-permute-start.25 = (bf16[1024,256]{1,0:T(8,128)(2,1)}, bf16[1024,256]{1,0:T(8,128)(2,1)S(1)}, u32[]{:S(2)}, u32[]{:S(2)}) collective-permute-start(bf16[1024,256]{1,0:T(8,128)(2,1)} %fusion.2), channel_id=1, source_target_pairs={{0,2},{1,3},{2,0},{3,1},{4,6},{5,7},{6,4},{7,5},{8,10},{9,11},{10,... | collective-permute-start | bytes 1572872 | tf_op jit(solution)/shard_map/ppermute | solution.py:34
  303.2 33.2 %collective-permute-start.23 = (bf16[2,128,1152]{2,1,0:T(8,128)(2,1)}, bf16[2,128,1152]{2,1,0:T(8,128)(2,1)}, u32[]{:S(2)}, u32[]{:S(2)}) collective-permute-start(bf16[2,128,1152]{2,1,0:T(8,128)(2,1)} %get-tuple-element.321), channel_id=1, source_target_pairs={{0,16},{4,20},{8,24},{12,28},{16,0},{20,4},{24,8},{28,12},{1,17},{... | collective-permute-start | bytes 1769480 | tf_op jit(solution)/shard_map/ppermute | solution.py:34
  372.2 48.3 %collective-permute-start.32 = (bf16[4,128,768]{2,1,0:T(8,128)(2,1)}, bf16[4,128,768]{2,1,0:T(8,128)(2,1)}, u32[]{:S(2)}, u32[]{:S(2)}) collective-permute-start(bf16[4,128,768]{2,1,0:T(8,128)(2,1)} %get-tuple-element.347), channel_id=1, source_target_pairs={{0,4},{4,0},{8,12},{12,8},{16,20},{20,16},{24,28},{28,24},{1,5},{5... | collective-permute-start | bytes 2359304 | tf_op jit(solution)/shard_map/ppermute | solution.py:34
  378.8 41.7 %collective-permute-start.33 = (bf16[288,1024]{1,0:T(8,128)(2,1)S(1)}, bf16[288,1024]{1,0:T(8,128)(2,1)}, u32[]{:S(2)}, u32[]{:S(2)}) collective-permute-start(bf16[288,1024]{1,0:T(8,128)(2,1)S(1)} %slice.124), channel_id=1, source_target_pairs={{0,2},{1,3},{2,0},{3,1},{4,6},{5,7},{6,4},{7,5},{8,10},{9,11},{10,... | collective-permute-start | bytes 1769480 | tf_op jit(solution)/shard_map/ppermute | solution.py:34
  385.7 34.8 %collective-permute-start.30 = (bf16[1,128,1152]{2,0,1:T(2,128)(2,1)S(1)}, bf16[1,128,1152]{2,0,1:T(2,128)(2,1)S(1)}, u32[]{:S(2)}, u32[]{:S(2)}) collective-permute-start(bf16[1,128,1152]{2,0,1:T(2,128)(2,1)S(1)} %copy.130), channel_id=1, source_target_pairs={{0,16},{4,20},{8,24},{12,28},{16,0},{20,4},{24,8},{28,12},{1,17},{... | collective-permute-start | bytes 884744 | tf_op jit(solution)/shard_map/ppermute | solution.py:34
  423.8 36.7 %collective-permute-start.37 = (bf16[1,128,2,1152]{3,2,1,0:T(2,128)(2,1)S(1)}, bf16[1,128,2,1152]{3,2,1,0:T(2,128)(2,1)}, u32[]{:S(2)}, u32[]{:S(2)}) collective-permute-start(bf16[1,128,2,1152]{3,2,1,0:T(2,128)(2,1)S(1)} %convert_bitcast_fusion), channel_id=1, source_target_pairs={{0,16},{4,20},{8,24},{12,28},{16,0},{20,4},{24,8},{28,12},{1,17},{... | collective-permute-start | bytes 1769480 | tf_op jit(solution)/shard_map/ppermute | solution.py:34
  424.8 35.8 %collective-permute-start.36 = (bf16[2,1152,128]{2,1,0:T(8,128)(2,1)}, bf16[2,1152,128]{2,1,0:T(8,128)(2,1)}, u32[]{:S(2)}, u32[]{:S(2)}) collective-permute-start(bf16[2,1152,128]{2,1,0:T(8,128)(2,1)} %pad_maximum_fusion.8), channel_id=1, source_target_pairs={{0,8},{4,12},{8,0},{12,4},{16,24},{20,28},{24,16},{28,20},{1,9},{5... | collective-permute-start | bytes 1769480 | tf_op jit(solution)/shard_map/ppermute | solution.py:34
  429.4 31.1 %collective-permute-start.35 = (bf16[2,128,768]{2,1,0:T(8,128)(2,1)}, bf16[2,128,768]{2,1,0:T(8,128)(2,1)}, u32[]{:S(2)}, u32[]{:S(2)}) collective-permute-start(bf16[2,128,768]{2,1,0:T(8,128)(2,1)} %get-tuple-element.359), channel_id=1, source_target_pairs={{0,8},{4,12},{8,0},{12,4},{16,24},{20,28},{24,16},{28,20},{1,9},{5... | collective-permute-start | bytes 1179656 | tf_op jit(solution)/shard_map/ppermute | solution.py:34
  464.4 30.7 %collective-permute-start.40 = (bf16[2,128,2,1152]{3,2,1,0:T(2,128)(2,1)}, bf16[2,128,2,1152]{3,2,1,0:T(2,128)(2,1)}, u32[]{:S(2)}, u32[]{:S(2)}) collective-permute-start(bf16[2,128,2,1152]{3,2,1,0:T(2,128)(2,1)} %pad_maximum_fusion.6), channel_id=1, source_target_pairs={{0,8},{4,12},{8,0},{12,4},{16,24},{20,28},{24,16},{28,20},{1,9},{5... | collective-permute-start | bytes 3538952 | tf_op jit(solution)/shard_map/ppermute | solution.py:34
  495.1 44.2 %all-to-all-start.2 = ((bf16[8,72,1024]{2,1,0:T(8,128)(2,1)}), bf16[8,72,1024]{2,1,0:T(8,128)(2,1)}, u32[]{:S(2)}, u32[]{:S(2)}) async-start(bf16[8,72,1024]{2,1,0:T(8,128)(2,1)} %shard_map.431), calls=%async_computation.2 | async-start | bytes 2359296 | tf_op jit(solution)/shard_map/all_to_all | solution.py:418
  507.7 31.6 %collective-permute-start.41 = (bf16[4,64,2,1152]{3,2,1,0:T(2,128)(2,1)}, bf16[4,64,2,1152]{3,2,1,0:T(2,128)(2,1)}, u32[]{:S(2)}, u32[]{:S(2)}) collective-permute-start(bf16[4,64,2,1152]{3,2,1,0:T(2,128)(2,1)} %get-tuple-element.536.refs_0_), channel_id=1, source_target_pairs={{0,4},{4,0},{8,12},{12,8},{16,20},{20,16},{24,28},{28,24},{1,5},{5... | collective-permute-start | bytes 3538952 | tf_op jit(solution)/shard_map/ppermute | solution.py:34
  552.5 43.6 %collective-permute-start.49 = (bf16[8,72,1024]{2,1,0:T(8,128)(2,1)}, bf16[8,72,1024]{2,1,0:T(8,128)(2,1)}, u32[]{:S(2)}, u32[]{:S(2)}) collective-permute-start(bf16[8,72,1024]{2,1,0:T(8,128)(2,1)} %all-to-all-done.2.refs_0_), channel_id=1, source_target_pairs={{0,2},{1,3},{2,0},{3,1},{4,6},{5,7},{6,4},{7,5},{8,10},{9,11},{10,... | collective-permute-start | bytes 3538952 | tf_op jit(solution)/shard_map/ppermute | solution.py:34
  555.0 62.2 %collective-permute-start.54 = (bf16[8,72,1024]{2,1,0:T(8,128)(2,1)}, bf16[8,72,1024]{2,1,0:T(8,128)(2,1)}, u32[]{:S(2)}, u32[]{:S(2)}) collective-permute-start(bf16[8,72,1024]{2,1,0:T(8,128)(2,1)} %all-to-all-done.2.refs_0_), channel_id=1, source_target_pairs={{0,1},{1,0},{2,3},{3,2},{4,5},{5,4},{6,7},{7,6},{8,9},{9,8},{10,11... | collective-permute-start | bytes 3538952 | tf_op jit(solution)/shard_map/ppermute | solution.py:34
  557.5 38.6 %collective-permute-start.48 = (bf16[4,64,2,1152]{3,2,1,0:T(2,128)(2,1)}, bf16[4,64,2,1152]{3,2,1,0:T(2,128)(2,1)}, u32[]{:S(2)}, u32[]{:S(2)}) collective-permute-start(bf16[4,64,2,1152]{3,2,1,0:T(2,128)(2,1)} %get-tuple-element.382.refs_2_), channel_id=1, source_target_pairs={{0,4},{4,0},{8,12},{12,8},{16,20},{20,16},{24,28},{28,24},{1,5},{5... | collective-permute-start | bytes 3538952 | tf_op jit(solution)/shard_map/ppermute | solution.py:34
  557.6 41.2 %all-to-all-start.3 = ((bf16[8,72,1024]{2,1,0:T(8,128)(2,1)}), bf16[8,72,1024]{2,1,0:T(8,128)(2,1)S(1)}, u32[]{:S(2)}, u32[]{:S(2)}) async-start(bf16[8,72,1024]{2,1,0:T(8,128)(2,1)} %shard_map.430), calls=%async_computation.3 | async-start | bytes 2359296 | tf_op jit(solution)/shard_map/all_to_all | solution.py:418
  598.8 28.6 %collective-permute-start.51 = (bf16[8,72,1024]{2,1,0:T(8,128)(2,1)S(1)}, bf16[8,72,1024]{2,1,0:T(8,128)(2,1)S(1)}, u32[]{:S(2)}, u32[]{:S(2)}) collective-permute-start(bf16[8,72,1024]{2,1,0:T(8,128)(2,1)S(1)} %all-to-all-done.3.refs_0_), channel_id=1, source_target_pairs={{0,2},{1,3},{2,0},{3,1},{4,6},{5,7},{6,4},{7,5},{8,10},{9,11},{10,... | collective-permute-start | bytes 3538952 | tf_op jit(solution)/shard_map/ppermute | solution.py:34
  598.8 28.6 %collective-permute-start.53 = (bf16[8,72,1024]{2,1,0:T(8,128)(2,1)S(1)}, bf16[8,72,1024]{2,1,0:T(8,128)(2,1)}, u32[]{:S(2)}, u32[]{:S(2)}) collective-permute-start(bf16[8,72,1024]{2,1,0:T(8,128)(2,1)S(1)} %all-to-all-done.3.refs_0_), channel_id=1, source_target_pairs={{0,1},{1,0},{2,3},{3,2},{4,5},{5,4},{6,7},{7,6},{8,9},{9,8},{10,11... | collective-permute-start | bytes 3538952 | tf_op jit(solution)/shard_map/ppermute | solution.py:34
  (135 other events, 1249.6 us)
Sparse Core Ops, SparseCore 0:
  94.3 79.7 all-gather.5
  176.1 44.4 all-gather.9
  222.8 59.9 all-gather.7

commit v4 on v3

--- a/solution.py
+++ b/solution.py
@@ -48,6 +48,15 @@
 
 def bits_of(count):
     return [1 << place for place in range(count.bit_length() - 1)]
+
+
+def coordinates(index, devices):
+    return [(index >> place) & 1 for place in range(len(bits_of(devices)))]
+
+
+def gather_masks(devices):
+    places = list(reversed(range(len(bits_of(devices)))))
+    return [1 << place for place in places]
 
 
 RELATIVE = (0, 2, 1, 3)
@@ -358,7 +367,6 @@
     if half:
         in_specs += [pl.BlockSpec(memory_space=pl.ANY)] * 4
         aliases = {7 + index: index for index in range(4)}
-    work = 2 * rows * width * hidden * 2 * 6
     return pl.pallas_call(
         feed_body,
         grid=(steps,),
@@ -370,7 +378,7 @@
             vmem_limit_bytes=VMEM_BYTES, dimension_semantics=("arbitrary",)
         ),
         cost_estimate=pl.CostEstimate(
-            flops=work, bytes_accessed=12 * rows * width * 4, transcendentals=0
+            flops=1_000_000_000, bytes_accessed=1_000_000, transcendentals=0
         ),
     )(n_own, n_near, c_own, c_near, w_gate, w_up, w_down, *(kept if half else ()))
 
@@ -502,8 +510,8 @@
 
 def places_apart(count):
     apart = [0]
-    for step in reversed(bits_of(count)):
-        apart = apart + [other + step for other in apart]
+    for mask in gather_masks(count):
+        apart = apart + [other ^ mask for other in apart]
     return apart
 
 
@@ -614,35 +622,63 @@
         leaving[index] = total.astype(LOW)
 
 
-def pairs_of(count, stride):
-    return [(index, stride) for index in range(count) if not (index // stride) % 2]
-
-
 class Halving:
-    def __init__(self, product, device, devices, order):
-        rows = product.shape[0] // devices
+    def __init__(self, device, devices, order):
         self.device = device
-        self.left = list(reversed(range(len(bits_of(devices)))))
+        self.devices = devices
         self.order = list(order)
-        place, bit, stride = self.next()
-        split = product.reshape((-1, 2, stride, rows) + product.shape[1:])
-        shape = (devices // 2, rows) + product.shape[1:]
-        leaving = lax.dynamic_index_in_dim(split, 1 - bit, 1, keepdims=False).reshape(shape)
-        self.kept = lax.dynamic_index_in_dim(split, bit, 1, keepdims=False).reshape(shape)
+        self.left = list(range(len(self.order)))
+        self.stands = {tuple(coordinates(index, devices)): index for index in range(devices)}
+
+    def start(self, product):
+        rows = product.shape[0] // self.devices
+        place, bit, pairs = self.next()
+        shape = (self.devices // 2, rows) + product.shape[1:]
+        if all(pair == (2 * index, 1) for index, pair in enumerate(pairs)):
+            split = product.reshape((-1, 2, rows) + product.shape[1:])
+            leaving, self.kept = [
+                lax.dynamic_index_in_dim(split, side, 1, keepdims=False) for side in (1 - bit, bit)
+            ]
+        else:
+            runs = []
+            for base, stride in pairs:
+                if runs and runs[-1][0] + runs[-1][2] == base and runs[-1][1] == stride:
+                    runs[-1][2] += 1
+                else:
+                    runs.append([base, stride, 1])
+            leaving, self.kept = [
+                jnp.concatenate(
+                    [
+                        lax.dynamic_slice_in_dim(product, (base + side * stride) * rows, length * rows)
+                        for base, stride, length in runs
+                    ]
+                ).reshape(shape)
+                for side in (1 - bit, bit)
+            ]
         self.got = swap(leaving.astype(LOW), "dp", 1 << place)
+        return self
 
     def next(self):
         place = self.order.pop(0)
-        stride = 1 << (len(self.left) - 1 - self.left.index(place))
+        at = self.left.index(place)
         self.left.remove(place)
-        return place, (self.device >> place) & 1, stride
+        pairs, stands = [], {}
+        for bits in sorted(self.stands):
+            if not bits[at]:
+                first = self.stands[bits]
+                second = self.stands[bits[:at] + (1,) + bits[at + 1 :]]
+                stands[bits[:at] + bits[at + 1 :]] = len(pairs)
+                pairs.append((first, second - first))
+        order = sorted(range(len(pairs)), key=lambda index: pairs[index][0])
+        pairs = [pairs[index] for index in order]
+        self.stands = {bits: order.index(index) for bits, index in stands.items()}
+        return place, coordinates(self.device, self.devices)[place], pairs
 
     def go(self):
-        place, bit, stride = self.next()
-        count = self.kept.shape[0]
-        shape = (count // 2,) + self.kept.shape[1:]
+        place, bit, pairs = self.next()
+        shape = (len(pairs),) + self.kept.shape[1:]
         leaving, self.kept = pl.pallas_call(
-            functools.partial(halve_body, pairs_of(count, stride)),
+            functools.partial(halve_body, pairs),
             in_specs=[SMEM, VMEM, VMEM],
             out_specs=[VMEM, VMEM],
             out_shape=[jax.ShapeDtypeStruct(shape, LOW), jax.ShapeDtypeStruct(shape, FULL)],
@@ -669,15 +705,12 @@
 
 
 def small_halving(parts, device, devices, order):
-    self = Halving.__new__(Halving)
-    self.device = device
-    self.left = list(reversed(range(len(bits_of(devices)))))
-    self.order = list(order)
-    place, bit, stride = self.next()
+    self = Halving(device, devices, order)
+    place, bit, pairs = self.next()
     size = parts[0].shape[0] // devices
     shape = (devices // 2, size, parts[0].shape[1] + parts[2].shape[1])
     leaving, self.kept = pl.pallas_call(
-        functools.partial(small_body, pairs_of(devices, stride), size),
+        functools.partial(small_body, pairs, size),
         in_specs=[SMEM] + [VMEM] * 4,
         out_specs=[VMEM, VMEM],
         out_shape=[jax.ShapeDtypeStruct(shape, LOW), jax.ShapeDtypeStruct(shape, FULL)],
@@ -830,7 +863,8 @@
     norm_one_f, inv_one = row_norm(x_full, norm_gains[0])
     norm_own = norm_one_f.astype(LOW)
     norm_near = near(norm_own)
-    dims = (slot_rows, slot_pieces, part_rows, slot_rows // 6, head_dim, heads)
+    dims = (slot_rows, slot_pieces, part_rows, slot_rows // 4, head_dim, heads)
+    back_dims = dims[:3] + (slot_rows // 6,) + dims[4:]
     shape = jax.ShapeDtypeStruct
 
     def attend(last, weights, more):
@@ -866,8 +900,8 @@
             ],
             compiler_params=pltpu.CompilerParams(vmem_limit_bytes=VMEM_BYTES),
             cost_estimate=pl.CostEstimate(
-                flops=12_000_000_000 if last else 1_000_000_000,
-                bytes_accessed=12_000_000 if last else 1_000_000,
+                flops=1_000_000_000,
+                bytes_accessed=1_000_000,
                 transcendentals=0,
             ),
         )(*arguments)
@@ -894,7 +928,7 @@
             *tables,
         ) + more
         return pl.pallas_call(
-            functools.partial(attend_back_body, last, dims),
+            functools.partial(attend_back_body, last, back_dims),
             in_specs=[SMEM] + [VMEM] * (len(arguments) - 1),
             out_specs=[VMEM] * len(outs),
             out_shape=outs,
@@ -908,7 +942,7 @@
             ],
             compiler_params=pltpu.CompilerParams(vmem_limit_bytes=VMEM_BYTES),
             cost_estimate=pl.CostEstimate(
-                flops=20_000_000_000, bytes_accessed=14_000_000, transcendentals=0
+                flops=1_000_000_000, bytes_accessed=1_000_000, transcendentals=0
             ),
         )(*arguments)
 
@@ -942,8 +976,7 @@
     *kept, d_own, d_near, y_own, y_near = feed(
         0, (), two_own, two_near, c_own, c_near, w_gate, w_up, w_down
     )
-    stepped = fence(two_far, d_own, d_near, y_near, ahead_gateup)
-    two_far, d_own, d_near, y_near, ahead_gateup = stepped
+    two_far, d_own, d_near, y_near = fence(two_far, d_own, d_near, y_near)
     two_across = near(two_far)
     c_across = near(c_far)
     d_got = near(d_near)
@@ -951,23 +984,26 @@
     *kept, far_own, far_near, far_y_own, far_y_near = feed(
         1, kept, two_far, two_across, c_far, c_across, w_gate, w_up, w_down
     )
+    far_own, far_near, ahead_gateup = fence(far_own, far_near, ahead_gateup)
     far_got = near(far_near)
     pair_far = add(far_own, far_got).astype(LOW)
     pair_far, kept, far_y_near = fence(pair_far, kept, far_y_near)
     inner, d_both, two_all, c_all = kept
     pair_got = far(pair_far)
     far_y_got = near(far_y_near)
-    places = list(range(len(bits_of(devices))))
+    x_first = list(range(len(bits_of(devices))))
+    z_first = x_first[1:] + x_first[:1]
+    *masks, mask_one, mask_two, mask_three = gather_masks(devices)
     grad_both = dot(two_all, d_both, 0, 0).astype(LOW)
-    gate = Halving(grad_both[:, :hidden], device, devices, places[1:] + places[:1])
-    up = Halving(grad_both[:, hidden:], device, devices, places)
     grad_down = dot(c_all, inner, 0, 0).astype(LOW)
-    down = Halving(grad_down, device, devices, places)
     y_pair = add(y_own, y_got) + hidden_one
     far_y_pair = add(far_y_own, far_y_got)
     y_leaving = jnp.concatenate([y_pair[quarter_rows:], far_y_pair[:quarter_rows]]).astype(LOW)
-    stepped = fence(pair_got, y_leaving, down.kept, gate.kept, up.kept)
-    pair_got, y_leaving, down.kept, gate.kept, up.kept = stepped
+    stepped = fence(pair_got, y_leaving, grad_both, grad_down)
+    pair_got, y_leaving, grad_both, grad_down = stepped
+    gate = Halving(device, devices, z_first).start(grad_both[:, :hidden])
+    down = Halving(device, devices, x_first).start(grad_down)
+    up = Halving(device, devices, x_first).start(grad_both[:, hidden:])
     y_arrived = far(y_leaving)
 
     d_norm_two = add(d_own, d_got) + pair_got.astype(FULL)
@@ -980,22 +1016,25 @@
         return dot(own, values[:half_rows], 0, 0) + dot(other, values[half_rows:], 0, 0)
 
     d_raw_far, gains_far = attend_back(False, groups[1], second_kept, dh_own, dh_near, ())
-    stepped = fence(d_raw_far, down.got, gate.got, ahead_down, y_arrived)
-    d_raw_far, down.got, gate.got, ahead_down, y_arrived = stepped
+    d_raw_far, y_arrived = fence(d_raw_far, y_arrived)
+
+    out_order = (place_from + (slot_count - slot) * slot_pieces) % pieces_dev
+
+    def to_send(rows):
+        return pick(rows.reshape(pieces_dev, part_rows, width), out_order)
+
+    y_mine = y_pair[:quarter_rows] + y_arrived[quarter_rows:].astype(FULL)
+    y_other = far_y_pair[quarter_rows:] + y_arrived[:quarter_rows].astype(FULL)
+    out_sent = to_send(jnp.concatenate([y_mine, y_other], axis=0).astype(LOW))
+    out_sent, down.got, gate.got = fence(out_sent, down.got, gate.got)
+    out_got = across_dp(out_sent)
     gate.go()
     down.go()
-
-    out_order = (place_from + (slot_count - slot) * slot_pieces) % pieces_dev
-
-    def to_send(rows):
-        return pick(rows.reshape(pieces_dev, part_rows, width), out_order)
-
-    y_mine = y_pair[:quarter_rows] + y_arrived[quarter_rows:].astype(FULL)
-    y_other = far_y_pair[quarter_rows:] + y_arrived[:quarter_rows].astype(FULL)
-    out_rows = jnp.concatenate([y_mine, y_other], axis=0).astype(LOW)
+    stepped = fence(gate.kept, down.kept, d_raw_far, dh_own)
+    gate.kept, down.kept, d_raw_far, dh_own = stepped
     grad_output_got = far(over_rows(dh_own, dh_near, second_kept[0]).astype(LOW))
     grad_qkv_got = far(over_rows(norm_own, norm_near, d_raw_far).astype(LOW))
-    grad_output_mine = over_rows(dh_own, dh_near, first_kept[0])
+    grad_output_mine = over_rows(dh_own, dh_near, first_kept[0]).astype(LOW)
     d_raw_own, gains_own, d_one_own, d_one_near = attend_back(
         True,
         groups[0],
@@ -1005,72 +1044,77 @@
         (groups[0][0], groups[0][1], groups[1][0], groups[1][1], d_raw_far),
     )
     stepped = fence(
-        (d_raw_own, d_one_near, down.got, gate.got, up.got), out_rows, grad_output_got, ahead_small
-    )
-    (d_raw_own, d_one_near, down.got, gate.got, up.got), *stepped = stepped
-    out_rows, grad_output_got, ahead_small = stepped
+        (d_raw_own, d_one_near, down.got, gate.got, up.got, out_got),
+        (grad_output_got, grad_qkv_got, grad_output_mine, ahead_small, ahead_down),
+    )
+    d_raw_own, d_one_near, down.got, gate.got, up.got, out_got = stepped[0]
+    grad_output_got, grad_qkv_got, grad_output_mine, ahead_small, ahead_down = stepped[1]
 
     d_one_got = near(d_one_near)
     down.go()
     gate.go()
     up.go()
-    stepped = fence(d_one_got, down.kept, gate.kept, up.kept, d_raw_own, out_rows)
-    d_one_got, down.kept, gate.kept, up.kept, d_raw_own, out_rows = stepped
+    stepped = fence(d_one_got, down.kept, gate.kept, up.kept, d_raw_own)
+    d_one_got, down.kept, gate.kept, up.kept, d_raw_own = stepped
     d_norm_one = add(d_one_own, d_one_got)
     d_input_part, gain_one = row_norm_back(d_norm_one, x_full, inv_one, norm_gains[0])
     dx_own = (d_hidden + d_input_part).astype(LOW)
-    stepped = fence(dx_own, up.got, down.got, gate.got, out_rows)
-    dx_own, up.got, down.got, gate.got, out_rows = stepped
+    dx_own, up.got, down.got, gate.got = fence(dx_own, up.got, down.got, gate.got)
 
     def grown(held, got):
         return jnp.concatenate([held, got], axis=0)
 
     def first_steps(own):
         held = own.astype(LOW)[None]
-        for bit in reversed(bits_of(devices)[3:]):
-            held = grown(held, swap(held, "dp", bit))
+        for mask in masks:
+            held = grown(held, swap(held, "dp", mask))
         return held
 
     dx_other = far(dx_own[quarter_rows:])
     up.go()
+    up.kept, down.kept, gate.kept, d_raw_own = fence(up.kept, down.kept, gate.kept, d_raw_own)
     own_down = down.own()
     owned_down = own_down.T
     held_down = first_steps(owned_down)
-    down_more = swap(held_down, "dp", 4)
+    down_more = swap(held_down, "dp", mask_one)
     own_gate = gate.own()
     grad_qkv_mine = over_rows(norm_own, norm_near, d_raw_own).astype(LOW)
     small_parts = (grad_qkv_mine, grad_qkv_got, grad_output_mine, grad_output_got)
-    rest = small_halving(small_parts, device, devices, places)
-    stepped = fence(up.got, rest.got, dx_own, dx_other, down_more, own_gate, out_rows)
-    up.got, rest.got, dx_own, dx_other, down_more, own_gate, out_rows = stepped
+    rest = small_halving(small_parts, device, devices, x_first)
+    stepped = fence(up.got, rest.got, dx_own, dx_other, down_more, own_gate, out_got)
+    up.got, rest.got, dx_own, dx_other, down_more, own_gate, out_got = stepped
 
     own_up = up.own()
     owned_gateup = jnp.stack([own_gate, own_up], axis=1)
-    held_gateup = first_steps(row_major(owned_gateup.astype(LOW)))
-    gateup_more = swap(held_gateup, "dp", 4)
+    low_gateup = row_major(owned_gateup.astype(LOW))
+    half_shard = low_gateup.shape[0] // 2
+    held_lower = first_steps(low_gateup[:half_shard])
+    held_upper = first_steps(low_gateup[half_shard:])
+    lower_more = swap(held_lower, "dp", mask_one)
     rest.go()
     held_down = grown(held_down, down_more)
-    down_more = swap(held_down, "dp", 2)
+    down_more = swap(held_down, "dp", mask_two)
     dx_sent = to_send(jnp.concatenate([dx_own[:quarter_rows], dx_other], axis=0))
-    out_sent = to_send(out_rows)
-    stepped = fence(rest.got, down_more, gateup_more, dx_sent, out_sent)
-    rest.got, down_more, gateup_more, dx_sent, out_sent = stepped
-
-    held_gateup = grown(held_gateup, gateup_more)
-    gateup_more = swap(held_gateup, "dp", 2)
+    stepped = fence(rest.got, down_more, lower_more, held_upper, dx_sent)
+    rest.got, down_more, lower_more, held_upper, dx_sent = stepped
+
+    upper_more = swap(held_upper, "dp", mask_one)
+    held_lower = grown(held_lower, lower_more)
+    lower_more = swap(held_lower, "dp", mask_two)
     held_down = grown(held_down, down_more)
-    down_more = swap(held_down, "dp", 1)
+    down_more = swap(held_down, "dp", mask_three)
     rest.go()
-    rest.got, down_more, gateup_more, out_sent = fence(rest.got, down_more, gateup_more, out_sent)
-
-    held_gateup = grown(held_gateup, gateup_more)
-    half_shard = held_gateup.shape[1] // 2
-    held_lower, held_upper = held_gateup[:, :half_shard], held_gateup[:, half_shard:]
-    lower_more = swap(held_lower, "dp", 1)
-    out_got = across_dp(out_sent)
+    out_far = far(out_got)
+    rest.got, lower_more, upper_more = fence(rest.got, lower_more, upper_more)
+
+    held_lower = grown(held_lower, lower_more)
+    lower_more = swap(held_lower, "dp", mask_three)
+    held_upper = grown(held_upper, upper_more)
+    upper_more = swap(held_upper, "dp", mask_two)
+    dx_got = across_dp(dx_sent)
     own_small = rest.own()
     held_small = first_steps(own_small)
-    small_more = swap(held_small, "dp", 4)
+    small_more = swap(held_small, "dp", mask_one)
     owned = (own_small, own_gate, own_up, own_down)
     own_square = sum([jnp.sum(part_grad * part_grad) for part_grad in owned])
     gains = jnp.sum((gains_far + gains_own).reshape(2, 8, LANES // head_dim, head_dim), axis=(1, 2))
@@ -1079,20 +1123,22 @@
     ).reshape(-1, LANES)
     for bit in bits_of(ways):
         packed = packed + swap(packed, "mp", bit)
-    stepped = fence(lower_more, out_got, small_more, own_small, held_upper, dx_sent, packed)
-    lower_more, out_got, small_more, own_small, held_upper, dx_sent, packed = stepped
-
-    for bit in bits_of(devices):
+    output = place_pieces((out_got, out_far, near(out_got), near(out_far)), target, member_ref)
+    stepped = fence(
+        (lower_more, upper_more, down_more, small_more), dx_got, packed, own_small, output
+    )
+    (lower_more, upper_more, down_more, small_more), dx_got, packed, own_small, output = stepped
+    packed = packed + swap(packed, "dp", 1)
+    stepped = fence(held_upper, held_small, dx_got, packed, upper_more, small_more)
+    held_upper, held_small, dx_got, packed, upper_more, small_more = stepped
+    held_upper = grown(held_upper, upper_more)
+    upper_more = swap(held_upper, "dp", mask_three)
+    dx_far = far(dx_got)
+    for bit in bits_of(devices)[1:]:
         packed = packed + swap(packed, "dp", bit)
-    stepped = fence(held_upper, dx_sent, out_got, small_more, packed)
-    held_upper, dx_sent, out_got, small_more, packed = stepped
-    upper_more = swap(held_upper, "dp", 1)
-    dx_got = across_dp(dx_sent)
-    out_far = far(out_got)
+    packed, held_small, small_more = fence(packed, held_small, small_more)
     held_small = grown(held_small, small_more)
-    small_more = swap(held_small, "dp", 2)
-    upper_more, dx_got, out_far, small_more = fence(upper_more, dx_got, out_far, small_more)
-    dx_far = far(dx_got)
+    small_more = swap(held_small, "dp", mask_two)
 
     flat = packed.reshape(-1)
     norm_sum = flat[: 2 * width].reshape(2, width)
@@ -1102,9 +1148,6 @@
     limit = math.sqrt(2 * D * H * HD + 2 * D * KV * HD + 3 * D * FF + 2 * D + 2 * HD)
     factor = jnp.minimum(1.0, limit / clip_value)
 
-    held_small = grown(held_small, small_more)
-    small_more = swap(held_small, "dp", 1)
-
     qkv_cols = query_cols + 2 * key_cols
     owned_parts = (
         own_small[:, :query_cols],
@@ -1121,17 +1164,18 @@
     next_heads = head_gains - step * moment_heads
 
     pull = (step * factor).reshape(1)
-    output = place_pieces((out_got, out_far, near(out_got), near(out_far)), target, member_ref)
     device_ref = device.reshape(1).astype(jnp.int32)
+    done_down = finish_down(device_ref, pull, ahead_down, held_down, down_more)
+    dx_far, done_down, small_more = fence(dx_far, done_down, small_more)
+    held_small = grown(held_small, small_more)
+    small_more = swap(held_small, "dp", mask_three)
+    input_grad = place_pieces((dx_got, dx_far, near(dx_got), near(dx_far)), target, member_ref)
+    upper_more, input_grad = fence(upper_more, input_grad)
     all_gateup = place_shards(
         device_ref, devices, (held_lower, lower_more), (held_upper, upper_more)
     ).reshape(ahead_gateup.shape)
     done_gateup = (ahead_gateup.astype(FULL) - pull[0] * all_gateup.astype(FULL)).astype(LOW)
-    done_down = finish_down(device_ref, pull, ahead_down, held_down, down_more)
-    near_got = near(dx_got)
-    stepped = fence(dx_far, small_more, near_got, output, done_gateup, done_down, moments, nexts)
-    dx_far, small_more, near_got, output, done_gateup, done_down, moments, nexts = stepped
-    input_grad = place_pieces((dx_got, dx_far, near_got, near(dx_far)), target, member_ref)
+    small_more, done_gateup = fence(small_more, done_gateup)
     done_query, done_keyval, done_output = finish_small(
         device_ref, pull, ahead_small, held_small, small_more, query_cols, qkv_cols
     )

time: 662 us -> 642 us (0.970)
  waiting for transfers between devices: 159 us -> 116 us
  local copies, waits for them, and re-layouts: 57.3 us -> 68.1 us
  other arithmetic: 86.9 us -> 95.9 us
  starting transfers between devices: 74.7 us -> 81.6 us
    ppermute x57 -> x59, waiting for transfers between devices: 140 us -> 116 us  [swap(): lax.ppermute(values, axis, [(place, place ^ bit) for place in range(size)])]
    all_gather x1, waiting for transfers between devices: 8.24 us -> 0.02 us  [local(): ahead_gateup = lax.all_gather(part_gateup, 'dp', axis=0, tiled=True)]
    all_gather x1, waiting for transfers between devices: 7.47 us -> 0.01 us  [local(): ahead_down = lax.all_gather(part_down, 'dp', axis=0, tiled=False)]
    ppermute x57 -> x59, starting transfers between devices: 50.4 us -> 57.2 us  [swap(): lax.ppermute(values, axis, [(place, place ^ bit) for place in range(size)])]
    unnamed x210 -> x190, local copies, waits for them, and re-layouts: 13.3 us -> 15.3 us
  transfers between devices with their start and end apart: 64 -> 66, of which waited for: 24 -> 19; matrix products, arithmetic and copies ran while one was open for 26% -> 30% of each run, Pallas kernels for 30% -> 30%
where the time goes in v4:
time: 642 us; the launch traced here: 632 us
  Pallas kernels  208 us (32%)
  waiting for transfers between devices  116 us (18%)
  other arithmetic  95.9 us (15%)
  starting transfers between devices  81.6 us (13%)
  local copies, waits for them, and re-layouts  68.1 us (11%)
  matrix products  40.3 us (6%)
  between operations  21.9 us (3%)
    ppermute x59, waiting for transfers between devices, swap(): lax.ppermute(values, axis, [(place, place ^ bit) for place in range(size)])  116 us
    ppermute x59, starting transfers between devices, swap(): lax.ppermute(values, axis, [(place, place ^ bit) for place in range(size)])  57.2 us
    pallas_call x2, Pallas kernels, feed(): pl.pallas_call(feed_body, grid=(steps,), in_specs=in_specs, out_specs=out...  53.8 us
    pallas_call x2, Pallas kernels, attend_back(): pl.pallas_call(functools.partial(attend_back_body, last, back_dims), in_s...  44.6 us
    dot_general x10, matrix products, dot(): lax.dot_general(left, right, (((left_dim,), (right_dim,)), ((), ())), pre...  40.3 us
    pallas_call x2, Pallas kernels, attend(): pl.pallas_call(functools.partial(attend_body, last, dims), in_specs=[SMEM...  28.4 us
    all_to_all x4, starting transfers between devices, across_dp(): return lax.all_to_all(values, 'dp', split_axis=0, concat_axis=0, tiled=True)  23.6 us
    pallas_call x8, Pallas kernels, go(): pl.pallas_call(functools.partial(halve_body, pairs), in_specs=[SMEM, VMEM...  21.6 us
  transfers between devices with their start and end apart: 66, of which 19 were waited for; matrix products, arithmetic and copies ran while one was open for 30% of the time, Pallas kernels for 30%

profile of v4, /device:TPU:0, one launch (start us, length us, event | category | flops | bytes accessed | tf_op | source)
XLA Modules:
  0.0 631.7 jit_solution(17943302008935860073)
XLA Ops:
  12.2 7.4 %all-to-all-start = ((bf16[8,72,1024]{2,1,0:T(8,128)(2,1)}), bf16[8,72,1024]{2,1,0:T(8,128)(2,1)S(1)}, u32[]{:S(2)}, u32[]{:S(2)}) async-start(bf16[8,72,1024]{2,1,0:T(8,128)(2,1)} %shard_map.408), calls=%async_computation | async-start | bytes 2359296 | tf_op jit(solution)/shard_map/all_to_all | solution.py:426
  22.5 10.5 %fusion.37 = (bf16[1024,1,1152]{2,1,0:T(2,128)(2,1)}, bf16[1024,1,1152]{2,1,0:T(2,128)(2,1)}) fusion(bf16[1024,2,1152]{2,1,0:T(2,128)(2,1)} %param.32), kind=kLoop, calls=%fused_computation.172 | loop fusion | bytes 9437184 | tf_op jit(solution)/shard_map/slice | solution.py:835
  35.4 6.8 %copy_bitcast_fusion = (bf16[1024,1152]{1,0:T(8,128)(2,1)}, bf16[1024,1152]{1,0:T(8,128)(2,1)}) fusion(bf16[1024,1,1152]{2,1,0:T(2,128)(2,1)} %get-tuple-element.535, bf16[1024,1,1152]{2,1,0:T(2,128)(2,1)} %get-tuple-element.536), kind=kLoop, calls=%fused_computation.5 | loop fusion | bytes 9437184 | tf_op jit(solution)/shard_map/squeeze | solution.py:835
  59.6 6.1 all-to-all-start.1
  83.3 13.3 %shard_map.411 = (bf16[1152,256]{1,0:T(8,128)(2,1)}, bf16[1152,384]{1,0:T(8,128)(2,1)}, f32[2,1152,128]{2,1,0:T(8,128)}, bf16[2,1152,128]{2,1,0:T(8,128)(2,1)}, ...) custom-call(s32[1]{0:T(128)} %bitcast.1.refs_0_.member, ...), custom_call_target="tpu_custom_call" | custom-call | flops 1000000000 | bytes 1000000 | tf_op jit(solution)/shard_map/pallas_call | solution.py:891
  103.6 15.1 %shard_map.415 = (bf16[1152,256]{1,0:T(8,128)(2,1)}, bf16[1152,384]{1,0:T(8,128)(2,1)}, f32[2,1152,128]{2,1,0:T(8,128)}, bf16[2,1152,128]{2,1,0:T(8,128)(2,1)}, ...) custom-call(s32[1]{0:T(128)} %bitcast.1.refs_0_.member, ...), custom_call_target="tpu_custom_call" | custom-call | flops 1000000000 | bytes 1000000 | tf_op jit(solution)/shard_map/pallas_call | solution.py:891
  130.5 4.3 collective-permute-done.7.first
  141.1 26.9 %shard_map.417 = (bf16[2304,1152]{1,0:T(8,128)(2,1)}, bf16[2304,2304]{1,0:T(8,128)(2,1)}, bf16[2304,1024]{1,0:T(8,128)(2,1)}, bf16[2304,1024]{1,0:T(8,128)(2,1)}...) custom-call(bf16[576,1024]{1,0:T(8,128)(2,1)} %multiply_convert_fusi, ...), custom_call_target="tpu_custom_call" | custom-call | flops 1000000000 | bytes 1000000 | tf_op jit(solution)/shard_map/pallas_call | solution.py:370
  171.4 26.9 %shard_map.419 = (bf16[2304,1152]{1,0:T(8,128)(2,1)}, bf16[2304,2304]{1,0:T(8,128)(2,1)}, bf16[2304,1024]{1,0:T(8,128)(2,1)}, bf16[2304,1024]{1,0:T(8,128)(2,1)}...) custom-call(bf16[576,1024]{1,0:T(8,128)(2,1)} %collective-permute-do, ...), custom_call_target="tpu_custom_call", output_to_operand_aliasing={{0}: (7, {}), {1}: (8, {}), {2}: (9, {}), {3}: (10, {})} | custom-call | flops 1000000000 | bytes 1000000 | tf_op jit(solution)/shard_map/pallas_call | solution.py:370
  206.5 14.3 %convolution_convert_fusion = bf16[1024,2304]{1,0:T(8,128)(2,1)S(1)} fusion(bf16[2304,1024]{1,0:T(8,128)(2,1)} %get-tuple-element.291, bf16[2304,2304]{1,0:T(8,128)(2,1)S(1)} %copy-done.3), kind=kOutput, calls=%fused_computation.3 | convolution fusion | flops 10873995264 | bytes 20054016 | tf_op jit(solution)/shard_map/dot_general | solution.py:27
  220.8 7.0 %convolution_convert_fusion.1 = bf16[1024,1152]{1,0:T(8,128)(2,1)S(1)} fusion(bf16[2304,1024]{1,0:T(8,128)(2,1)S(1)} %bitcast.137, bf16[2304,1152]{1,0:T(8,128)(2,1)S(1)} %bitcast.135), kind=kOutput, calls=%fused_computation.4 | convolution fusion | flops 5436997632 | bytes 12386304 | tf_op jit(solution)/shard_map/dot_general | solution.py:27
  237.5 4.1 fusion.35
  255.0 20.6 %shard_map.420 = (bf16[1152,512]{1,0:T(8,128)(2,1)}, f32[16,128]{1,0:T(8,128)}) custom-call(s32[1]{0:T(128)} %bitcast.1.refs_0_.member, bf16[576,1024]{1,0:T(8,128)(2,1)} %get-tuple-element.316.refs_1_, bf16[576,1024]{1,0:T(8,128)(2,1)} %collective-permute-done.18.refs_2_, bf16[256,1024]{1,0:T(8,128)(2,1)} %collective-permute-done.4.refs_10_.refs_3_, ...), custom_call_target="tpu_custom_call" | custom-call | flops 1000000000 | bytes 1000000 | tf_op jit(solution)/shard_map/pallas_call | solution.py:930
  281.9 9.9 %collective-permute-done.21.got = bf16[4,128,1152]{2,1,0:T(8,128)(2,1)} collective-permute-done((bf16[4,128,1152]{2,1,0:T(8,128)(2,1)}, bf16[4,128,1152]{2,1,0:T(8,128)(2,1)}, u32[]{:S(2)}, u32[]{:S(2)}) %collective-permute-start.21) | collective-permute-done | bytes 1179680 | tf_op jit(solution)/shard_map/ppermute | solution.py:34
  291.8 5.7 all-to-all-start.2
  321.3 24.0 %shard_map.424 = (bf16[1152,512]{1,0:T(8,128)(2,1)}, f32[16,128]{1,0:T(8,128)}, bf16[576,1024]{1,0:T(8,128)(2,1)}, bf16[576,1024]{1,0:T(8,128)(2,1)}) custom-call(s32[1]{0:T(128)} %bitcast.1.refs_0_.member, bf16[576,1024]{1,0:T(8,128)(2,1)} %get-tuple-element.316.refs_1_, bf16[576,1024]{1,0:T(8,128)(2,1)} %collective-permute-done.18.refs_2_, ...), custom_call_target="tpu_custom_call" | custom-call | flops 1000000000 | bytes 1000000 | tf_op jit(solution)/shard_map/pallas_call | solution.py:930
  364.7 4.0 multiply_reduce_fusion.1
  371.8 7.2 %collective-permute-done.29 = bf16[1,128,1152]{1,2,0:T(8,128)(2,1)} collective-permute-done((bf16[1,128,1152]{1,2,0:T(8,128)(2,1)}, bf16[1,128,1152]{1,2,0:T(8,128)(2,1)}, u32[]{:S(2)}, u32[]{:S(2)}) %collective-permute-start.29) | collective-permute-done | bytes 294944 | tf_op jit(solution)/shard_map/ppermute | solution.py:34
  398.5 22.0 %collective-permute-done.34 = bf16[1,1152,128]{2,1,0:T(8,128)(2,1)S(1)} collective-permute-done((bf16[1,1152,128]{2,1,0:T(8,128)(2,1)S(1)}, bf16[1,1152,128]{2,1,0:T(8,128)(2,1)S(1)}, u32[]{:S(2)}, u32[]{:S(2)}) %collective-permute-start.34) | collective-permute-done | bytes 294944 | tf_op jit(solution)/shard_map/ppermute | solution.py:34
  420.4 12.5 %collective-permute-done.31 = bf16[1,128,1152]{2,0,1:T(2,128)(2,1)S(1)} collective-permute-done((bf16[1,128,1152]{2,0,1:T(2,128)(2,1)S(1)}, bf16[1,128,1152]{2,0,1:T(2,128)(2,1)S(1)}, u32[]{:S(2)}, u32[]{:S(2)}) %collective-permute-start.31) | collective-permute-done | bytes 294944 | tf_op jit(solution)/shard_map/ppermute | solution.py:34
  455.3 8.7 %collective-permute-done.37 = bf16[1,64,2,1152]{3,2,1,0:T(2,128)(2,1)} collective-permute-done((bf16[1,64,2,1152]{3,2,1,0:T(2,128)(2,1)}, bf16[1,64,2,1152]{3,2,1,0:T(2,128)(2,1)}, u32[]{:S(2)}, u32[]{:S(2)}) %collective-permute-start.37) | collective-permute-done | bytes 294944 | tf_op jit(solution)/shard_map/ppermute | solution.py:34
  478.2 4.4 all-to-all-start.3
  483.5 5.0 collective-permute-done.38
  489.3 11.8 %collective-permute-done.40 = bf16[1,64,2,1152]{3,2,1,0:T(2,128)(2,1)} collective-permute-done((bf16[1,64,2,1152]{3,2,1,0:T(2,128)(2,1)}, bf16[1,64,2,1152]{3,2,1,0:T(2,128)(2,1)}, u32[]{:S(2)}, u32[]{:S(2)}) %collective-permute-start.40) | collective-permute-done | bytes 294944 | tf_op jit(solution)/shard_map/ppermute | solution.py:34
  523.9 5.7 shard_map.433
  533.6 5.7 collective-permute-done.42
  539.3 9.4 %collective-permute-done.41.refs_1_ = bf16[4,64,2,1152]{3,2,1,0:T(2,128)(2,1)} collective-permute-done((bf16[4,64,2,1152]{3,2,1,0:T(2,128)(2,1)}, bf16[4,64,2,1152]{3,2,1,0:T(2,128)(2,1)}, u32[]{:S(2)}, u32[]{:S(2)}) %collective-permute-start.41) | collective-permute-done | bytes 1179680 | tf_op jit(solution)/shard_map/ppermute | solution.py:34
  568.3 5.6 shard_map.434
  593.3 5.5 shard_map.435
  598.9 4.7 shard_map.436
  607.2 9.2 %fusion = bf16[1024,2,1152]{2,1,0:T(2,128)(2,1)} fusion(f32[8,128,2,1152]{3,2,1,0:T(2,128)S(1)} %bitcast.130, bf16[1024,2,1152]{2,1,0:T(2,128)(2,1)S(1)} %bitcast.151), kind=kLoop, calls=%fused_computation.1 | loop fusion | flops 7077888 | bytes 18874368 | tf_op jit(solution)/shard_map/convert_element_type | solution.py:1177
  617.3 4.5 shard_map.437
  (460 shorter events, 281.1 us)
Async XLA Ops:
  12.2 38.9 %all-to-all-start = ((bf16[8,72,1024]{2,1,0:T(8,128)(2,1)}), bf16[8,72,1024]{2,1,0:T(8,128)(2,1)S(1)}, u32[]{:S(2)}, u32[]{:S(2)}) async-start(bf16[8,72,1024]{2,1,0:T(8,128)(2,1)} %shard_map.408), calls=%async_computation | async-start | bytes 2359296 | tf_op jit(solution)/shard_map/all_to_all | solution.py:426
  19.7 31.3 %collective-permute-start.1 = (bf16[1024,256]{1,0:T(8,128)(2,1)S(1)}, bf16[1024,256]{1,0:T(8,128)(2,1)S(1)}, u32[]{:S(2)}, u32[]{:S(2)}) collective-permute-start(bf16[1024,256]{1,0:T(8,128)(2,1)S(1)} %bitcast.140), channel_id=1, source_target_pairs={{0,2},{1,3},{2,0},{3,1},{4,6},{5,7},{6,4},{7,5},{8,10},{9,11},{10,... | collective-permute-start | bytes 1572872 | tf_op jit(solution)/shard_map/ppermute | solution.py:34
  21.3 29.8 %collective-permute-start = (bf16[1024,256]{1,0:T(8,128)(2,1)S(1)}, bf16[1024,256]{1,0:T(8,128)(2,1)S(1)}, u32[]{:S(2)}, u32[]{:S(2)}) collective-permute-start(bf16[1024,256]{1,0:T(8,128)(2,1)S(1)} %copy-done.25), channel_id=1, source_target_pairs={{0,2},{1,3},{2,0},{3,1},{4,6},{5,7},{6,4},{7,5},{8,10},{9,11},{10,... | collective-permute-start | bytes 1572872 | tf_op jit(solution)/shard_map/ppermute | solution.py:34
  59.6 37.0 %all-to-all-start.1 = ((bf16[8,72,1024]{2,1,0:T(8,128)(2,1)}), bf16[8,72,1024]{2,1,0:T(8,128)(2,1)S(1)}, u32[]{:S(2)}, u32[]{:S(2)}) async-start(bf16[8,72,1024]{2,1,0:T(8,128)(2,1)} %shard_map.412), calls=%async_computation.1 | async-start | bytes 2359296 | tf_op jit(solution)/shard_map/all_to_all | solution.py:426
  65.8 132.6 %all-gather.6.cloned.1.call-start = ((), (), s32[]{:S(2)}) async-start(), calls=%async_computation.4 | async-start | bytes 5308416 | tf_op jit(solution)/shard_map/all_gather | solution.py:956
  96.7 153.3 %all-gather.8.cloned.1.call-start = ((), (), s32[]{:S(2)}) async-start(), calls=%async_computation.5 | async-start | bytes 1769472 | tf_op jit(solution)/shard_map/all_gather | solution.py:958
  135.4 32.7 %collective-permute-start.8 = (bf16[576,1024]{1,0:T(8,128)(2,1)}, bf16[576,1024]{1,0:T(8,128)(2,1)}, u32[]{:S(2)}, u32[]{:S(2)}) collective-permute-start(bf16[576,1024]{1,0:T(8,128)(2,1)} %multiply_convert_fusion.n_own), channel_id=1, source_target_pairs={{0,2},{1,3},{2,0},{3,1},{4,6},{5,7},{6,4},{7,5},{8,10},{9,11},{10,... | collective-permute-start | bytes 3538952 | tf_op jit(solution)/shard_map/ppermute | solution.py:34
  136.9 213.1 %all-gather.10.cloned.1.call-start = ((), (), s32[]{:S(2)}) async-start(), calls=%async_computation.6 | async-start | bytes 2654208 | tf_op jit(solution)/shard_map/all_gather | solution.py:957
  168.6 31.0 %collective-permute-start.15 = (bf16[576,1024]{1,0:T(8,128)(2,1)}, bf16[576,1024]{1,0:T(8,128)(2,1)}, u32[]{:S(2)}, u32[]{:S(2)}) collective-permute-start(bf16[576,1024]{1,0:T(8,128)(2,1)} %get-tuple-element.288), channel_id=1, source_target_pairs={{0,1},{1,0},{2,3},{3,2},{4,5},{5,4},{6,7},{7,6},{8,9},{9,8},{10,11... | collective-permute-start | bytes 3538952 | tf_op jit(solution)/shard_map/ppermute | solution.py:34
  199.4 36.5 %collective-permute-start.17 = (bf16[576,1024]{1,0:T(8,128)(2,1)}, bf16[576,1024]{1,0:T(8,128)(2,1)S(1)}, u32[]{:S(2)}, u32[]{:S(2)}) collective-permute-start(bf16[576,1024]{1,0:T(8,128)(2,1)} %get-tuple-element.297), channel_id=1, source_target_pairs={{0,1},{1,0},{2,3},{3,2},{4,5},{5,4},{6,7},{7,6},{8,9},{9,8},{10,11... | collective-permute-start | bytes 3538952 | tf_op jit(solution)/shard_map/ppermute | solution.py:34
  206.1 28.0 %collective-permute-start.14 = (bf16[576,1024]{1,0:T(8,128)(2,1)S(1)}, bf16[576,1024]{1,0:T(8,128)(2,1)S(1)}, u32[]{:S(2)}, u32[]{:S(2)}) collective-permute-start(bf16[576,1024]{1,0:T(8,128)(2,1)S(1)} %add_convert_fusion.1), channel_id=1, source_target_pairs={{0,2},{1,3},{2,0},{3,1},{4,6},{5,7},{6,4},{7,5},{8,10},{9,11},{10,... | collective-permute-start | bytes 3538952 | tf_op jit(solution)/shard_map/ppermute | solution.py:34
  241.6 34.0 %collective-permute-start.19 = (bf16[576,1024]{1,0:T(8,128)(2,1)}, bf16[576,1024]{1,0:T(8,128)(2,1)}, u32[]{:S(2)}, u32[]{:S(2)}) collective-permute-start(bf16[576,1024]{1,0:T(8,128)(2,1)} %pad_maximum_fusion), channel_id=1, source_target_pairs={{0,2},{1,3},{2,0},{3,1},{4,6},{5,7},{6,4},{7,5},{8,10},{9,11},{10,... | collective-permute-start | bytes 3538952 | tf_op jit(solution)/shard_map/ppermute | solution.py:34
  244.4 47.4 %collective-permute-start.21 = (bf16[4,128,1152]{2,1,0:T(8,128)(2,1)}, bf16[4,128,1152]{2,1,0:T(8,128)(2,1)}, u32[]{:S(2)}, u32[]{:S(2)}) collective-permute-start(bf16[4,128,1152]{2,1,0:T(8,128)(2,1)} %bitcast.25), channel_id=1, source_target_pairs={{0,8},{4,12},{8,0},{12,4},{16,24},{20,28},{24,16},{28,20},{1,9},{5... | collective-permute-start | bytes 3538952 | tf_op jit(solution)/shard_map/ppermute | solution.py:34
  247.9 43.9 %collective-permute-start.20 = (bf16[4,128,1152]{2,1,0:T(8,128)(2,1)}, bf16[4,128,1152]{2,1,0:T(8,128)(2,1)}, u32[]{:S(2)}, u32[]{:S(2)}) collective-permute-start(bf16[4,128,1152]{2,1,0:T(8,128)(2,1)} %get-tuple-element.540), channel_id=1, source_target_pairs={{0,4},{4,0},{8,12},{12,8},{16,20},{20,16},{24,28},{28,24},{1,5},{5... | collective-permute-start | bytes 3538952 | tf_op jit(solution)/shard_map/ppermute | solution.py:34
  254.5 95.5 %collective-permute-start.24 = (bf16[4,128,1152]{2,1,0:T(8,128)(2,1)}, bf16[4,128,1152]{2,1,0:T(8,128)(2,1)}, u32[]{:S(2)}, u32[]{:S(2)}) collective-permute-start(bf16[4,128,1152]{2,1,0:T(8,128)(2,1)} %get-tuple-element.538), channel_id=1, source_target_pairs={{0,4},{4,0},{8,12},{12,8},{16,20},{20,16},{24,28},{28,24},{1,5},{5... | collective-permute-start | bytes 3538952 | tf_op jit(solution)/shard_map/ppermute | solution.py:34
  291.8 59.4 %all-to-all-start.2 = ((bf16[8,72,1024]{2,1,0:T(8,128)(2,1)}), bf16[8,72,1024]{2,1,0:T(8,128)(2,1)S(1)}, u32[]{:S(2)}, u32[]{:S(2)}) async-start(bf16[8,72,1024]{2,1,0:T(8,128)(2,1)} %shard_map.421), calls=%async_computation.2 | async-start | bytes 2359296 | tf_op jit(solution)/shard_map/all_to_all | solution.py:426
  310.3 40.9 %collective-permute-start.26 = (bf16[1024,512]{1,0:T(8,128)(2,1)}, bf16[1024,512]{1,0:T(8,128)(2,1)}, u32[]{:S(2)}, u32[]{:S(2)}) collective-permute-start(bf16[1024,512]{1,0:T(8,128)(2,1)} %add_convert_fusion.3), channel_id=1, source_target_pairs={{0,2},{1,3},{2,0},{3,1},{4,6},{5,7},{6,4},{7,5},{8,10},{9,11},{10,... | collective-permute-start | bytes 3145736 | tf_op jit(solution)/shard_map/ppermute | solution.py:34
  316.5 33.5 %collective-permute-start.25 = (bf16[1024,256]{1,0:T(8,128)(2,1)}, bf16[1024,256]{1,0:T(8,128)(2,1)}, u32[]{:S(2)}, u32[]{:S(2)}) collective-permute-start(bf16[1024,256]{1,0:T(8,128)(2,1)} %fusion.2), channel_id=1, source_target_pairs={{0,2},{1,3},{2,0},{3,1},{4,6},{5,7},{6,4},{7,5},{8,10},{9,11},{10,... | collective-permute-start | bytes 1572872 | tf_op jit(solution)/shard_map/ppermute | solution.py:34
  316.9 33.1 %collective-permute-start.22 = (bf16[2,128,1152]{2,1,0:T(8,128)(2,1)}, bf16[2,128,1152]{2,1,0:T(8,128)(2,1)}, u32[]{:S(2)}, u32[]{:S(2)}) collective-permute-start(bf16[2,128,1152]{2,1,0:T(8,128)(2,1)} %get-tuple-element.327), channel_id=1, source_target_pairs={{0,8},{4,12},{8,0},{12,4},{16,24},{20,28},{24,16},{28,20},{1,9},{5... | collective-permute-start | bytes 1769480 | tf_op jit(solution)/shard_map/ppermute | solution.py:34
  318.9 32.3 %collective-permute-start.23 = (bf16[2,128,1152]{2,1,0:T(8,128)(2,1)}, bf16[2,128,1152]{2,1,0:T(8,128)(2,1)}, u32[]{:S(2)}, u32[]{:S(2)}) collective-permute-start(bf16[2,128,1152]{2,1,0:T(8,128)(2,1)} %get-tuple-element.328), channel_id=1, source_target_pairs={{0,16},{4,20},{8,24},{12,28},{16,0},{20,4},{24,8},{28,12},{1,17},{... | collective-permute-start | bytes 1769480 | tf_op jit(solution)/shard_map/ppermute | solution.py:34
  389.3 45.3 %collective-permute-start.32 = (bf16[4,128,768]{2,1,0:T(8,128)(2,1)}, bf16[4,128,768]{2,1,0:T(8,128)(2,1)}, u32[]{:S(2)}, u32[]{:S(2)}) collective-permute-start(bf16[4,128,768]{2,1,0:T(8,128)(2,1)} %get-tuple-element.358), channel_id=1, source_target_pairs={{0,4},{4,0},{8,12},{12,8},{16,20},{20,16},{24,28},{28,24},{1,5},{5... | collective-permute-start | bytes 2359304 | tf_op jit(solution)/shard_map/ppermute | solution.py:34
  390.6 42.4 %collective-permute-start.33 = (bf16[288,1024]{1,0:T(8,128)(2,1)S(1)}, bf16[288,1024]{1,0:T(8,128)(2,1)S(1)}, u32[]{:S(2)}, u32[]{:S(2)}) collective-permute-start(bf16[288,1024]{1,0:T(8,128)(2,1)S(1)} %slice.124), channel_id=1, source_target_pairs={{0,2},{1,3},{2,0},{3,1},{4,6},{5,7},{6,4},{7,5},{8,10},{9,11},{10,... | collective-permute-start | bytes 1769480 | tf_op jit(solution)/shard_map/ppermute | solution.py:34
  394.5 38.5 %collective-permute-start.31 = (bf16[1,128,1152]{2,0,1:T(2,128)(2,1)S(1)}, bf16[1,128,1152]{2,0,1:T(2,128)(2,1)S(1)}, u32[]{:S(2)}, u32[]{:S(2)}) collective-permute-start(bf16[1,128,1152]{2,0,1:T(2,128)(2,1)S(1)} %copy.122), channel_id=1, source_target_pairs={{0,16},{4,20},{8,24},{12,28},{16,0},{20,4},{24,8},{28,12},{1,17},{... | collective-permute-start | bytes 884744 | tf_op jit(solution)/shard_map/ppermute | solution.py:34
  435.9 30.3 %collective-permute-start.36 = (bf16[2,1152,128]{2,1,0:T(8,128)(2,1)}, bf16[2,1152,128]{2,1,0:T(8,128)(2,1)}, u32[]{:S(2)}, u32[]{:S(2)}) collective-permute-start(bf16[2,1152,128]{2,1,0:T(8,128)(2,1)} %pad_maximum_fusion.8), channel_id=1, source_target_pairs={{0,8},{4,12},{8,0},{12,4},{16,24},{20,28},{24,16},{28,20},{1,9},{5... | collective-permute-start | bytes 1769480 | tf_op jit(solution)/shard_map/ppermute | solution.py:34
  449.9 58.8 %collective-permute-start.47 = (bf16[8,72,1024]{2,1,0:T(8,128)(2,1)S(1)}, bf16[8,72,1024]{2,1,0:T(8,128)(2,1)}, u32[]{:S(2)}, u32[]{:S(2)}) collective-permute-start(bf16[8,72,1024]{2,1,0:T(8,128)(2,1)S(1)} %all-to-all-done.2.refs_0_), channel_id=1, source_target_pairs={{0,2},{1,3},{2,0},{3,1},{4,6},{5,7},{6,4},{7,5},{8,10},{9,11},{10,... | collective-permute-start | bytes 3538952 | tf_op jit(solution)/shard_map/ppermute | solution.py:34
  450.3 65.9 %collective-permute-start.48 = (bf16[8,72,1024]{2,1,0:T(8,128)(2,1)S(1)}, bf16[8,72,1024]{2,1,0:T(8,128)(2,1)}, u32[]{:S(2)}, u32[]{:S(2)}) collective-permute-start(bf16[8,72,1024]{2,1,0:T(8,128)(2,1)S(1)} %all-to-all-done.2.refs_0_), channel_id=1, source_target_pairs={{0,1},{1,0},{2,3},{3,2},{4,5},{5,4},{6,7},{7,6},{8,9},{9,8},{10,11... | collective-permute-start | bytes 3538952 | tf_op jit(solution)/shard_map/ppermute | solution.py:34
  469.0 32.1 %collective-permute-start.39 = (bf16[2,64,2,1152]{3,2,1,0:T(2,128)(2,1)}, bf16[2,64,2,1152]{3,2,1,0:T(2,128)(2,1)}, u32[]{:S(2)}, u32[]{:S(2)}) collective-permute-start(bf16[2,64,2,1152]{3,2,1,0:T(2,128)(2,1)} %pad_maximum_fusion.9), channel_id=1, source_target_pairs={{0,8},{4,12},{8,0},{12,4},{16,24},{20,28},{24,16},{28,20},{1,9},{5... | collective-permute-start | bytes 1769480 | tf_op jit(solution)/shard_map/ppermute | solution.py:34
  478.2 70.4 %all-to-all-start.3 = ((bf16[8,72,1024]{2,1,0:T(8,128)(2,1)}), bf16[8,72,1024]{2,1,0:T(8,128)(2,1)}, u32[]{:S(2)}, u32[]{:S(2)}) async-start(bf16[8,72,1024]{2,1,0:T(8,128)(2,1)} %shard_map.431), calls=%async_computation.3 | async-start | bytes 2359296 | tf_op jit(solution)/shard_map/all_to_all | solution.py:426
  488.5 50.8 %collective-permute-start.43 = (bf16[4,1152,128]{2,1,0:T(8,128)(2,1)}, bf16[4,1152,128]{2,1,0:T(8,128)(2,1)}, u32[]{:S(2)}, u32[]{:S(2)}) collective-permute-start(bf16[4,1152,128]{2,1,0:T(8,128)(2,1)} %pad_maximum_fusion.7.held), channel_id=1, source_target_pairs={{0,4},{4,0},{8,12},{12,8},{16,20},{20,16},{24,28},{28,24},{1,5},{5... | collective-permute-start | bytes 3538952 | tf_op jit(solution)/shard_map/ppermute | solution.py:34
  504.7 43.9 %collective-permute-start.41 = (bf16[4,64,2,1152]{3,2,1,0:T(2,128)(2,1)}, bf16[4,64,2,1152]{3,2,1,0:T(2,128)(2,1)}, u32[]{:S(2)}, u32[]{:S(2)}) collective-permute-start(bf16[4,64,2,1152]{3,2,1,0:T(2,128)(2,1)} %pad_maximum_fusion.6.refs_0_), channel_id=1, source_target_pairs={{0,4},{4,0},{8,12},{12,8},{16,20},{20,16},{24,28},{28,24},{1,5},{5... | collective-permute-start | bytes 3538952 | tf_op jit(solution)/shard_map/ppermute | solution.py:34
  552.8 40.5 %collective-permute-start.56 = (bf16[8,72,1024]{2,1,0:T(8,128)(2,1)}, bf16[8,72,1024]{2,1,0:T(8,128)(2,1)}, u32[]{:S(2)}, u32[]{:S(2)}) collective-permute-start(bf16[8,72,1024]{2,1,0:T(8,128)(2,1)} %all-to-all-done.3.refs_0_), channel_id=1, source_target_pairs={{0,1},{1,0},{2,3},{3,2},{4,5},{5,4},{6,7},{7,6},{8,9},{9,8},{10,11... | collective-permute-start | bytes 3538952 | tf_op jit(solution)/shard_map/ppermute | solution.py:34
  562.2 36.6 %collective-permute-start.51 = (bf16[4,64,2,1152]{3,2,1,0:T(2,128)(2,1)}, bf16[4,64,2,1152]{3,2,1,0:T(2,128)(2,1)}, u32[]{:S(2)}, u32[]{:S(2)}) collective-permute-start(bf16[4,64,2,1152]{3,2,1,0:T(2,128)(2,1)} %constant_dynamic-update-slice_fusion.2.refs_2_), channel_id=1, source_target_pairs={{0,4},{4,0},{8,12},{12,8},{16,20},{20,16},{24,28},{28,24},{1,5},{5... | collective-permute-start | bytes 3538952 | tf_op jit(solution)/shard_map/ppermute | solution.py:34
  (125 other events, 1359.2 us)
Sparse Core Ops, SparseCore 0:
  96.8 80.0 all-gather.5
  178.9 43.4 all-gather.7
  224.6 66.1 all-gather.9
